TPU v7x, 256 devices: a whole 4x4x8 slice. The times are simulated.
256 devices in a mesh: wide: 32 (over z_hi, x, core), narrow: 8 (over z_lo, y).
Axes of the slice: x: 4, y: 4, z: 8 (z_hi: 4, z_lo: 2; z = z_hi * 2 + z_lo), core: 2. Of those that a mesh axis runs over, the one named last changes fastest.
Arguments:
- resid: bfloat16 [1024, 5120], P('wide'), may hold values from -6 to 6
- final_gain: float32 [5120], replicated, may hold values from 0.25 to 1.75
- unembed: bfloat16 [16384, 5120], P('narrow', 'wide'), may hold values from -12 to 12
- labels: int32 [1024, 4], replicated, may hold values from 0 to 16383
- layer_in: bfloat16 [1024, 5120], P('wide'), may hold values from -6 to 6
- gate_value: bfloat16 [1024, 13824], P('wide', 'narrow'), may hold values from -0.29882812 to 2
- down_weight: bfloat16 [13824, 5120], P('narrow', 'wide'), may hold values from -0.078125 to 0.078125
- basis_in: bfloat16 [5120, 5120], P('wide', 'narrow'), may hold values from -0.078125 to 0.078125
- basis_out: bfloat16 [13824, 13824], P('narrow', 'wide'), may hold values from -0.0546875 to 0.0546875
Outputs:
- corrected: float32 [13824, 5120], P('wide', 'narrow')
All inputs are finite; a program needn't handle non-finite values.
Results may differ from a plain program's by a relative error of at most 0.002.
The roundings to bfloat16 on the way count: a program that leaves them out, or rounds other values in their place, can miss the bound.
Values may be sent and summed in bfloat16 or wider, within the bound.
A program may use at most 128 MiB of HBM per device.

v0:
```python
import jax
import jax.numpy as jnp
from jax import lax
from jax.sharding import PartitionSpec as P

SEQ = 256
EXAMPLES = 4


EPSILON = 1e-05


def sent_to_all(value, axis):
    copies = jnp.broadcast_to(value, (lax.axis_size(axis), *value.shape))
    return lax.all_to_all(copies, axis, split_axis=0, concat_axis=0, tiled=True)


def of_everyone(value, axis):
    return sent_to_all(value, axis).sum(axis=0)


def taken_together(value, axis):
    return sent_to_all(value, axis).max(axis=0)


def contract_last(left, right):
    return lax.dot_general(
        left, right, (((1,), (1,)), ((), ())), preferred_element_type=jnp.float32
    )


def per_device(
    resid, final_gain, unembed, labels, layer_in, gate_value, down_weight, basis_in, basis_out
):
    wide_count = lax.axis_size("wide")
    wide_place = lax.axis_index("wide")
    narrow_place = lax.axis_index("narrow")
    local_tokens, width = resid.shape
    all_tokens, samples = labels.shape
    column_part = width // wide_count
    vocab_part = unembed.shape[0]
    hidden_part = down_weight.shape[0]
    grad_rows = local_tokens * samples
    resid_cols, inputs_cols = (
        lax.all_to_all(resid, "wide", split_axis=1, concat_axis=0, tiled=True),
        lax.all_to_all(layer_in, "wide", split_axis=1, concat_axis=0, tiled=True),
    )
    resid_float = resid_cols.astype(jnp.float32)
    gain_cols = lax.dynamic_slice_in_dim(final_gain, wide_place * column_part, column_part, 0)
    square_sums = of_everyone(jnp.sum(resid_float * resid_float, axis=1), "wide")
    inverse = lax.rsqrt(square_sums / width + EPSILON)
    normed = (resid_float * inverse[:, None] * gain_cols).astype(jnp.bfloat16)
    logits = lax.psum_scatter(
        contract_last(normed, unembed), "wide", scatter_dimension=0, tiled=True
    )
    largest = taken_together(jnp.max(logits, axis=1), "narrow")
    scaled = jnp.exp(logits - largest[:, None])
    totals = of_everyone(jnp.sum(scaled, axis=1), "narrow")
    probs = (scaled / totals[:, None]).astype(jnp.bfloat16)
    common = jnp.dot(
        lax.all_gather(probs, "wide", axis=0, tiled=True),
        unembed,
        preferred_element_type=jnp.float32,
    )
    shifted = labels - narrow_place * vocab_part
    inside = ((shifted >= 0) & (shifted < vocab_part)).astype(jnp.float32)
    picked = (
        jnp.take(unembed, jnp.clip(shifted, 0, vocab_part - 1), axis=0).astype(jnp.float32)
        * inside[:, :, None]
    )
    label_part = (common[:, None, :] - picked).reshape(all_tokens * samples, column_part)
    label_grads = lax.psum(label_part, "narrow")
    grads_local = lax.all_to_all(
        label_grads, "wide", split_axis=0, concat_axis=1, tiled=True
    ).reshape(local_tokens, samples, width)
    resid_local = resid.astype(jnp.float32)
    inverse_local = lax.rsqrt(jnp.mean(resid_local * resid_local, axis=1) + EPSILON)
    inner = jnp.sum(final_gain * grads_local * resid_local[:, None, :], axis=2)
    back = (
        inverse_local[:, None, None] * final_gain * grads_local
        - resid_local[:, None, :] * (inverse_local**3)[:, None, None] * inner[:, :, None] / width
    )
    back = back.astype(jnp.bfloat16).reshape(grad_rows, width)
    hidden_grads = contract_last(back, lax.all_gather(down_weight, "wide", axis=1, tiled=True))
    gated = (
        hidden_grads.reshape(local_tokens, samples, hidden_part)
        * gate_value.astype(jnp.float32)[:, None, :]
    )
    gated = gated.astype(jnp.bfloat16).reshape(grad_rows, hidden_part)
    rotated_part = jnp.dot(
        lax.all_gather(gated, "wide", axis=0, tiled=True),
        basis_out,
        preferred_element_type=jnp.float32,
    )
    rotated = lax.psum(rotated_part, "narrow").astype(jnp.bfloat16)
    inputs_part = jnp.dot(inputs_cols, basis_in, preferred_element_type=jnp.float32)
    inputs_rot = lax.psum(inputs_part, "wide").astype(jnp.bfloat16)
    rot_blocks = rotated.reshape(EXAMPLES, SEQ, samples, rotated.shape[1])
    input_blocks = inputs_rot.reshape(EXAMPLES, SEQ, inputs_rot.shape[1])
    blocks = jnp.einsum(
        "etsj,etd->esjd", rot_blocks, input_blocks, preferred_element_type=jnp.float32
    )
    return jnp.mean(blocks * blocks, axis=(0, 1))


def solution(mesh):
    in_specs = (
        P("wide", None),
        P(),
        P("narrow", "wide"),
        P(),
        P("wide", None),
        P("wide", "narrow"),
        P("narrow", "wide"),
        P("wide", "narrow"),
        P("narrow", "wide"),
    )
    out_specs = P("wide", "narrow")
    return jax.shard_map(
        per_device, mesh=mesh, in_specs=in_specs, out_specs=out_specs, check_vma=False
    )
```

profile of v0, /device:TPU:1, one launch (start us, length us, event | category | flops | bytes accessed | tf_op | source)
XLA Modules:
  0.0 961.0 jit_solution(15569779703708332936)
XLA Ops:
  6.5 1.8 all_to_all.48
  8.6 30.5 %all_to_all.66 = bf16[32,32,160]{2,0,1:T(8,128)(2,1)S(1)} all-to-all(bf16[32,32,160]{2,0,1:T(8,128)(2,1)S(1)} %copy.52), channel_id=1, replica_groups=mesh['wide'=32,'narrow'=8] {'wide'}, dimensions={1} | all-to-all | bytes 655360 | tf_op jit(solution)/shard_map/all_to_all | solution.py:45
  39.4 0.7 broadcast_in_dim.40
  40.1 4.2 all-to-all-start.1
  44.5 11.0 %all-to-all-done.1 = f32[32,1,1024]{2,1,0:T(1,128)S(1)} async-done(((f32[32,1,1024]{2,1,0:T(1,128)}), f32[32,1,1024]{2,1,0:T(1,128)S(1)}, u32[]{:S(2)}, u32[]{:S(2)}) %all-to-all-start.1) | async-done | bytes 131104 | tf_op jit(solution)/shard_map/all_to_all | solution.py:15
  55.9 4.5 fusion.13
  60.4 114.8 %reduce-scatter.2.cloned.1.call-done = f32[32,2048]{1,0:T(8,128)} async-done(((f32[1024,2048]{1,0:T(8,128)}), f32[32,2048]{1,0:T(8,128)}) %reduce-scatter.2.cloned.1.call-update) | async-done | bytes 262160 | tf_op jit(solution)/shard_map/reduce_scatter | solution.py:53
  175.2 1.1 reduce_max.18
  176.3 8.8 all_to_all.67
  185.2 1.2 fusion.12
  186.3 7.4 all_to_all.68
  193.8 1.7 divide_convert_fusion
  196.1 1.0 copy.58
  197.1 1.3 reshape.135
  198.4 1.0 copy.60
  199.5 1.3 reshape.132
  201.4 16.9 %gather_fusion = bf16[4096,160]{1,0:T(8,128)(2,1)} fusion(bf16[2048,160]{1,0:T(8,128)(2,1)S(1)} %copy.59, s32[4096]{0:T(1024)S(1)} %broadcast_clamp_fusion), kind=kCustom, calls=%fused_computation | custom fusion | bytes 2637824 | tf_op jit(solution)/shard_map/jit(_take)/gather | solution.py:68
  218.3 38.6 %all-gather.4.cloned.1.call-done = bf16[1024,2048]{1,0:T(8,128)(2,1)} async-done(((bf16[32,2048]{1,0:T(8,128)(2,1)}), bf16[1024,2048]{1,0:T(8,128)(2,1)}) %all-gather.4.cloned.1.call-update) | async-done | bytes 4194320 | tf_op jit(solution)/shard_map/all_gather | solution.py:61
  257.0 3.5 fusion.14
  260.5 2.6 sub.32
  263.1 5.3 sub.33
  268.4 7.0 multiply_subtract_fusion
  275.4 5.1 copy.61
  280.6 0.5 all-gather.6.cloned.1.call-update
  281.1 84.4 %all-reduce.4.cloned.1.call-done = f32[32,128,160]{1,2,0:T(8,128)} async-done(((f32[32,128,160]{1,2,0:T(8,128)}), f32[32,128,160]{1,2,0:T(8,128)}) %all-reduce.4.cloned.1.call-update) | async-done | bytes 2621456 | tf_op jit(solution)/shard_map/psum | solution.py:72
  365.5 13.1 %all-to-all-start.4 = ((f32[32,128,160]{1,2,0:T(8,128)}), f32[32,128,160]{1,2,0:T(8,128)}, u32[]{:S(2)}, u32[]{:S(2)}) async-start(f32[32,128,160]{1,2,0:T(8,128)} %all-reduce.4.cloned.1.call-done), calls=%async_computation.5 | async-start | bytes 5242880 | tf_op jit(solution)/shard_map/all_to_all | solution.py:73
  379.0 2.1 mul.153
  381.1 5.7 mul.154
  386.8 0.7 convert_element_type.53
  387.8 0.9 broadcast_multiply_fusion.1
  388.8 63.1 %all-to-all-done.4 = f32[32,128,160]{1,2,0:T(8,128)} async-done(((f32[32,128,160]{1,2,0:T(8,128)}), f32[32,128,160]{1,2,0:T(8,128)}, u32[]{:S(2)}, u32[]{:S(2)}) %all-to-all-start.4) | async-done | bytes 2621472 | tf_op jit(solution)/shard_map/all_to_all | solution.py:73
  451.8 5.1 copy.62
  457.0 4.5 multiply_reduce_fusion.1
  461.6 6.1 reshape.127
  467.7 2.7 subtract_convert_fusion
  470.4 65.5 %all-gather.6.cloned.1.call-done = bf16[1728,5120]{0,1:T(8,128)(2,1)} async-done(((bf16[1728,160]{0,1:T(8,128)(2,1)}), bf16[1728,5120]{0,1:T(8,128)(2,1)}) %all-gather.6.cloned.1.call-update) | async-done | bytes 17694736 | tf_op jit(solution)/shard_map/all_gather | solution.py:84
  535.9 9.0 fusion.6
  545.3 1.0 reshape.128
  546.3 0.6 all_to_all.56
  547.3 38.1 %all_to_all.69 = bf16[32,32,160]{2,0,1:T(8,128)(2,1)S(1)} all-to-all(bf16[32,32,160]{2,0,1:T(8,128)(2,1)S(1)} %copy.66), channel_id=1, replica_groups=mesh['wide'=32,'narrow'=8] {'wide'}, dimensions={1} | all-to-all | bytes 655360 | tf_op jit(solution)/shard_map/all_to_all | solution.py:46
  585.4 2.0 fusion.16
  587.4 199.5 %all-reduce.6 = bf16[1024,640]{1,0:T(8,128)(2,1)S(1)} all-reduce(f32[1024,640]{1,0:T(8,128)} %fusion.16), channel_id=1, replica_groups=mesh['wide'=32,'narrow'=8] {'wide'}, use_global_device_ids=true, to_apply=%region_11.12 | all-reduce | flops 655360 | bytes 3932160 | tf_op jit(solution)/shard_map/psum | solution.py:97
  786.9 11.7 %fusion.15 = f32[4096,432]{0,1:T(8,128)} fusion(bf16[4096,1728]{1,0:T(8,128)(2,1)} %all-gather.8.cloned.1.call-done, bf16[1728,432]{0,1:T(8,128)(2,1)S(1)} %copy-done), kind=kOutput, calls=%fused_computation.31 | convolution fusion | flops 6115295232 | bytes 22726656 | tf_op jit(solution)/shard_map/dot_general | solution.py:90
  798.7 135.7 %all-reduce.5 = bf16[4096,432]{0,1:T(8,128)(2,1)} all-reduce(f32[4096,432]{0,1:T(8,128)} %fusion.15), channel_id=1, replica_groups=mesh['wide'=32,'narrow'=8] {'narrow'}, use_global_device_ids=true, to_apply=%region_10.11 | all-reduce | flops 1769472 | bytes 10616832 | tf_op jit(solution)/shard_map/psum | solution.py:95
  934.4 6.4 copy.65
  940.8 7.0 reshape.129
  947.8 5.6 multiply_reduce_fusion
  953.4 1.1 broadcast_multiply_fusion
  (49 shorter events, 3.8 us)
Async XLA Ops:
  6.5 780.4 %copy-start = (bf16[1728,432]{0,1:T(8,128)(2,1)S(1)}, bf16[1728,432]{0,1:T(8,128)(2,1)}, u32[]{:S(2)}) copy-start(bf16[1728,432]{0,1:T(8,128)(2,1)} %param.17) | copy-start | bytes 4478980
  6.5 37.9 %copy-start.6 = (f32[5120]{0:T(1024)S(1)}, f32[5120]{0:T(1024)}, u32[]{:S(2)}) copy-start(f32[5120]{0:T(1024)} %param.10) | copy-start | bytes 61444
  6.5 49.3 %copy-start.2 = (bf16[2048,160]{0,1:T(8,128)(2,1)S(1)}, bf16[2048,160]{0,1:T(8,128)(2,1)}, u32[]{:S(2)}) copy-start(bf16[2048,160]{0,1:T(8,128)(2,1)} %param.11) | copy-start | bytes 1966084
  40.1 15.4 %all-to-all-start.1 = ((f32[32,1,1024]{2,1,0:T(1,128)}), f32[32,1,1024]{2,1,0:T(1,128)S(1)}, u32[]{:S(2)}, u32[]{:S(2)}) async-start(f32[32,1,1024]{2,1,0:T(1,128)} %broadcast_in_dim.40), calls=%async_computation.1 | async-start | bytes 262144 | tf_op jit(solution)/shard_map/all_to_all | solution.py:15
  44.4 130.8 %reduce-scatter.2.cloned.1.call-start = ((), (), s32[]{:S(2)}) async-start(), calls=%async_computation.7 | async-start | bytes 8650752 | tf_op jit(solution)/shard_map/reduce_scatter | solution.py:53
  60.3 135.7 %copy-start.7 = (s32[1024,4]{0,1:T(4,128)S(1)}, s32[1024,4]{0,1:T(4,128)}, u32[]{:S(2)}) copy-start(s32[1024,4]{0,1:T(4,128)} %param.12) | copy-start | bytes 49156
  60.4 196.6 %all-gather.4.cloned.1.call-start = ((), (), s32[]{:S(2)}) async-start(), calls=%async_computation.8 | async-start | bytes 4325376 | tf_op jit(solution)/shard_map/all_gather | solution.py:61
  195.5 170.0 %all-reduce.4.cloned.1.call-start = ((), (), s32[]{:S(2)}) async-start(), calls=%async_computation.9 | async-start | bytes 5242880 | tf_op jit(solution)/shard_map/psum | solution.py:72
  280.5 255.4 %all-gather.6.cloned.1.call-start = ((), (), s32[]{:S(2)}) async-start(), calls=%async_computation.10 | async-start | bytes 18923520 | tf_op jit(solution)/shard_map/all_gather | solution.py:84
  281.1 97.9 %copy-start.1 = (bf16[32,5120]{1,0:T(8,128)(2,1)S(1)}, bf16[32,5120]{1,0:T(8,128)(2,1)}, u32[]{:S(2)}) copy-start(bf16[32,5120]{1,0:T(8,128)(2,1)} %param.9) | copy-start | bytes 983044
  365.5 86.3 %all-to-all-start.4 = ((f32[32,128,160]{1,2,0:T(8,128)}), f32[32,128,160]{1,2,0:T(8,128)}, u32[]{:S(2)}, u32[]{:S(2)}) async-start(f32[32,128,160]{1,2,0:T(8,128)} %all-reduce.4.cloned.1.call-done), calls=%async_computation.5 | async-start | bytes 5242880 | tf_op jit(solution)/shard_map/all_to_all | solution.py:73
  378.6 408.3 %all-gather.8.cloned.1.call-start = ((), (), s32[]{:S(2)}) async-start(), calls=%async_computation.11 | async-start | bytes 15138816 | tf_op jit(solution)/shard_map/all_gather | solution.py:91
  381.1 5.7 copy-start.5
  470.4 75.9 %copy-start.3 = (bf16[32,5120]{1,0:T(8,128)(2,1)S(1)}, bf16[32,5120]{1,0:T(8,128)(2,1)}, u32[]{:S(2)}) copy-start(bf16[32,5120]{1,0:T(8,128)(2,1)} %param.13) | copy-start | bytes 983044
  544.9 40.4 %copy-start.4 = (bf16[160,640]{1,0:T(8,128)(2,1)S(1)}, bf16[160,640]{1,0:T(8,128)(2,1)}, u32[]{:S(2)}) copy-start(bf16[160,640]{1,0:T(8,128)(2,1)} %param.16) | copy-start | bytes 614404
Sparse Core Ops, SparseCore 0:
  60.5 114.7 reduce-scatter.1
  195.6 61.3 all-gather.3
  280.6 84.8 all-reduce.3
  367.9 167.9 all-gather.5
  546.4 137.2 all-gather.7
where the time goes:
time: 970 us; the launch traced here: 961 us
  blocking collectives  420 us (43%)
  waiting for transfers between devices  378 us (39%)
  local copies, waits for them, and re-layouts  73.6 us (8%)
  matrix products  36.4 us (4%)
  other arithmetic  21.8 us (2%)
  starting transfers between devices  17.7 us (2%)
  between operations  13.4 us (1%)
    psum x1, blocking collectives, per_device(): inputs_rot = lax.psum(inputs_part, 'wide').astype(jnp.bfloat16)  199 us
    psum x1, blocking collectives, per_device(): rotated = lax.psum(rotated_part, 'narrow').astype(jnp.bfloat16)  136 us
    reduce_scatter x1, waiting for transfers between devices, per_device(): lax.psum_scatter(contract_last(normed, unembed), 'wide', scatter_dimensio...  115 us
    psum x1, waiting for transfers between devices, per_device(): label_grads = lax.psum(label_part, 'narrow')  84.4 us
    all_gather x1, waiting for transfers between devices, per_device(): lax.all_gather(down_weight, 'wide', axis=1, tiled=True)  65.5 us
    all_to_all x1, waiting for transfers between devices, per_device(): lax.all_to_all(label_grads, 'wide', split_axis=0, concat_axis=1, tiled=True)  63.1 us
    all_gather x1, waiting for transfers between devices, per_device(): lax.all_gather(probs, 'wide', axis=0, tiled=True)  38.6 us
    all_to_all x1, blocking collectives, per_device(): lax.all_to_all(layer_in, 'wide', split_axis=1, concat_axis=0, tiled=True)  38.1 us
  transfers between devices with their start and end apart: 7, of which 6 were waited for; matrix products, arithmetic and copies ran while one was open for 6% of the time, Pallas kernels for 0%

commit v1 on v0

v1 whole, which is shorter than its diff:
```python
import functools

import jax
import jax.numpy as jnp
from jax import lax
from jax.experimental import pallas as pl
from jax.experimental.pallas import tpu as pltpu
from jax.sharding import PartitionSpec as P

EPSILON = 1e-05
MESH = pl.DeviceIdType.MESH
F32 = jnp.float32
BF16 = jnp.bfloat16
ANY = pl.BlockSpec(memory_space=pl.ANY)
VMEM = pl.BlockSpec(memory_space=pltpu.VMEM)


class Net:
    def __init__(self, send_sem, recv_sem):
        self.send_sem, self.recv_sem = send_sem, recv_sem
        self.started = []
        wide, narrow = lax.axis_index("wide"), lax.axis_index("narrow")
        self.wide, self.narrow = wide, narrow
        self.core = lax.rem(wide, 2)
        self.x = lax.rem(lax.div(wide, 2), 4)
        self.z = lax.div(wide, 8)
        self.y = lax.rem(narrow, 4)
        self.zl = lax.div(narrow, 4)

    def on_x(self, step):
        return {"wide": self.z * 8 + lax.rem(self.x + step, 4) * 2 + self.core}

    def on_z(self, step):
        return {"wide": lax.rem(self.z + step, 4) * 8 + self.x * 2 + self.core}

    def on_y(self, step):
        return {"narrow": self.zl * 4 + lax.rem(self.y + step, 4)}

    def on_zl(self, step):
        return {"narrow": (1 - self.zl) * 4 + self.y}

    def on_core(self):
        return {"wide": self.wide + 1 - 2 * self.core}

    def greet(self, devices):
        barrier = pltpu.get_barrier_semaphore()
        for device in devices:
            pl.semaphore_signal(barrier, inc=1, device_id=device, device_id_type=MESH)
        pl.semaphore_wait(barrier, len(devices))

    def copy(self, slot, src, dst, device):
        return pltpu.make_async_remote_copy(
            src_ref=src,
            dst_ref=dst,
            send_sem=self.send_sem.at[slot],
            recv_sem=self.recv_sem.at[slot],
            device_id=device,
            device_id_type=MESH,
        )

    def send(self, slot, src, dst, device):
        copy = self.copy(slot, src, dst, device)
        copy.start()
        self.started.append(copy)

    def recv(self, slot, dst):
        self.copy(slot, dst, dst, self.on_core()).wait_recv()

    def finish(self):
        for copy in self.started:
            copy.wait_send()


def turn(place, step, size):
    return lax.rem(place + step, size)


def gather_stage(net, base, own, slot, outer_size, me_o, me_i, on_o, on_i):
    ip, im, i2 = (turn(me_i, s, 4) for s in (1, 3, 2))
    inner = lambda row: base + 6 + 6 * row

    def along(row, o, first):
        b = inner(row)
        src = own if first else (lambda h: slot(o, me_i, h))
        net.send(b, src(0), slot(o, me_i, 0), on_i(1))
        net.send(b + 2, src(1), slot(o, me_i, 1), on_i(3))
        net.send(b + 1, src(1), slot(o, me_i, 1), on_i(1))
        net.send(b + 3, src(0), slot(o, me_i, 0), on_i(3))

    def forward(row, o):
        b = inner(row)
        net.recv(b, slot(o, im, 0))
        net.send(b + 4, slot(o, im, 0), slot(o, im, 0), on_i(1))
        net.recv(b + 2, slot(o, ip, 1))
        net.send(b + 5, slot(o, ip, 1), slot(o, ip, 1), on_i(3))

    def rest(row, o):
        b = inner(row)
        net.recv(b + 1, slot(o, im, 1))
        net.recv(b + 3, slot(o, ip, 0))
        net.recv(b + 4, slot(o, i2, 0))
        net.recv(b + 5, slot(o, i2, 1))

    if outer_size == 4:
        op, om, o2 = (turn(me_o, s, 4) for s in (1, 3, 2))
        net.send(base, own(0), slot(me_o, me_i, 0), on_o(1))
        net.send(base + 2, own(1), slot(me_o, me_i, 1), on_o(3))
        net.send(base + 1, own(1), slot(me_o, me_i, 1), on_o(1))
        net.send(base + 3, own(0), slot(me_o, me_i, 0), on_o(3))
        along(0, me_o, True)
        net.recv(base, slot(om, me_i, 0))
        net.send(base + 4, slot(om, me_i, 0), slot(om, me_i, 0), on_o(1))
        net.recv(base + 2, slot(op, me_i, 1))
        net.send(base + 5, slot(op, me_i, 1), slot(op, me_i, 1), on_o(3))
        forward(0, me_o)
        net.recv(base + 1, slot(om, me_i, 1))
        along(1, om, False)
        net.recv(base + 3, slot(op, me_i, 0))
        along(2, op, False)
        forward(1, om)
        net.recv(base + 4, slot(o2, me_i, 0))
        net.recv(base + 5, slot(o2, me_i, 1))
        along(3, o2, False)
        forward(2, op)
        forward(3, o2)
        for row, o in enumerate((me_o, om, op, o2)):
            rest(row, o)
    else:
        oq = 1 - me_o
        for h in range(2):
            net.send(base + h, own(h), slot(me_o, me_i, h), on_o(1))
        along(0, me_o, True)
        forward(0, me_o)
        for h in range(2):
            net.recv(base + h, slot(oq, me_i, h))
        along(1, oq, False)
        forward(1, oq)
        rest(0, me_o)
        rest(1, oq)


def gather_slots(outer_size):
    return 6 + 6 * outer_size


class Sum:
    def __init__(self, part, fwd, mid, got, tot, zfwd, zgot):
        self.part, self.fwd, self.mid, self.got = part, fwd, mid, got
        self.tot, self.zfwd, self.zgot = tot, zfwd, zgot
        self.half = part.shape[2] // 2

    @staticmethod
    def scratch(outer, rows, columns, dtype):
        half = rows // 2
        return [
            pltpu.VMEM((outer, 2, half, columns), dtype),
            pltpu.VMEM((outer, 2, half, columns), dtype),
            pltpu.VMEM((outer, 2, rows, columns), dtype),
            pltpu.VMEM((outer, rows, columns), dtype),
            pltpu.VMEM((2, half, columns), dtype),
            pltpu.VMEM((2, rows, columns), dtype),
        ]

    def h(self, k):
        return pl.ds(k * self.half, self.half)


def reduce_slots(outer_size):
    return 6 * outer_size + 6


def reduce_stage(net, base, sums, outer_size, me_o, me_i, on_o, on_i):
    ip, im, i2 = (turn(me_i, s, 4) for s in (1, 3, 2))
    offsets = (2, 1, 3, 0) if outer_size == 4 else (1, 0)
    rows = [turn(me_o, off, outer_size) for off in offsets]
    count = reduce_slots(outer_size)

    def at(a, k, j):
        return base + a * count + 6 * k + j

    def start_far(k):
        for a, s in enumerate(sums):
            net.send(at(a, k, 0), s.part.at[rows[k], i2, s.h(0)], s.fwd.at[k, 0], on_i(1))
            net.send(at(a, k, 1), s.part.at[rows[k], i2, s.h(1)], s.fwd.at[k, 1], on_i(3))

    def start_near(k):
        for a, s in enumerate(sums):
            net.send(at(a, k, 2), s.part.at[rows[k], ip, s.h(1)], s.got.at[k, 0, s.h(1)], on_i(1))
            net.send(at(a, k, 3), s.part.at[rows[k], im, s.h(0)], s.got.at[k, 1, s.h(0)], on_i(3))

    def middle(k):
        for a, s in enumerate(sums):
            net.recv(at(a, k, 0), s.fwd.at[k, 0])
            s.mid[k, 0] = s.part[rows[k], ip, s.h(0)] + s.fwd[k, 0]
            net.send(at(a, k, 4), s.mid.at[k, 0], s.got.at[k, 0, s.h(0)], on_i(1))
            net.recv(at(a, k, 1), s.fwd.at[k, 1])
            s.mid[k, 1] = s.part[rows[k], im, s.h(1)] + s.fwd[k, 1]
            net.send(at(a, k, 5), s.mid.at[k, 1], s.got.at[k, 1, s.h(1)], on_i(3))

    def total(k):
        for a, s in enumerate(sums):
            z = base + a * count + 6 * outer_size
            net.recv(at(a, k, 2), s.got.at[k, 0, s.h(1)])
            net.recv(at(a, k, 3), s.got.at[k, 1, s.h(0)])
            net.recv(at(a, k, 4), s.got.at[k, 0, s.h(0)])
            net.recv(at(a, k, 5), s.got.at[k, 1, s.h(1)])
            for h in range(2):
                s.tot[k, s.h(h)] = (
                    s.part[rows[k], me_i, s.h(h)] + s.got[k, 0, s.h(h)] + s.got[k, 1, s.h(h)]
                )
            if outer_size == 2:
                if k == 0:
                    for h in range(2):
                        net.send(z + h, s.tot.at[0, s.h(h)], s.zgot.at[0, s.h(h)], on_o(1))
            elif k == 0:
                net.send(z, s.tot.at[0, s.h(0)], s.zfwd.at[0], on_o(1))
                net.send(z + 1, s.tot.at[0, s.h(1)], s.zfwd.at[1], on_o(3))
            elif k == 1:
                net.send(z + 2, s.tot.at[1, s.h(1)], s.zgot.at[0, s.h(1)], on_o(1))
                net.recv(z, s.zfwd.at[0])
                s.tot[1, s.h(0)] += s.zfwd[0]
                net.send(z + 3, s.tot.at[1, s.h(0)], s.zgot.at[0, s.h(0)], on_o(1))
            elif k == 2:
                net.send(z + 4, s.tot.at[2, s.h(0)], s.zgot.at[1, s.h(0)], on_o(3))
                net.recv(z + 1, s.zfwd.at[1])
                s.tot[2, s.h(1)] += s.zfwd[1]
                net.send(z + 5, s.tot.at[2, s.h(1)], s.zgot.at[1, s.h(1)], on_o(3))

    start_far(0)
    start_far(1)
    start_near(0)
    for k in range(outer_size):
        if k + 2 < outer_size:
            start_far(k + 2)
        if k + 1 < outer_size:
            start_near(k + 1)
        middle(k)
        if k >= 1:
            total(k - 1)
    total(outer_size - 1)

    def final(a):
        s = sums[a]
        z = base + a * count + 6 * outer_size
        last = outer_size - 1

        def value(h):
            if outer_size == 2:
                net.recv(z + h, s.zgot.at[0, s.h(h)])
                return s.tot[last, s.h(h)] + s.zgot[0, s.h(h)]
            first, second = ((z + 3, z + 4), (z + 2, z + 5))[h]
            net.recv(first, s.zgot.at[0, s.h(h)])
            net.recv(second, s.zgot.at[1, s.h(h)])
            return s.tot[last, s.h(h)] + s.zgot[0, s.h(h)] + s.zgot[1, s.h(h)]

        return value

    return [final(a) for a in range(len(sums))]


def sems(slots):
    return [pltpu.SemaphoreType.DMA((slots,)), pltpu.SemaphoreType.DMA((slots,))]


def call(kernel, collective_id, outs, in_specs, out_specs, scratch, args, name):
    return pl.pallas_call(
        kernel,
        out_shape=outs,
        in_specs=in_specs,
        out_specs=out_specs,
        scratch_shapes=scratch,
        compiler_params=pltpu.CompilerParams(
            collective_id=collective_id, has_side_effects=True, vmem_limit_bytes=60 << 20
        ),
        name=name,
    )(*args)


def like(shape, dtype):
    return jax.ShapeDtypeStruct(shape, dtype)


def exchange(arrays, pairs, collective_id, name):
    na, np_ = len(arrays), len(pairs)

    def kernel(*refs):
        ins, shared = refs[:na], refs[na : na + np_]
        outs, both = refs[na + np_ : 2 * na + np_], refs[2 * na + np_ : 2 * (na + np_)]
        local, send_sem, recv_sem = refs[2 * (na + np_) :]
        net = Net(send_sem, recv_sem)
        steps = [(dz, dx) for dz in range(4) for dx in range(4) if (dz, dx) != (0, 0)]
        steps.sort(key=lambda s: -(min(s[0], 4 - s[0]) * 2 + min(s[1], 4 - s[1])))

        def to(dz, dx):
            return turn(net.z, dz, 4) * 4 + turn(net.x, dx, 4)

        me = net.z * 4 + net.x
        peers = [{"wide": to(*s) * 2 + net.core} for s in steps]
        net.greet(peers + ([net.on_core()] if np_ else []))
        copies = []
        for j, s in enumerate(steps):
            for a in range(na):
                net.send(j * na + a, ins[a].at[to(*s)], outs[a].at[me], peers[j])
        for a in range(na):
            copies.append(pltpu.make_async_copy(ins[a].at[me], outs[a].at[me], local.at[a]))
        for b in range(np_):
            net.send(15 * na + b, shared[b], both[b].at[net.core], net.on_core())
            copies.append(
                pltpu.make_async_copy(shared[b], both[b].at[net.core], local.at[na + b])
            )
        for copy in copies:
            copy.start()
        for j, (dz, dx) in enumerate(steps):
            source = to((4 - dz) % 4, (4 - dx) % 4)
            for a in range(na):
                net.recv(j * na + a, outs[a].at[source])
        for b in range(np_):
            net.recv(15 * na + b, both[b].at[1 - net.core])
        for copy in copies:
            copy.wait()
        net.finish()

    outs = [like(a.shape, a.dtype) for a in arrays] + [like((2, *p.shape), p.dtype) for p in pairs]
    return call(
        kernel,
        collective_id,
        outs,
        [ANY] * (na + np_),
        [ANY] * (na + np_),
        [pltpu.SemaphoreType.DMA((na + np_,)), *sems(15 * na + max(np_, 1))],
        (*arrays, *pairs),
        name,
    )


def gather_wide(shard, spread, collective_id, name):
    half = shard.shape[0] // 2
    shape = (4, shard.shape[0], 4, *shard.shape[1:]) if spread else (4, 4, *shard.shape)

    def kernel(x_ref, o_ref, local, send_sem, recv_sem):
        net = Net(send_sem, recv_sem)

        def slot(o, i, h):
            part = pl.ds(h * half, half)
            return o_ref.at[o, part, i] if spread else o_ref.at[o, i, part]

        net.greet([net.on_x(1), net.on_x(3), net.on_z(1), net.on_z(3)])
        own = lambda h: x_ref.at[pl.ds(h * half, half)]
        copies = [
            pltpu.make_async_copy(own(h), slot(net.z, net.x, h), local.at[h]) for h in range(2)
        ]
        for copy in copies:
            copy.start()
        gather_stage(net, 0, own, slot, 4, net.z, net.x, net.on_z, net.on_x)
        for copy in copies:
            copy.wait()
        net.finish()

    return call(
        kernel,
        collective_id,
        like(shape, shard.dtype),
        [ANY],
        ANY,
        [pltpu.SemaphoreType.DMA((2,)), *sems(gather_slots(4))],
        (shard,),
        name,
    )


def gather_narrow(shard, collective_id, name):
    half = shard.shape[0] // 2

    def kernel(x_ref, o_ref, local, send_sem, recv_sem):
        net = Net(send_sem, recv_sem)
        slot = lambda o, i, h: o_ref.at[o, i, pl.ds(h * half, half)]
        net.greet([net.on_y(1), net.on_y(3), net.on_zl(1)])
        own = lambda h: x_ref.at[pl.ds(h * half, half)]
        copies = [
            pltpu.make_async_copy(own(h), slot(net.zl, net.y, h), local.at[h]) for h in range(2)
        ]
        for copy in copies:
            copy.start()
        gather_stage(net, 0, own, slot, 2, net.zl, net.y, net.on_zl, net.on_y)
        for copy in copies:
            copy.wait()
        net.finish()

    return call(
        kernel,
        collective_id,
        like((2, 4, *shard.shape), shard.dtype),
        [ANY],
        ANY,
        [pltpu.SemaphoreType.DMA((2,)), *sems(gather_slots(2))],
        (shard,),
        name,
    )


def reduce_over(axis, parts, dtypes, collective_id, name):
    n = len(parts)
    outer = parts[0].shape[0]

    def kernel(*refs):
        ins, outs = refs[:n], refs[n : 2 * n]
        buffers, (send_sem, recv_sem) = refs[2 * n : -2], refs[-2:]
        net = Net(send_sem, recv_sem)
        sums = [Sum(ins[a], *buffers[6 * a : 6 * a + 6]) for a in range(n)]
        if axis == "wide":
            net.greet([net.on_x(1), net.on_x(3), net.on_z(1), net.on_z(3)])
            ends = reduce_stage(net, 0, sums, 4, net.z, net.x, net.on_z, net.on_x)
        else:
            net.greet([net.on_y(1), net.on_y(3), net.on_zl(1)])
            ends = reduce_stage(net, 0, sums, 2, net.zl, net.y, net.on_zl, net.on_y)
        for a in range(n):
            for h in range(2):
                outs[a][sums[a].h(h), :] = ends[a](h).astype(outs[a].dtype)
        net.finish()

    scratch = []
    for p in parts:
        scratch += Sum.scratch(outer, p.shape[2], p.shape[3], p.dtype)
    return call(
        kernel,
        collective_id,
        [like(p.shape[2:], d) for p, d in zip(parts, dtypes)],
        [VMEM] * n,
        [VMEM] * n,
        [*scratch, *sems(n * reduce_slots(outer))],
        tuple(parts),
        name,
    )


def softmax_narrow(logits, collective_id, name):
    rows, columns = logits.shape

    def kernel(l_ref, p_ref, mine, got, send_sem, recv_sem):
        net = Net(send_sem, recv_sem)
        peers = [{"narrow": turn(net.narrow, k, 8)} for k in range(1, 8)]
        top = jnp.max(l_ref[...], axis=1, keepdims=True)
        mine[0] = jnp.broadcast_to(top, (rows, 128))
        mine[1] = jnp.broadcast_to(
            jnp.sum(jnp.exp(l_ref[...] - top), axis=1, keepdims=True), (rows, 128)
        )
        net.greet(peers)
        for k in range(7):
            net.send(k, mine, got.at[k], peers[k])
        for k in range(7):
            net.recv(k, got.at[k])
        largest = mine[0]
        for k in range(7):
            largest = jnp.maximum(largest, got[k, 0])
        total = mine[1] * jnp.exp(mine[0] - largest)
        for k in range(7):
            total += got[k, 1] * jnp.exp(got[k, 0] - largest)
        p_ref[...] = (jnp.exp(l_ref[...] - largest[:, :1]) / total[:, :1]).astype(BF16)
        net.finish()

    return call(
        kernel,
        collective_id,
        like((rows, columns), BF16),
        [VMEM],
        VMEM,
        [pltpu.VMEM((2, rows, 128), F32), pltpu.VMEM((7, 2, rows, 128), F32), *sems(7)],
        (logits,),
        name,
    )


def rotate(gated, basis):
    chunks, rows, depth = gated.shape
    columns = basis.shape[0]

    def kernel(g_ref, b_ref, o_ref):
        o_ref[0] = lax.dot_general(
            b_ref[...], g_ref[0], (((1,), (1,)), ((), ())), preferred_element_type=F32
        )

    return pl.pallas_call(
        kernel,
        grid=(chunks,),
        out_shape=like((chunks, columns, rows), F32),
        in_specs=[
            pl.BlockSpec((1, rows, depth), lambda i: (i, 0, 0)),
            pl.BlockSpec((columns, depth), lambda i: (0, 0)),
        ],
        out_specs=pl.BlockSpec((1, columns, rows), lambda i: (i, 0, 0)),
        name="rotate",
    )(gated, basis)


def total_narrow(part, inputs, collective_id, name):
    rows, columns = part.shape[2] // 2, part.shape[3]

    def kernel(p_ref, i_ref, o_ref, j_ref, *refs):
        buffers, (mine, local, send_sem, recv_sem) = refs[:6], refs[6:]
        net = Net(send_sem, recv_sem)
        net.greet([net.on_y(1), net.on_y(3), net.on_zl(1), net.on_core()])
        base = reduce_slots(2)
        net.send(base, i_ref, j_ref, net.on_core())
        sums = [Sum(p_ref, *buffers)]
        (end,) = reduce_stage(net, 0, sums, 2, net.zl, net.y, net.on_zl, net.on_y)
        for h in range(2):
            mine[h] = end(h).astype(BF16)
        net.send(base + 1, mine.at[1 - net.core], mine.at[2], net.on_core())
        net.recv(base + 1, mine.at[2])
        slot = lambda o, i, h: o_ref.at[o, i, h]
        own = lambda h: mine.at[2 if h else net.core]
        copies = [
            pltpu.make_async_copy(own(h), slot(net.zl, net.y, h), local.at[h]) for h in range(2)
        ]
        for copy in copies:
            copy.start()
        gather_stage(net, base + 2, own, slot, 2, net.zl, net.y, net.on_zl, net.on_y)
        net.recv(base, j_ref)
        for copy in copies:
            copy.wait()
        net.finish()

    return call(
        kernel,
        collective_id,
        [like((2, 4, 2, rows, columns), BF16), like(inputs.shape, BF16)],
        [VMEM, ANY],
        [ANY, ANY],
        [
            *Sum.scratch(2, 2 * rows, columns, F32),
            pltpu.VMEM((3, rows, columns), BF16),
            pltpu.SemaphoreType.DMA((2,)),
            *sems(reduce_slots(2) + 2 + gather_slots(2)),
        ],
        (part, inputs),
        name,
    )


def squares(rotated, own_inputs, other_inputs):
    rows, width = rotated.shape[2], own_inputs.shape[2]

    def kernel(r_ref, a_ref, b_ref, o_ref):
        step = pl.program_id(0)

        @pl.when(step == 0)
        def _():
            o_ref[...] = jnp.zeros_like(o_ref)

        for s in range(2):
            cut = pl.ds(s * 128, 128)
            block = jnp.dot(r_ref[0, 0, :, cut], a_ref[0], preferred_element_type=F32)
            block += jnp.dot(r_ref[0, 1, :, cut], b_ref[0], preferred_element_type=F32)
            o_ref[...] += block * block * (1.0 / 16.0)

    return pl.pallas_call(
        kernel,
        grid=(8,),
        out_shape=like((rows, width), F32),
        in_specs=[
            pl.BlockSpec((1, 2, rows, 256), lambda i: (i, 0, 0, 0)),
            pl.BlockSpec((1, 128, width), lambda i: (i // 2, 0, 0)),
            pl.BlockSpec((1, 128, width), lambda i: (i // 2, 0, 0)),
        ],
        out_specs=pl.BlockSpec((rows, width), lambda i: (0, 0)),
        name="squares",
    )(rotated, own_inputs, other_inputs)


def contract_last(left, right):
    return lax.dot_general(left, right, (((1,), (1,)), ((), ())), preferred_element_type=F32)


def per_device(
    resid, final_gain, unembed, labels, layer_in, gate_value, down_weight, basis_in, basis_out
):
    wide, narrow = lax.axis_index("wide"), lax.axis_index("narrow")
    core = lax.rem(wide, 2)
    tokens, width = resid.shape
    samples = labels.shape[1]
    vocab, part = unembed.shape
    hidden = down_weight.shape[0]
    columns = basis_out.shape[1]
    width_in = basis_in.shape[1]
    pair = 2 * part
    core_tokens = 16 * tokens
    few = tokens // 8

    down_rows = lax.all_gather(down_weight.T, "wide", axis=0, tiled=True)

    resid_float = resid.astype(F32)
    inverse = lax.rsqrt(jnp.mean(resid_float * resid_float, axis=1) + EPSILON)
    normed = (resid_float * inverse[:, None] * final_gain).astype(BF16)

    def blocks(rows):
        return rows.reshape(tokens, 16, pair).transpose(1, 0, 2)

    normed_cols, inputs_cols, unembed_rows, basis_in_rows, basis_rows = exchange(
        [blocks(normed), blocks(layer_in)],
        [unembed.T, basis_in, basis_out.T],
        0,
        "exchange",
    )
    unembed_rows = unembed_rows.reshape(pair, vocab)
    basis_in_rows = basis_in_rows.reshape(pair, width_in)
    logits_part = jnp.dot(
        normed_cols.reshape(core_tokens, pair), unembed_rows, preferred_element_type=F32
    )
    inputs_part = jnp.dot(
        inputs_cols.reshape(core_tokens, pair), basis_in_rows, preferred_element_type=F32
    )
    logits, inputs_rot = reduce_over(
        "wide",
        [logits_part.reshape(4, 4, tokens, vocab), inputs_part.reshape(4, 4, tokens, width_in)],
        [F32, BF16],
        1,
        "reduce_logits",
    )
    probs = softmax_narrow(logits, 2, "softmax")
    both = jnp.concatenate([probs, inputs_rot], axis=1)
    both = gather_wide(both.reshape(2, tokens // 2, vocab + width_in), False, 3, "gather_probs")
    both = both.reshape(core_tokens, vocab + width_in)
    inputs_all = both[:, vocab:].reshape(4, 4 * tokens, width_in)
    common = contract_last(both[:, :vocab], unembed_rows)
    common = common.reshape(16, 8, few, pair).transpose(1, 0, 2, 3).reshape(2, 4, 16 * few, pair)

    mine = lax.dynamic_index_in_dim(
        labels.reshape(16, 2, 8, few, samples), core, 1, keepdims=False
    )
    shifted = mine.transpose(1, 0, 2, 3).reshape(core_tokens * samples) - narrow * vocab
    chosen = (shifted[:, None] == lax.broadcasted_iota(jnp.int32, (1, vocab), 1)).astype(BF16)
    picked = contract_last(chosen, unembed_rows).astype(BF16)
    picked = picked.reshape(2, 4, 16 * few * samples, pair)
    common, picked = reduce_over("narrow", [common, picked], [F32, BF16], 4, "reduce_grads")
    grads = common.reshape(16, few, 1, pair) - picked.astype(F32).reshape(16, few, samples, pair)
    (grads,) = exchange([grads.reshape(16, few * samples, pair)], [], 5, "exchange_grads")
    grads = grads.transpose(1, 0, 2).reshape(few, samples, width)
    resid_few = lax.dynamic_slice_in_dim(resid_float, narrow * few, few, 0)
    inverse_few = lax.dynamic_slice_in_dim(inverse, narrow * few, few, 0)
    inner = jnp.sum(final_gain * grads * resid_few[:, None, :], axis=2)
    back = (
        inverse_few[:, None, None] * final_gain * grads
        - resid_few[:, None, :] * (inverse_few**3)[:, None, None] * inner[:, :, None] / width
    )
    back = back.astype(BF16).reshape(2, few * samples // 2, width)
    back = gather_narrow(back, 6, "gather_back").reshape(tokens * samples, width)
    hidden_grads = jnp.dot(back, down_rows, preferred_element_type=F32)
    gated = hidden_grads.reshape(tokens, samples, hidden) * gate_value.astype(F32)[:, None, :]
    gated = gated.astype(BF16).transpose(1, 0, 2)
    gated = gather_wide(gated, True, 7, "gather_gated")
    part_rot = rotate(
        gated.reshape(8, 8 * tokens, hidden), basis_rows.reshape(2 * columns, hidden)
    )
    rotated, inputs_other = total_narrow(
        part_rot.reshape(2, 4, 2 * columns, 8 * tokens), inputs_all, 8, "total"
    )
    return squares(rotated.reshape(8, 2, columns, 8 * tokens), inputs_all, inputs_other)


def solution(mesh):
    in_specs = (
        P("wide", None),
        P(),
        P("narrow", "wide"),
        P(),
        P("wide", None),
        P("wide", "narrow"),
        P("narrow", "wide"),
        P("wide", "narrow"),
        P("narrow", "wide"),
    )
    out_specs = P("wide", "narrow")
    return jax.shard_map(
        per_device, mesh=mesh, in_specs=in_specs, out_specs=out_specs, check_vma=False
    )
```

time: 970 us -> 528 us (0.54)
  Pallas kernels: 0 us -> 465 us
  blocking collectives: 420 us -> 0 us
  waiting for transfers between devices: 378 us -> 0.73 us
  local copies, waits for them, and re-layouts: 73.6 us -> 17 us
  starting transfers between devices: 17.7 us -> 0.01 us
  other arithmetic: 21.8 us -> 6.78 us
  matrix products: 36.4 us -> 24.6 us
    pallas_call x0 -> x11, Pallas kernels: none -> 465 us  [the longest x9 442 us: call(): pl.pallas_call(kernel, out_shape=outs, in_specs=in_specs, out_specs=out_s...]
    psum x2 -> x0, blocking collectives: 335 us -> none  [the longest x1 199 us: per_device(): inputs_rot = lax.psum(inputs_part, 'wide').astype(jnp.bfloat16)]
    reduce_scatter x1 -> x0, waiting for transfers between devices: 115 us -> none  [per_device(): lax.psum_scatter(contract_last(normed, unembed), 'wide', scatter_dimensio...]
    all_gather x3 -> x1, waiting for transfers between devices: 104 us -> 0.02 us  [per_device(): down_rows = lax.all_gather(down_weight.T, 'wide', axis=0, tiled=True)]
    all_to_all x4 -> x0, blocking collectives: 84.8 us -> none  [the longest x1 38.1 us: per_device(): lax.all_to_all(layer_in, 'wide', split_axis=1, concat_axis=0, tiled=True)]
    psum x1 -> x0, waiting for transfers between devices: 84.4 us -> none  [per_device(): label_grads = lax.psum(label_part, 'narrow')]
    all_to_all x2 -> x0, waiting for transfers between devices: 74.1 us -> none  [the longest x1 63.1 us: per_device(): lax.all_to_all(label_grads, 'wide', split_axis=0, concat_axis=1, tiled=True)]
    all_to_all x2 -> x0, starting transfers between devices: 17.4 us -> none  [the longest x1 13.1 us: per_device(): lax.all_to_all(label_grads, 'wide', split_axis=0, concat_axis=1, tiled=True)]
  transfers between devices with their start and end apart: 7 -> 1, of which waited for: 6 -> 0; matrix products, arithmetic and copies ran while one was open for 6% -> 7% of each run, Pallas kernels for 0% -> 49%
where the time goes in v1:
time: 528 us; the launch traced here: 527 us
  Pallas kernels  465 us (88%)
  matrix products  24.6 us (5%)
  local copies, waits for them, and re-layouts  17 us (3%)
  between operations  13.8 us (3%)
  other arithmetic  6.78 us (1%)
    pallas_call x9, Pallas kernels, call(): pl.pallas_call(kernel, out_shape=outs, in_specs=in_specs, out_specs=out_s...  442 us
    pallas_call x1, Pallas kernels, rotate(): pl.pallas_call(kernel, grid=(chunks,), out_shape=like((chunks, columns, r...  13.1 us
  transfers between devices with their start and end apart: 1, of which 0 were waited for; matrix products, arithmetic and copies ran while one was open for 7% of the time, Pallas kernels for 49%

profile of v1, /device:TPU:1, one launch (start us, length us, event | category | flops | bytes accessed | tf_op | source)
XLA Modules:
  0.0 527.4 jit_solution(10331796507723593941)
XLA Ops:
  6.5 0.7 all-gather.2.cloned.1.call-update
  7.3 1.9 convert_element_type.25
  9.1 0.1 mul.131
  9.2 0.2 multiply_reduce_fusion
  9.4 0.2 multiply_convert_fusion
  9.5 0.3 reshape.133
  9.9 0.3 reshape.134
  10.2 1.1 copy_bitcast_fusion.1
  11.3 86.6 %exchange.1 = (bf16[16,32,320]{2,1,0:T(8,128)(2,1)}, bf16[16,32,320]{2,1,0:T(8,128)(2,1)}, bf16[2,160,2048]{2,1,0:T(8,128)(2,1)}, bf16[2,160,640]{2,1,0:T(8,128)(2,1)}, bf16[2,432,1728]{2,1,0:T(8,128)(2,1)}) custom-call(bf16[16,32,320]{2,1,0:T(8,128)(2,1)} %get-tuple-element.33.refs_0_, bf16[16,32,320]{2,1,0:T(8,128)(2,1)} %get-tuple-element.32.refs_1_, ...), custom_call_target="tpu_custom_call" | custom-call | tf_op jit(solution)/shard_map/exchange/pallas_call | solution.py:266
  97.9 2.8 fusion.17.refs_1_
  100.7 3.3 fusion.16.refs_0_
  104.0 69.1 %reduce_logits.1 = (f32[32,2048]{1,0:T(8,128)}, bf16[32,640]{1,0:T(8,128)(2,1)}) custom-call(f32[4,4,32,2048]{3,2,1,0:T(8,128)} %fusion.16.refs_0_, f32[4,4,32,640]{3,2,1,0:T(8,128)} %fusion.17.refs_1_), custom_call_target="tpu_custom_call" | custom-call | tf_op jit(solution)/shard_map/reduce_logits/pallas_call | solution.py:266
  173.1 19.0 %softmax.1 = bf16[32,2048]{1,0:T(8,128)(2,1)} custom-call(f32[32,2048]{1,0:T(8,128)} %get-tuple-element.20.l_ref), custom_call_target="tpu_custom_call" | custom-call | tf_op jit(solution)/shard_map/softmax/pallas_call | solution.py:266
  192.1 1.6 pad_maximum_fusion
  193.7 30.6 %gather_probs.1 = bf16[4,4,2,16,2688]{4,3,2,1,0:T(8,128)(2,1)} custom-call(bf16[2,16,2688]{2,1,0:T(8,128)(2,1)} %bitcast.79), custom_call_target="tpu_custom_call" | custom-call | tf_op jit(solution)/shard_map/gather_probs/pallas_call | solution.py:266
  224.3 1.7 slice.8
  226.1 2.0 slice.9
  228.1 0.5 reshape.140
  228.7 0.9 copy.18
  229.6 0.3 sub.40
  229.8 5.2 fusion.4
  235.0 1.6 copy.19
  236.6 2.2 dot_general.27
  238.8 3.5 fusion.18
  242.4 0.2 reshape.155
  242.6 1.0 copy.27.refs_0_
  243.6 24.2 %reduce_grads.1 = (f32[64,320]{1,0:T(8,128)}, bf16[256,320]{1,0:T(8,128)(2,1)}) custom-call(f32[2,4,64,320]{3,2,1,0:T(8,128)} %copy.27.refs_0_, bf16[2,4,256,320]{3,2,1,0:T(8,128)(2,1)} %bitcast.68), custom_call_target="tpu_custom_call" | custom-call | tf_op jit(solution)/shard_map/reduce_grads/pallas_call | solution.py:266
  267.8 1.0 sub.41
  268.9 0.1 sub.43
  269.0 0.8 convert_subtract_fusion.refs_0_
  269.8 14.6 %exchange_grads.1 = f32[16,16,320]{2,1,0:T(8,128)} custom-call(f32[16,16,320]{2,1,0:T(8,128)} %convert_subtract_fusion.refs_0_), custom_call_target="tpu_custom_call" | custom-call | tf_op jit(solution)/shard_map/exchange_grads/pallas_call | solution.py:266
  284.4 0.1 multiply_multiply_fusion
  284.5 1.0 broadcast_multiply_fusion
  285.6 0.2 mul.135
  285.8 0.3 fusion.15
  286.1 0.1 mul.137
  286.1 0.1 copy.20
  286.3 0.1 reshape.144
  286.5 0.1 mul.120
  286.7 0.1 mul.130
  286.8 0.8 subtract_convert_fusion.x_ref
  287.6 12.1 %gather_back.1 = bf16[2,4,2,8,5120]{4,3,2,1,0:T(8,128)(2,1)} custom-call(bf16[2,8,5120]{2,1,0:T(8,128)(2,1)} %subtract_convert_fusion.x_ref), custom_call_target="tpu_custom_call" | custom-call | tf_op jit(solution)/shard_map/gather_back/pallas_call | solution.py:266
  299.7 2.6 dot_general.30
  302.4 9.8 %fusion.11.x_ref = bf16[4,32,1728]{2,1,0:T(8,128)(2,1)} fusion(bf16[5120,1728]{1,0:T(8,128)(2,1)} %all-gather.2.cloned.1.call-done, bf16[32,4,5120]{2,1,0:T(4,128)(2,1)S(1)} %dot_general.30, f32[32,1728]{1,0:T(8,128)S(1)} %convert_element_type.29), kind=kOutput, calls=%fused_computation.8 | convolution fusion | flops 2265366528 | bytes 19668992 | tf_op jit(solution)/shard_map/dot_general | solution.py:647
  312.2 56.7 %gather_gated.1 = bf16[4,4,4,32,1728]{4,3,2,1,0:T(8,128)(2,1)} custom-call(bf16[4,32,1728]{2,1,0:T(8,128)(2,1)} %fusion.11.x_ref), custom_call_target="tpu_custom_call" | custom-call | tf_op jit(solution)/shard_map/gather_gated/pallas_call | solution.py:266
  368.9 13.1 %rotate.1 = f32[8,864,256]{2,1,0:T(8,128)} custom-call(bf16[8,256,1728]{2,1,0:T(8,128)(2,1)} %bitcast.64, bf16[864,1728]{1,0:T(8,128)(2,1)} %bitcast.74), custom_call_target="tpu_custom_call" | custom-call | tf_op jit(solution)/shard_map/rotate/pallas_call | solution.py:482
  382.0 128.7 %total.1 = (bf16[2,4,2,432,256]{4,3,2,1,0:T(8,128)(2,1)}, bf16[4,128,640]{2,1,0:T(8,128)(2,1)}) custom-call(f32[2,4,864,256]{3,2,1,0:T(8,128)} %bitcast.65, bf16[4,128,640]{2,1,0:T(8,128)(2,1)} %bitcast.69), custom_call_target="tpu_custom_call" | custom-call | tf_op jit(solution)/shard_map/total/pallas_call | solution.py:266
  510.7 9.9 %squares.1 = f32[432,640]{1,0:T(8,128)} custom-call(bf16[8,2,432,256]{3,2,1,0:T(8,128)(2,1)} %bitcast.72, bf16[4,128,640]{2,1,0:T(8,128)(2,1)} %bitcast.70, bf16[4,128,640]{2,1,0:T(8,128)(2,1)} %get-tuple-element.26.b_ref), custom_call_target="tpu_custom_call" | custom-call | tf_op jit(solution)/shard_map/squares/pallas_call | solution.py:556
  (30 shorter events, 0.4 us)
Async XLA Ops:
  6.5 2.7 copy-start.1
  6.5 2.6 copy-start.7
  6.5 295.9 %all-gather.2.cloned.1.call-start = ((), (), s32[]{:S(2)}) async-start(), calls=%async_computation | async-start | bytes 18923520 | tf_op jit(solution)/shard_map/all_gather | solution.py:589
  6.5 3.3 copy-start.5
  97.8 2.8 copy-start.2
  97.9 2.8 copy-start.4
  224.3 3.8 copy-start.9
  236.6 2.2 copy-start.3
  267.8 1.2 copy-start.6
  284.4 1.4 copy-start
  299.7 2.6 copy-start.8
Sparse Core Ops, SparseCore 0:
  9.9 130.0 all-gather.1

commit v2 on v1

--- a/solution.py
+++ b/solution.py
@@ -130,11 +130,14 @@
         for h in range(2):
             net.send(base + h, own(h), slot(me_o, me_i, h), on_o(1))
         along(0, me_o, True)
+        yield
         forward(0, me_o)
         for h in range(2):
             net.recv(base + h, slot(oq, me_i, h))
         along(1, oq, False)
+        yield
         forward(1, oq)
+        yield
         rest(0, me_o)
         rest(1, oq)
 
@@ -226,18 +229,21 @@
                 s.tot[2, s.h(1)] += s.zfwd[1]
                 net.send(z + 5, s.tot.at[2, s.h(1)], s.zgot.at[1, s.h(1)], on_o(3))
 
-    start_far(0)
-    start_far(1)
-    start_near(0)
-    for k in range(outer_size):
-        if k + 2 < outer_size:
-            start_far(k + 2)
-        if k + 1 < outer_size:
-            start_near(k + 1)
-        middle(k)
-        if k >= 1:
-            total(k - 1)
-    total(outer_size - 1)
+    def steps():
+        start_far(0)
+        start_far(1)
+        start_near(0)
+        yield
+        for k in range(outer_size):
+            if k + 2 < outer_size:
+                start_far(k + 2)
+            if k + 1 < outer_size:
+                start_near(k + 1)
+            middle(k)
+            if k >= 1:
+                total(k - 1)
+            yield
+        total(outer_size - 1)
 
     def final(a):
         s = sums[a]
@@ -255,14 +261,20 @@
 
         return value
 
-    return [final(a) for a in range(len(sums))]
+    return steps(), [final(a) for a in range(len(sums))]
+
+
+def drive(*stages):
+    stages = list(stages)
+    while stages:
+        stages = [stage for stage in stages if next(stage, 0) is None]
 
 
 def sems(slots):
     return [pltpu.SemaphoreType.DMA((slots,)), pltpu.SemaphoreType.DMA((slots,))]
 
 
-def call(kernel, collective_id, outs, in_specs, out_specs, scratch, args, name):
+def call(kernel, collective_id, outs, in_specs, out_specs, scratch, args, name, cost):
     return pl.pallas_call(
         kernel,
         out_shape=outs,
@@ -272,6 +284,7 @@
         compiler_params=pltpu.CompilerParams(
             collective_id=collective_id, has_side_effects=True, vmem_limit_bytes=60 << 20
         ),
+        cost_estimate=pl.CostEstimate(flops=cost * 10**9, bytes_accessed=0, transcendentals=0),
         name=name,
     )(*args)
 
@@ -280,7 +293,7 @@
     return jax.ShapeDtypeStruct(shape, dtype)
 
 
-def exchange(arrays, pairs, collective_id, name):
+def exchange(arrays, pairs, collective_id, name, cost):
     na, np_ = len(arrays), len(pairs)
 
     def kernel(*refs):
@@ -330,20 +343,18 @@
         [pltpu.SemaphoreType.DMA((na + np_,)), *sems(15 * na + max(np_, 1))],
         (*arrays, *pairs),
         name,
-    )
-
-
-def gather_wide(shard, spread, collective_id, name):
+        cost,
+    )
+
+
+def gather_wide(shard, collective_id, name, cost):
     half = shard.shape[0] // 2
-    shape = (4, shard.shape[0], 4, *shard.shape[1:]) if spread else (4, 4, *shard.shape)
+    shape = (4, 4, *shard.shape)
 
     def kernel(x_ref, o_ref, local, send_sem, recv_sem):
         net = Net(send_sem, recv_sem)
 
-        def slot(o, i, h):
-            part = pl.ds(h * half, half)
-            return o_ref.at[o, part, i] if spread else o_ref.at[o, i, part]
-
+        slot = lambda o, i, h: o_ref.at[o, i, pl.ds(h * half, half)]
         net.greet([net.on_x(1), net.on_x(3), net.on_z(1), net.on_z(3)])
         own = lambda h: x_ref.at[pl.ds(h * half, half)]
         copies = [
@@ -351,7 +362,7 @@
         ]
         for copy in copies:
             copy.start()
-        gather_stage(net, 0, own, slot, 4, net.z, net.x, net.on_z, net.on_x)
+        drive(gather_stage(net, 0, own, slot, 4, net.z, net.x, net.on_z, net.on_x))
         for copy in copies:
             copy.wait()
         net.finish()
@@ -365,54 +376,35 @@
         [pltpu.SemaphoreType.DMA((2,)), *sems(gather_slots(4))],
         (shard,),
         name,
-    )
-
-
-def gather_narrow(shard, collective_id, name):
-    half = shard.shape[0] // 2
-
-    def kernel(x_ref, o_ref, local, send_sem, recv_sem):
-        net = Net(send_sem, recv_sem)
-        slot = lambda o, i, h: o_ref.at[o, i, pl.ds(h * half, half)]
-        net.greet([net.on_y(1), net.on_y(3), net.on_zl(1)])
-        own = lambda h: x_ref.at[pl.ds(h * half, half)]
-        copies = [
-            pltpu.make_async_copy(own(h), slot(net.zl, net.y, h), local.at[h]) for h in range(2)
-        ]
-        for copy in copies:
-            copy.start()
-        gather_stage(net, 0, own, slot, 2, net.zl, net.y, net.on_zl, net.on_y)
-        for copy in copies:
-            copy.wait()
-        net.finish()
-
-    return call(
-        kernel,
-        collective_id,
-        like((2, 4, *shard.shape), shard.dtype),
-        [ANY],
-        ANY,
-        [pltpu.SemaphoreType.DMA((2,)), *sems(gather_slots(2))],
-        (shard,),
-        name,
-    )
-
-
-def reduce_over(axis, parts, dtypes, collective_id, name):
-    n = len(parts)
-    outer = parts[0].shape[0]
+        cost,
+    )
+
+
+def reduce_over(wide_parts, narrow_parts, dtypes, collective_id, name, cost):
+    parts = [*wide_parts, *narrow_parts]
+    n, split = len(parts), len(wide_parts)
 
     def kernel(*refs):
         ins, outs = refs[:n], refs[n : 2 * n]
         buffers, (send_sem, recv_sem) = refs[2 * n : -2], refs[-2:]
         net = Net(send_sem, recv_sem)
         sums = [Sum(ins[a], *buffers[6 * a : 6 * a + 6]) for a in range(n)]
-        if axis == "wide":
-            net.greet([net.on_x(1), net.on_x(3), net.on_z(1), net.on_z(3)])
-            ends = reduce_stage(net, 0, sums, 4, net.z, net.x, net.on_z, net.on_x)
-        else:
-            net.greet([net.on_y(1), net.on_y(3), net.on_zl(1)])
-            ends = reduce_stage(net, 0, sums, 2, net.zl, net.y, net.on_zl, net.on_y)
+        stages, ends, peers = [], [], []
+        if split:
+            peers += [net.on_x(1), net.on_x(3), net.on_z(1), net.on_z(3)]
+            stage, end = reduce_stage(net, 0, sums[:split], 4, net.z, net.x, net.on_z, net.on_x)
+            stages.append(stage)
+            ends += end
+        if n > split:
+            peers += [net.on_y(1), net.on_y(3), net.on_zl(1)]
+            base = split * reduce_slots(4)
+            stage, end = reduce_stage(
+                net, base, sums[split:], 2, net.zl, net.y, net.on_zl, net.on_y
+            )
+            stages.append(stage)
+            ends += end
+        net.greet(peers)
+        drive(*stages)
         for a in range(n):
             for h in range(2):
                 outs[a][sums[a].h(h), :] = ends[a](h).astype(outs[a].dtype)
@@ -420,20 +412,22 @@
 
     scratch = []
     for p in parts:
-        scratch += Sum.scratch(outer, p.shape[2], p.shape[3], p.dtype)
+        scratch += Sum.scratch(p.shape[0], p.shape[2], p.shape[3], p.dtype)
+    slots = split * reduce_slots(4) + (n - split) * reduce_slots(2)
     return call(
         kernel,
         collective_id,
         [like(p.shape[2:], d) for p, d in zip(parts, dtypes)],
         [VMEM] * n,
         [VMEM] * n,
-        [*scratch, *sems(n * reduce_slots(outer))],
+        [*scratch, *sems(slots)],
         tuple(parts),
         name,
-    )
-
-
-def softmax_narrow(logits, collective_id, name):
+        cost,
+    )
+
+
+def softmax_narrow(logits, collective_id, name, cost):
     rows, columns = logits.shape
 
     def kernel(l_ref, p_ref, mine, got, send_sem, recv_sem):
@@ -467,55 +461,26 @@
         [pltpu.VMEM((2, rows, 128), F32), pltpu.VMEM((7, 2, rows, 128), F32), *sems(7)],
         (logits,),
         name,
-    )
-
-
-def rotate(gated, basis):
-    chunks, rows, depth = gated.shape
-    columns = basis.shape[0]
-
-    def kernel(g_ref, b_ref, o_ref):
-        o_ref[0] = lax.dot_general(
-            b_ref[...], g_ref[0], (((1,), (1,)), ((), ())), preferred_element_type=F32
-        )
-
-    return pl.pallas_call(
-        kernel,
-        grid=(chunks,),
-        out_shape=like((chunks, columns, rows), F32),
-        in_specs=[
-            pl.BlockSpec((1, rows, depth), lambda i: (i, 0, 0)),
-            pl.BlockSpec((columns, depth), lambda i: (0, 0)),
-        ],
-        out_specs=pl.BlockSpec((1, columns, rows), lambda i: (i, 0, 0)),
-        name="rotate",
-    )(gated, basis)
-
-
-def total_narrow(part, inputs, collective_id, name):
-    rows, columns = part.shape[2] // 2, part.shape[3]
-
-    def kernel(p_ref, i_ref, o_ref, j_ref, *refs):
-        buffers, (mine, local, send_sem, recv_sem) = refs[:6], refs[6:]
+        cost,
+    )
+
+
+def gather_back(shard, collective_id, name, cost):
+    _, rows, features = shard.shape
+
+    def kernel(x_ref, o_ref, mine, local, send_sem, recv_sem):
         net = Net(send_sem, recv_sem)
         net.greet([net.on_y(1), net.on_y(3), net.on_zl(1), net.on_core()])
-        base = reduce_slots(2)
-        net.send(base, i_ref, j_ref, net.on_core())
-        sums = [Sum(p_ref, *buffers)]
-        (end,) = reduce_stage(net, 0, sums, 2, net.zl, net.y, net.on_zl, net.on_y)
-        for h in range(2):
-            mine[h] = end(h).astype(BF16)
-        net.send(base + 1, mine.at[1 - net.core], mine.at[2], net.on_core())
-        net.recv(base + 1, mine.at[2])
-        slot = lambda o, i, h: o_ref.at[o, i, h]
-        own = lambda h: mine.at[2 if h else net.core]
+        net.send(0, x_ref.at[1 - net.core], mine, net.on_core())
+        slot = lambda o, i, h: o_ref.at[o, i, lax.rem(net.core + h, 2)]
+        own = lambda h: mine if h else x_ref.at[net.core]
+        net.recv(0, mine)
         copies = [
             pltpu.make_async_copy(own(h), slot(net.zl, net.y, h), local.at[h]) for h in range(2)
         ]
         for copy in copies:
             copy.start()
-        gather_stage(net, base + 2, own, slot, 2, net.zl, net.y, net.on_zl, net.on_y)
-        net.recv(base, j_ref)
+        drive(gather_stage(net, 1, own, slot, 2, net.zl, net.y, net.on_zl, net.on_y))
         for copy in copies:
             copy.wait()
         net.finish()
@@ -523,46 +488,260 @@
     return call(
         kernel,
         collective_id,
-        [like((2, 4, 2, rows, columns), BF16), like(inputs.shape, BF16)],
-        [VMEM, ANY],
+        like((2, 4, 2, rows, features), shard.dtype),
+        [ANY],
+        ANY,
+        [
+            pltpu.VMEM((rows, features), shard.dtype),
+            pltpu.SemaphoreType.DMA((2,)),
+            *sems(1 + gather_slots(2)),
+        ],
+        (shard,),
+        name,
+        cost,
+    )
+
+
+def rotate_all(hidden, gate, bases, inputs, collective_id, name, cost):
+    tokens, depth = gate.shape
+    columns = bases[0].shape[0]
+    rows = 2 * tokens
+
+    def kernel(*refs):
+        h_ref, g_ref = refs[:2]
+        b_refs, i_ref, o_ref, j_ref = refs[2:6], refs[6], refs[7], refs[8]
+        half_in, gated, other, every, part, fwd, mid, got, mine = refs[9:18]
+        local, send_sem, recv_sem = refs[18:]
+        net = Net(send_sem, recv_sem)
+        ones = [net.on_x(1), net.on_x(3), net.on_z(1), net.on_z(3)]
+        net.greet(ones + [net.on_y(1), net.on_y(3), net.on_zl(1), net.on_core()])
+        c, z, x, zl, y = net.core, net.z, net.x, net.zl, net.y
+        base_z, base_r, base_n = 8, 40, 64
+
+        net.send(0, h_ref.at[1 - c], half_in, net.on_core())
+        net.send(1, i_ref, j_ref, net.on_core())
+        net.recv(0, half_in)
+
+        def gate_rows(s):
+            cut = pl.ds(pl.multiple_of(s * tokens, tokens), tokens)
+            value = (h_ref[c, cut] + half_in[cut]) * g_ref[...].astype(F32)
+            gated[s] = value.astype(BF16)
+
+        for s in range(2):
+            gate_rows(2 * (1 - zl) + s)
+        net.send(2, gated.at[pl.ds(2 * (1 - zl), 2)], other, net.on_zl(1))
+        for s in range(2):
+            gate_rows(2 * zl + s)
+
+        own = lambda h: other if h else gated.at[pl.ds(2 * zl, 2)]
+        slot = lambda o, i, h: every.at[o, h, i]
+        zp, zm, z2 = (turn(z, s, 4) for s in (1, 3, 2))
+        xp, xm, x2 = (turn(x, s, 4) for s in (1, 3, 2))
+        yp, ym, y2 = (turn(y, s, 4) for s in (1, 3, 2))
+        order = (z, zm, zp, z2)
+        inner = lambda row: base_z + 6 + 6 * row
+
+        def along(row, h):
+            o, b = order[row], inner(row)
+            src = own(h) if row == 0 else slot(o, x, h)
+            net.send(b + (0, 1)[h], src, slot(o, x, h), net.on_x(1))
+            net.send(b + (3, 2)[h], src, slot(o, x, h), net.on_x(3))
+
+        def forward(row):
+            o, b = order[row], inner(row)
+            net.recv(b, slot(o, xm, 0))
+            net.send(b + 4, slot(o, xm, 0), slot(o, xm, 0), net.on_x(1))
+            net.recv(b + 2, slot(o, xp, 1))
+            net.send(b + 5, slot(o, xp, 1), slot(o, xp, 1), net.on_x(3))
+
+        def rest(row):
+            o, b = order[row], inner(row)
+            net.recv(b + 1, slot(o, xm, 1))
+            net.recv(b + 3, slot(o, xp, 0))
+            net.recv(b + 4, slot(o, x2, 0))
+            net.recv(b + 5, slot(o, x2, 1))
+
+        def multiply(row):
+            o = order[row]
+            for m in range(2):
+                block = None
+                for h in range(2):
+                    left = every[o, h].reshape(4 * rows, depth)
+                    term = contract_last(left, b_refs[2 * h + m][...])
+                    block = term if block is None else block + term
+                part[row, :, m] = block.reshape(4, rows, columns)
+
+        def reduce_start(k):
+            b = base_r + 6 * k
+            net.send(b, part.at[k, y2, 0], fwd.at[k, 0], net.on_y(1))
+            net.send(b + 1, part.at[k, y2, 1], fwd.at[k, 1], net.on_y(3))
+            net.send(b + 2, part.at[k, yp, 1], got.at[k, 0, 1], net.on_y(1))
+            net.send(b + 3, part.at[k, ym, 0], got.at[k, 1, 0], net.on_y(3))
+
+        def reduce_middle(k):
+            b = base_r + 6 * k
+            net.recv(b, fwd.at[k, 0])
+            mid[k, 0] = part[k, yp, 0] + fwd[k, 0]
+            net.send(b + 4, mid.at[k, 0], got.at[k, 0, 0], net.on_y(1))
+            net.recv(b + 1, fwd.at[k, 1])
+            mid[k, 1] = part[k, ym, 1] + fwd[k, 1]
+            net.send(b + 5, mid.at[k, 1], got.at[k, 1, 1], net.on_y(3))
+
+        def reduce_end(k):
+            b = base_r + 6 * k
+            net.recv(b + 2, got.at[k, 0, 1])
+            net.recv(b + 5, got.at[k, 1, 1])
+            value = part[k, y, 1] + got[k, 0, 1] + got[k, 1, 1]
+            mine[k, 1] = value.astype(BF16).reshape(2, tokens, columns)
+            net.send(3 + k, mine.at[k, 1], mine.at[k, 2], net.on_core())
+            net.recv(b + 3, got.at[k, 1, 0])
+            net.recv(b + 4, got.at[k, 0, 0])
+            value = part[k, y, 0] + got[k, 0, 0] + got[k, 1, 0]
+            mine[k, 0] = value.astype(BF16).reshape(2, tokens, columns)
+
+        last = []
+
+        def spread(k):
+            mine_k = lambda h: mine.at[k, 2 * h]
+            place = lambda o, i, h: o_ref.at[order[k], o, :, h, i]
+            net.recv(3 + k, mine.at[k, 2])
+            for h in range(2):
+                copy = pltpu.make_async_copy(mine_k(h), place(zl, y, h), local.at[2 + 2 * k + h])
+                copy.start()
+                last.append(copy)
+            base = base_n + gather_slots(2) * k
+            return gather_stage(net, base, mine_k, place, 2, zl, y, net.on_zl, net.on_y)
+
+        net.send(base_z, own(0), slot(z, x, 0), net.on_z(1))
+        net.send(base_z + 3, own(0), slot(z, x, 0), net.on_z(3))
+        along(0, 0)
+        net.recv(2, other)
+        net.send(base_z + 2, own(1), slot(z, x, 1), net.on_z(3))
+        net.send(base_z + 1, own(1), slot(z, x, 1), net.on_z(1))
+        along(0, 1)
+        copies = [pltpu.make_async_copy(own(h), slot(z, x, h), local.at[h]) for h in range(2)]
+        for copy in copies:
+            copy.start()
+        net.recv(base_z, slot(zm, x, 0))
+        net.send(base_z + 4, slot(zm, x, 0), slot(zm, x, 0), net.on_z(1))
+        net.recv(base_z + 2, slot(zp, x, 1))
+        net.send(base_z + 5, slot(zp, x, 1), slot(zp, x, 1), net.on_z(3))
+        forward(0)
+        net.recv(base_z + 1, slot(zm, x, 1))
+        for h in range(2):
+            along(1, h)
+        rest(0)
+        for copy in copies:
+            copy.wait()
+        multiply(0)
+        reduce_start(0)
+        net.recv(base_z + 3, slot(zp, x, 0))
+        for h in range(2):
+            along(2, h)
+        forward(1)
+        reduce_middle(0)
+        rest(1)
+        multiply(1)
+        reduce_start(1)
+        net.recv(base_z + 4, slot(z2, x, 0))
+        net.recv(base_z + 5, slot(z2, x, 1))
+        for h in range(2):
+            along(3, h)
+        forward(2)
+        reduce_end(0)
+        reduce_middle(1)
+        spread_0 = spread(0)
+        next(spread_0)
+        rest(2)
+        multiply(2)
+        reduce_start(2)
+        forward(3)
+        next(spread_0)
+        reduce_end(1)
+        reduce_middle(2)
+        spread_1 = spread(1)
+        next(spread_1)
+        next(spread_0)
+        rest(3)
+        multiply(3)
+        reduce_start(3)
+        next(spread_1)
+        reduce_end(2)
+        reduce_middle(3)
+        spread_2 = spread(2)
+        next(spread_2)
+        next(spread_1)
+        reduce_end(3)
+        spread_3 = spread(3)
+        next(spread_3)
+        drive(spread_0)
+        for stage in (spread_2, spread_3, spread_2, spread_3):
+            next(stage)
+        drive(spread_1)
+        drive(spread_2)
+        drive(spread_3)
+        for copy in last:
+            copy.wait()
+        net.recv(1, j_ref)
+        net.finish()
+
+    return call(
+        kernel,
+        collective_id,
+        [like((4, 2, 2, 2, 4, tokens, columns), BF16), like(inputs.shape, BF16)],
+        [VMEM] * 6 + [ANY],
         [ANY, ANY],
         [
-            *Sum.scratch(2, 2 * rows, columns, F32),
-            pltpu.VMEM((3, rows, columns), BF16),
-            pltpu.SemaphoreType.DMA((2,)),
-            *sems(reduce_slots(2) + 2 + gather_slots(2)),
+            pltpu.VMEM((4 * tokens, depth), F32),
+            pltpu.VMEM((4, tokens, depth), BF16),
+            pltpu.VMEM((2, tokens, depth), BF16),
+            pltpu.VMEM((4, 2, 4, 2, tokens, depth), BF16),
+            pltpu.VMEM((4, 4, 2, rows, columns), F32),
+            pltpu.VMEM((4, 2, rows, columns), F32),
+            pltpu.VMEM((4, 2, rows, columns), F32),
+            pltpu.VMEM((4, 2, 2, rows, columns), F32),
+            pltpu.VMEM((4, 3, 2, tokens, columns), BF16),
+            pltpu.SemaphoreType.DMA((10,)),
+            *sems(64 + 4 * gather_slots(2)),
         ],
-        (part, inputs),
+        (hidden, gate, *bases, inputs),
         name,
+        cost,
     )
 
 
 def squares(rotated, own_inputs, other_inputs):
-    rows, width = rotated.shape[2], own_inputs.shape[2]
-
-    def kernel(r_ref, a_ref, b_ref, o_ref):
-        step = pl.program_id(0)
-
-        @pl.when(step == 0)
+    rows, width = rotated.shape[3], own_inputs.shape[2]
+    depth = own_inputs.shape[1]
+
+    def kernel(r_ref, a_ref, b_ref, o_ref, both):
+        example, sample = pl.program_id(0), pl.program_id(1)
+
+        @pl.when((example == 0) & (sample == 0))
         def _():
             o_ref[...] = jnp.zeros_like(o_ref)
 
-        for s in range(2):
-            cut = pl.ds(s * 128, 128)
-            block = jnp.dot(r_ref[0, 0, :, cut], a_ref[0], preferred_element_type=F32)
-            block += jnp.dot(r_ref[0, 1, :, cut], b_ref[0], preferred_element_type=F32)
-            o_ref[...] += block * block * (1.0 / 16.0)
+        @pl.when(sample == 0)
+        def _():
+            both[:depth] = a_ref[0]
+            both[depth:] = b_ref[0]
+
+        block = lax.dot_general(
+            r_ref[0, 0], both[...], (((0,), (0,)), ((), ())), preferred_element_type=F32
+        )
+        o_ref[...] += block * block * (1.0 / 16.0)
 
     return pl.pallas_call(
         kernel,
-        grid=(8,),
+        grid=(4, 4),
         out_shape=like((rows, width), F32),
         in_specs=[
-            pl.BlockSpec((1, 2, rows, 256), lambda i: (i, 0, 0, 0)),
-            pl.BlockSpec((1, 128, width), lambda i: (i // 2, 0, 0)),
-            pl.BlockSpec((1, 128, width), lambda i: (i // 2, 0, 0)),
+            pl.BlockSpec((1, 1, 2 * depth, rows), lambda e, s: (e, s, 0, 0)),
+            pl.BlockSpec((1, depth, width), lambda e, s: (e, 0, 0)),
+            pl.BlockSpec((1, depth, width), lambda e, s: (e, 0, 0)),
         ],
-        out_specs=pl.BlockSpec((rows, width), lambda i: (0, 0)),
+        out_specs=pl.BlockSpec((rows, width), lambda e, s: (0, 0)),
+        scratch_shapes=[pltpu.VMEM((2 * depth, width), BF16)],
         name="squares",
     )(rotated, own_inputs, other_inputs)
 
@@ -586,8 +765,6 @@
     core_tokens = 16 * tokens
     few = tokens // 8
 
-    down_rows = lax.all_gather(down_weight.T, "wide", axis=0, tiled=True)
-
     resid_float = resid.astype(F32)
     inverse = lax.rsqrt(jnp.mean(resid_float * resid_float, axis=1) + EPSILON)
     normed = (resid_float * inverse[:, None] * final_gain).astype(BF16)
@@ -595,11 +772,8 @@
     def blocks(rows):
         return rows.reshape(tokens, 16, pair).transpose(1, 0, 2)
 
-    normed_cols, inputs_cols, unembed_rows, basis_in_rows, basis_rows = exchange(
-        [blocks(normed), blocks(layer_in)],
-        [unembed.T, basis_in, basis_out.T],
-        0,
-        "exchange",
+    normed_cols, inputs_cols, unembed_rows, basis_in_rows = exchange(
+        [blocks(normed), blocks(layer_in)], [unembed.T, basis_in], 0, "exchange", 20
     )
     unembed_rows = unembed_rows.reshape(pair, vocab)
     basis_in_rows = basis_in_rows.reshape(pair, width_in)
@@ -609,31 +783,49 @@
     inputs_part = jnp.dot(
         inputs_cols.reshape(core_tokens, pair), basis_in_rows, preferred_element_type=F32
     )
-    logits, inputs_rot = reduce_over(
-        "wide",
+    mine = lax.dynamic_index_in_dim(
+        labels.reshape(16, 2, 8, few, samples), core, 1, keepdims=False
+    )
+    shifted = mine.transpose(1, 0, 2, 3).reshape(core_tokens * samples) - narrow * vocab
+    chosen = (shifted[:, None] == lax.broadcasted_iota(jnp.int32, (1, vocab), 1)).astype(BF16)
+    picked = contract_last(chosen, unembed_rows).astype(BF16)
+    logits, inputs_rot, picked = reduce_over(
         [logits_part.reshape(4, 4, tokens, vocab), inputs_part.reshape(4, 4, tokens, width_in)],
-        [F32, BF16],
+        [picked.reshape(2, 4, 16 * few * samples, pair)],
+        [F32, BF16, BF16],
         1,
         "reduce_logits",
-    )
-    probs = softmax_narrow(logits, 2, "softmax")
+        45,
+    )
+
+    down_cols, basis_rows, logits = lax.optimization_barrier(
+        (down_weight.T, basis_out.T, logits)
+    )
+    wide_count = lax.axis_size("wide")
+    same_core = [list(range(c, wide_count, 2)) for c in range(2)]
+    down_rows = lax.all_gather(
+        down_cols, "wide", axis=0, tiled=True, axis_index_groups=same_core
+    )
+    to_core = [(w, w + 1 - 2 * (w % 2)) for w in range(wide_count)]
+    to_zl = [(n, (n + 4) % 8) for n in range(8)]
+    basis_zl = lax.ppermute(basis_rows, "narrow", to_zl)
+    bases = [
+        basis_rows,
+        lax.ppermute(basis_rows, "wide", to_core),
+        basis_zl,
+        lax.ppermute(basis_zl, "wide", to_core),
+    ]
+
+    probs = softmax_narrow(logits, 2, "softmax", 6)
     both = jnp.concatenate([probs, inputs_rot], axis=1)
-    both = gather_wide(both.reshape(2, tokens // 2, vocab + width_in), False, 3, "gather_probs")
+    both = gather_wide(both.reshape(2, tokens // 2, vocab + width_in), 3, "gather_probs", 24)
     both = both.reshape(core_tokens, vocab + width_in)
     inputs_all = both[:, vocab:].reshape(4, 4 * tokens, width_in)
     common = contract_last(both[:, :vocab], unembed_rows)
     common = common.reshape(16, 8, few, pair).transpose(1, 0, 2, 3).reshape(2, 4, 16 * few, pair)
-
-    mine = lax.dynamic_index_in_dim(
-        labels.reshape(16, 2, 8, few, samples), core, 1, keepdims=False
-    )
-    shifted = mine.transpose(1, 0, 2, 3).reshape(core_tokens * samples) - narrow * vocab
-    chosen = (shifted[:, None] == lax.broadcasted_iota(jnp.int32, (1, vocab), 1)).astype(BF16)
-    picked = contract_last(chosen, unembed_rows).astype(BF16)
-    picked = picked.reshape(2, 4, 16 * few * samples, pair)
-    common, picked = reduce_over("narrow", [common, picked], [F32, BF16], 4, "reduce_grads")
+    (common,) = reduce_over([], [common], [F32], 4, "reduce_common", 10)
     grads = common.reshape(16, few, 1, pair) - picked.astype(F32).reshape(16, few, samples, pair)
-    (grads,) = exchange([grads.reshape(16, few * samples, pair)], [], 5, "exchange_grads")
+    (grads,) = exchange([grads.reshape(16, few * samples, pair)], [], 5, "exchange_grads", 12)
     grads = grads.transpose(1, 0, 2).reshape(few, samples, width)
     resid_few = lax.dynamic_slice_in_dim(resid_float, narrow * few, few, 0)
     inverse_few = lax.dynamic_slice_in_dim(inverse, narrow * few, few, 0)
@@ -642,19 +834,24 @@
         inverse_few[:, None, None] * final_gain * grads
         - resid_few[:, None, :] * (inverse_few**3)[:, None, None] * inner[:, :, None] / width
     )
-    back = back.astype(BF16).reshape(2, few * samples // 2, width)
-    back = gather_narrow(back, 6, "gather_back").reshape(tokens * samples, width)
-    hidden_grads = jnp.dot(back, down_rows, preferred_element_type=F32)
-    gated = hidden_grads.reshape(tokens, samples, hidden) * gate_value.astype(F32)[:, None, :]
-    gated = gated.astype(BF16).transpose(1, 0, 2)
-    gated = gather_wide(gated, True, 7, "gather_gated")
-    part_rot = rotate(
-        gated.reshape(8, 8 * tokens, hidden), basis_rows.reshape(2 * columns, hidden)
-    )
-    rotated, inputs_other = total_narrow(
-        part_rot.reshape(2, 4, 2 * columns, 8 * tokens), inputs_all, 8, "total"
-    )
-    return squares(rotated.reshape(8, 2, columns, 8 * tokens), inputs_all, inputs_other)
+    back = back.astype(BF16).reshape(few * samples, 16, 2, part).transpose(2, 0, 1, 3)
+    back = gather_back(back.reshape(2, few * samples, width // 2), 6, "gather_back", 16)
+    back = back.reshape(8, 2, few, samples, width // 2).transpose(1, 3, 0, 2, 4)
+    hidden_part = jnp.dot(
+        back.reshape(2 * tokens * samples, width // 2), down_rows, preferred_element_type=F32
+    )
+    rotated, inputs_other = rotate_all(
+        hidden_part.reshape(2, samples * tokens, hidden),
+        gate_value,
+        bases,
+        inputs_all,
+        7,
+        "rotate_all",
+        90,
+    )
+    return squares(
+        rotated.reshape(4, samples, 8 * tokens, columns), inputs_all, inputs_other
+    )
 
 
 def solution(mesh):

time: 528 us -> 508 us (0.962)
  Pallas kernels: 465 us -> 421 us
  starting transfers between devices: 0.01 us -> 25.8 us
    pallas_call x9 -> x8, Pallas kernels: 442 us -> 408 us  [call(): pl.pallas_call(kernel, out_shape=outs, in_specs=in_specs, out_specs=out_s...]
    ppermute x0 -> x3, starting transfers between devices: none -> 25.8 us  [the longest x1 23.6 us: per_device(): lax.ppermute(basis_zl, 'wide', to_core)]
    pallas_call x2 -> x1, Pallas kernels: 23 us -> 12.9 us  [squares(): pl.pallas_call(kernel, grid=(4, 4), out_shape=like((rows, width), F32), i...]
  transfers between devices with their start and end apart: 1 -> 4, of which waited for: 0 -> 0; matrix products, arithmetic and copies ran while one was open for 7% -> 6% of each run, Pallas kernels for 49% -> 32%
where the time goes in v2:
time: 508 us; the launch traced here: 507 us
  Pallas kernels  421 us (83%)
  starting transfers between devices  25.8 us (5%)
  matrix products  20.9 us (4%)
  local copies, waits for them, and re-layouts  20 us (4%)
  between operations  13.8 us (3%)
  other arithmetic  5.48 us (1%)
    pallas_call x8, Pallas kernels, call(): pl.pallas_call(kernel, out_shape=outs, in_specs=in_specs, out_specs=out_s...  408 us
    ppermute x1, starting transfers between devices, per_device(): lax.ppermute(basis_zl, 'wide', to_core)  23.6 us
    pallas_call x1, Pallas kernels, squares(): pl.pallas_call(kernel, grid=(4, 4), out_shape=like((rows, width), F32), i...  12.9 us
  transfers between devices with their start and end apart: 4, of which 0 were waited for; matrix products, arithmetic and copies ran while one was open for 6% of the time, Pallas kernels for 32%

profile of v2, /device:TPU:1, one launch (start us, length us, event | category | flops | bytes accessed | tf_op | source)
XLA Modules:
  0.0 507.1 jit_solution(12181838928612042282)
XLA Ops:
  6.5 1.3 reshape.133
  7.9 0.9 copy.17
  8.8 0.3 sub.40
  9.1 0.2 multiply_reduce_fusion
  9.3 0.1 multiply_convert_fusion
  9.4 0.3 reshape.129
  9.7 0.3 reshape.130
  10.1 1.0 copy_bitcast_fusion.1
  11.1 39.6 %exchange.1 = (bf16[16,32,320]{2,1,0:T(8,128)(2,1)}, bf16[16,32,320]{2,1,0:T(8,128)(2,1)}, bf16[2,160,2048]{2,1,0:T(8,128)(2,1)}, bf16[2,160,640]{2,1,0:T(8,128)(2,1)}) custom-call(bf16[16,32,320]{2,1,0:T(8,128)(2,1)} %get-tuple-element.35.refs_0_, bf16[16,32,320]{2,1,0:T(8,128)(2,1)} %get-tuple-element.34.refs_1_, bf16[160,2048]{1,0:T(8,128)(2,1)} %bitcast.79, ...), custom_call_target="tpu_custom_call" | custom-call | flops 20000000000 | tf_op jit(solution)/shard_map/exchange/pallas_call | solution.py:278
  50.7 5.1 fusion.4
  55.8 1.6 copy.18
  57.4 3.3 fusion.9.refs_0_
  60.7 1.6 fusion.10.refs_1_
  62.3 64.3 %reduce_logits.1 = (f32[32,2048]{1,0:T(8,128)}, bf16[32,640]{1,0:T(8,128)(2,1)}, bf16[256,320]{1,0:T(8,128)(2,1)}) custom-call(f32[4,4,32,2048]{3,2,1,0:T(8,128)} %fusion.9.refs_0_, f32[4,4,32,640]{3,2,1,0:T(8,128)} %fusion.10.refs_1_, bf16[2,4,256,320]{3,2,1,0:T(8,128)(2,1)} %bitcast.69), custom_call_target="tpu_custom_call" | custom-call | flops 44999999488 | tf_op jit(solution)/shard_map/reduce_logits/pallas_call | solution.py:278
  126.6 0.1 collective-permute-start.1
  126.8 2.1 collective-permute-start
  128.9 0.9 convert_element_type.15
  129.9 52.1 %softmax.1 = bf16[32,2048]{1,0:T(8,128)(2,1)} custom-call(f32[32,2048]{1,0:T(8,128)} %get-tuple-element.22.l_ref), custom_call_target="tpu_custom_call" | custom-call | flops 6000000000 | tf_op jit(solution)/shard_map/softmax/pallas_call | solution.py:278
  181.9 1.6 pad_maximum_fusion
  183.5 71.9 %gather_probs.1 = bf16[4,4,2,16,2688]{4,3,2,1,0:T(8,128)(2,1)} custom-call(bf16[2,16,2688]{2,1,0:T(8,128)(2,1)} %bitcast.78), custom_call_target="tpu_custom_call" | custom-call | flops 24000000000 | tf_op jit(solution)/shard_map/gather_probs/pallas_call | solution.py:278
  255.4 1.7 slice.8
  257.1 2.2 dot_general.28
  259.4 3.5 fusion.11
  262.9 0.2 reshape.150
  263.1 1.0 copy.31.refs_0_
  264.2 10.0 %reduce_common.1 = f32[64,320]{1,0:T(8,128)} custom-call(f32[2,4,64,320]{3,2,1,0:T(8,128)} %copy.31.refs_0_), custom_call_target="tpu_custom_call" | custom-call | flops 10000000000 | tf_op jit(solution)/shard_map/reduce_common/pallas_call | solution.py:278
  274.2 1.0 sub.41
  275.3 0.1 sub.43
  275.4 0.8 convert_subtract_fusion.refs_0_
  276.2 12.2 %exchange_grads.1 = f32[16,16,320]{2,1,0:T(8,128)} custom-call(f32[16,16,320]{2,1,0:T(8,128)} %convert_subtract_fusion.refs_0_), custom_call_target="tpu_custom_call" | custom-call | flops 12000000000 | tf_op jit(solution)/shard_map/exchange_grads/pallas_call | solution.py:278
  288.4 1.4 reshape.140
  289.8 0.1 multiply_multiply_fusion
  289.9 1.0 broadcast_multiply_fusion
  291.0 0.2 mul.123
  291.3 0.8 mul.108
  292.1 0.8 mul.118
  292.9 0.3 fusion.7
  293.2 0.5 fusion.8
  293.8 1.0 reshape.141.x_ref
  294.8 23.6 %collective-permute-start.2 = (bf16[432,1728]{1,0:T(8,128)(2,1)}, bf16[432,1728]{1,0:T(8,128)(2,1)}, u32[]{:S(2)}, u32[]{:S(2)}) collective-permute-start(bf16[432,1728]{1,0:T(8,128)(2,1)} %collective-permute-done.1.refs_4_), channel_id=1, source_target_pairs={{0,8},{8,0},{16,24},{24,16},{32,40},{40,32},{48,56},{56,48},{64,72... | collective-permute-start | bytes 4478984 | tf_op jit(solution)/shard_map/ppermute | solution.py:816
  318.3 15.6 %gather_back.1 = bf16[2,4,2,16,2560]{4,3,2,1,0:T(8,128)(2,1)} custom-call(bf16[2,16,2560]{2,1,0:T(8,128)(2,1)} %reshape.141.x_ref), custom_call_target="tpu_custom_call" | custom-call | flops 16000000000 | tf_op jit(solution)/shard_map/gather_back/pallas_call | solution.py:278
  333.9 2.1 slice.9
  336.0 0.3 reshape.142
  336.4 0.5 copy.24
  336.9 0.3 dot_general.30
  337.2 7.4 %fusion.1.refs_0_ = f32[2,128,1728]{2,1,0:T(8,128)} fusion(bf16[2,128,2560]{2,1,0:T(8,128)(2,1)S(1)} %dot_general.30, bf16[2560,1728]{1,0:T(8,128)(2,1)} %all-gather.2.cloned.1.call-done), kind=kOutput, calls=%fused_computation.2 | convolution fusion | flops 2264924160 | bytes 11927552 | tf_op jit(solution)/shard_map/dot_general | solution.py:840
  344.7 142.6 %rotate_all.1 = (bf16[4,2,2,2,4,32,432]{6,5,4,3,2,1,0:T(8,128)(2,1)}, bf16[4,128,640]{2,1,0:T(8,128)(2,1)}) custom-call(f32[2,128,1728]{2,1,0:T(8,128)} %fusion.1.refs_0_, bf16[32,1728]{1,0:T(8,128)(2,1)} %refs_1_.1, bf16[432,1728]{1,0:T(8,128)(2,1)} %bitcast.1.refs_2_, bf16[432,1728]{1,0:T(8,128)(2,1)} %collective-permute-done.refs_3_, ...), custom_call_target="tpu_custom_call" | custom-call | flops 89999998976 | tf_op jit(solution)/shard_map/rotate_all/pallas_call | solution.py:278
  487.3 12.9 %squares.1 = f32[432,640]{1,0:T(8,128)} custom-call(bf16[4,4,256,432]{3,2,1,0:T(8,128)(2,1)} %bitcast.62, bf16[4,128,640]{2,1,0:T(8,128)(2,1)} %bitcast.67, bf16[4,128,640]{2,1,0:T(8,128)(2,1)} %get-tuple-element.28.b_ref), custom_call_target="tpu_custom_call" | custom-call | tf_op jit(solution)/shard_map/squares/pallas_call | solution.py:734
  (37 shorter events, 0.5 us)
Async XLA Ops:
  6.5 2.5 copy-start
  6.5 2.7 copy-start.9
  6.5 330.7 %all-gather.2.cloned.1.call-start = ((), (), s32[]{:S(2)}) async-start(), calls=%async_computation | async-start | bytes 9748480 | tf_op jit(solution)/shard_map/all_gather | solution.py:806
  7.8 1.9 copy-start.7
  55.8 1.6 copy-start.3
  55.8 1.6 copy-start.6
  57.4 3.3 copy-start.4
  57.4 3.3 copy-start.5
  126.6 168.1 %collective-permute-start.1 = (bf16[432,1728]{1,0:T(8,128)(2,1)}, bf16[432,1728]{1,0:T(8,128)(2,1)}, u32[]{:S(2)}, u32[]{:S(2)}) collective-permute-start(bf16[432,1728]{1,0:T(8,128)(2,1)} %bitcast.1.refs_2_), channel_id=1, source_target_pairs={{0,4},{1,5},{2,6},{3,7},{4,0},{5,1},{6,2},{7,3},{8,12},{9,13},{10,... | collective-permute-start | bytes 4478984 | tf_op jit(solution)/shard_map/ppermute | solution.py:811
  126.8 217.9 %collective-permute-start = (bf16[432,1728]{1,0:T(8,128)(2,1)}, bf16[432,1728]{1,0:T(8,128)(2,1)}, u32[]{:S(2)}, u32[]{:S(2)}) collective-permute-start(bf16[432,1728]{1,0:T(8,128)(2,1)} %bitcast.1.refs_2_), channel_id=1, source_target_pairs={{0,8},{8,0},{16,24},{24,16},{32,40},{40,32},{48,56},{56,48},{64,72... | collective-permute-start | bytes 4478984 | tf_op jit(solution)/shard_map/ppermute | solution.py:814
  129.9 52.1 %copy-start.10 = (bf16[32,640]{1,0:T(8,128)(2,1)S(1)}, bf16[32,640]{1,0:T(8,128)(2,1)}, u32[]{:S(2)}) copy-start(bf16[32,640]{1,0:T(8,128)(2,1)} %get-tuple-element.23) | copy-start | bytes 122884
  274.2 1.2 copy-start.8
  291.0 2.0 copy-start.1
  294.8 49.9 %collective-permute-start.2 = (bf16[432,1728]{1,0:T(8,128)(2,1)}, bf16[432,1728]{1,0:T(8,128)(2,1)}, u32[]{:S(2)}, u32[]{:S(2)}) collective-permute-start(bf16[432,1728]{1,0:T(8,128)(2,1)} %collective-permute-done.1.refs_4_), channel_id=1, source_target_pairs={{0,8},{8,0},{16,24},{24,16},{32,40},{40,32},{48,56},{56,48},{64,72... | collective-permute-start | bytes 4478984 | tf_op jit(solution)/shard_map/ppermute | solution.py:816
  333.9 2.1 copy-start.2
Sparse Core Ops, SparseCore 0:
  126.8 138.5 all-gather.1

commit v3 on v2

--- a/solution.py
+++ b/solution.py
@@ -108,6 +108,7 @@
         net.send(base + 1, own(1), slot(me_o, me_i, 1), on_o(1))
         net.send(base + 3, own(0), slot(me_o, me_i, 0), on_o(3))
         along(0, me_o, True)
+        yield
         net.recv(base, slot(om, me_i, 0))
         net.send(base + 4, slot(om, me_i, 0), slot(om, me_i, 0), on_o(1))
         net.recv(base + 2, slot(op, me_i, 1))
@@ -115,13 +116,16 @@
         forward(0, me_o)
         net.recv(base + 1, slot(om, me_i, 1))
         along(1, om, False)
+        yield
         net.recv(base + 3, slot(op, me_i, 0))
         along(2, op, False)
         forward(1, om)
+        yield
         net.recv(base + 4, slot(o2, me_i, 0))
         net.recv(base + 5, slot(o2, me_i, 1))
         along(3, o2, False)
         forward(2, op)
+        yield
         forward(3, o2)
         for row, o in enumerate((me_o, om, op, o2)):
             rest(row, o)
@@ -270,6 +274,81 @@
         stages = [stage for stage in stages if next(stage, 0) is None]
 
 
+def ring(net, base, own, slot, me, on):
+    plus, minus, far = (turn(me, s, 4) for s in (1, 3, 2))
+    net.send(base, own(0), slot(me, 0), on(1))
+    net.send(base + 2, own(1), slot(me, 1), on(3))
+    yield
+    net.send(base + 1, own(1), slot(me, 1), on(1))
+    net.send(base + 3, own(0), slot(me, 0), on(3))
+    yield
+    net.recv(base, slot(minus, 0))
+    net.send(base + 4, slot(minus, 0), slot(minus, 0), on(1))
+    net.recv(base + 2, slot(plus, 1))
+    net.send(base + 5, slot(plus, 1), slot(plus, 1), on(3))
+    yield
+    net.recv(base + 1, slot(minus, 1))
+    net.recv(base + 3, slot(plus, 0))
+    net.recv(base + 4, slot(far, 0))
+    net.recv(base + 5, slot(far, 1))
+
+
+class Side:
+    def __init__(self, tasks):
+        self.tasks = tasks
+        self.arrays = [array for _, array, _ in tasks]
+        self.outs = []
+        for kind, array, _ in tasks:
+            rows, depth = array.shape[-2:]
+            shape = (2, rows // 3, depth) if kind == "basis" else (4, rows, depth)
+            self.outs.append(like(shape, array.dtype))
+        self.slots = 6 * len(tasks)
+
+    def local(self):
+        return [pltpu.SemaphoreType.DMA((max(len(self.tasks), 1),))]
+
+    def peers(self, net):
+        found = []
+        for kind, _, _ in self.tasks:
+            if kind == "x":
+                found += [net.on_x(1), net.on_x(3)]
+            elif kind == "z":
+                found += [net.on_z(1), net.on_z(3)]
+            else:
+                found += [net.on_zl(1), net.on_core()]
+        return found
+
+    def stages(self, net, base, ins, outs, local):
+        return [
+            self.stage(net, base + 6 * t, kind, ins[t], outs[t], step, local.at[t])
+            for t, (kind, _, step) in enumerate(self.tasks)
+        ]
+
+    def stage(self, net, base, kind, src, out, step, local):
+        if kind == "basis":
+            rows = out.shape[1]
+            net.send(base, src.at[pl.ds(rows * step, rows)], out.at[0], net.on_zl(1))
+            yield
+            yield
+            net.recv(base, out.at[0])
+            net.send(base + 1, out.at[0], out.at[1], net.on_core())
+            yield
+            net.recv(base + 1, out.at[1])
+            return
+        half = out.shape[1] // 2
+        cut = lambda h: pl.ds(h * half, half)
+        row = src if len(src.shape) == 2 else src.at[turn(net.z, step, 4)]
+        own = lambda h: row.at[cut(h)]
+        slot = lambda i, h: out.at[i, cut(h)]
+        if kind == "z":
+            yield from ring(net, base, own, slot, net.z, net.on_z)
+        else:
+            copy = pltpu.make_async_copy(row, out.at[net.x], local)
+            copy.start()
+            yield from ring(net, base, own, slot, net.x, net.on_x)
+            copy.wait()
+
+
 def sems(slots):
     return [pltpu.SemaphoreType.DMA((slots,)), pltpu.SemaphoreType.DMA((slots,))]
 
@@ -293,13 +372,15 @@
     return jax.ShapeDtypeStruct(shape, dtype)
 
 
-def exchange(arrays, pairs, collective_id, name, cost):
-    na, np_ = len(arrays), len(pairs)
+def exchange(arrays, pairs, tasks, collective_id, name, cost):
+    na, np_, nt = len(arrays), len(pairs), len(tasks)
+    side = Side(tasks)
 
     def kernel(*refs):
-        ins, shared = refs[:na], refs[na : na + np_]
-        outs, both = refs[na + np_ : 2 * na + np_], refs[2 * na + np_ : 2 * (na + np_)]
-        local, send_sem, recv_sem = refs[2 * (na + np_) :]
+        ins, shared, side_in = refs[:na], refs[na : na + np_], refs[na + np_ : na + np_ + nt]
+        refs = refs[na + np_ + nt :]
+        outs, both, side_out = refs[:na], refs[na : na + np_], refs[na + np_ : na + np_ + nt]
+        local, side_local, send_sem, recv_sem = refs[na + np_ + nt :]
         net = Net(send_sem, recv_sem)
         steps = [(dz, dx) for dz in range(4) for dx in range(4) if (dz, dx) != (0, 0)]
         steps.sort(key=lambda s: -(min(s[0], 4 - s[0]) * 2 + min(s[1], 4 - s[1])))
@@ -309,7 +390,7 @@
 
         me = net.z * 4 + net.x
         peers = [{"wide": to(*s) * 2 + net.core} for s in steps]
-        net.greet(peers + ([net.on_core()] if np_ else []))
+        net.greet(peers + ([net.on_core()] if np_ else []) + side.peers(net))
         copies = []
         for j, s in enumerate(steps):
             for a in range(na):
@@ -323,12 +404,17 @@
             )
         for copy in copies:
             copy.start()
+        extra = side.stages(net, 15 * na + max(np_, 1), side_in, side_out, side_local)
+        for _ in range(3):
+            for stage in extra:
+                next(stage)
         for j, (dz, dx) in enumerate(steps):
             source = to((4 - dz) % 4, (4 - dx) % 4)
             for a in range(na):
                 net.recv(j * na + a, outs[a].at[source])
         for b in range(np_):
             net.recv(15 * na + b, both[b].at[1 - net.core])
+        drive(*extra)
         for copy in copies:
             copy.wait()
         net.finish()
@@ -337,32 +423,48 @@
     return call(
         kernel,
         collective_id,
-        outs,
-        [ANY] * (na + np_),
-        [ANY] * (na + np_),
-        [pltpu.SemaphoreType.DMA((na + np_,)), *sems(15 * na + max(np_, 1))],
-        (*arrays, *pairs),
+        outs + side.outs,
+        [ANY] * (na + np_ + nt),
+        [ANY] * (na + np_ + nt),
+        [
+            pltpu.SemaphoreType.DMA((na + np_,)),
+            *side.local(),
+            *sems(15 * na + max(np_, 1) + side.slots),
+        ],
+        (*arrays, *pairs, *side.arrays),
         name,
         cost,
     )
 
 
-def gather_wide(shard, collective_id, name, cost):
-    half = shard.shape[0] // 2
-    shape = (4, 4, *shard.shape)
-
-    def kernel(x_ref, o_ref, local, send_sem, recv_sem):
+def gather_wide(shards, tasks, collective_id, name, cost):
+    n, nt = len(shards), len(tasks)
+    side = Side(tasks)
+
+    def kernel(*refs):
+        ins, side_in = refs[:n], refs[n : n + nt]
+        outs, side_out = refs[n + nt : 2 * n + nt], refs[2 * n + nt : 2 * (n + nt)]
+        local, side_local, send_sem, recv_sem = refs[2 * (n + nt) :]
         net = Net(send_sem, recv_sem)
-
-        slot = lambda o, i, h: o_ref.at[o, i, pl.ds(h * half, half)]
-        net.greet([net.on_x(1), net.on_x(3), net.on_z(1), net.on_z(3)])
-        own = lambda h: x_ref.at[pl.ds(h * half, half)]
-        copies = [
-            pltpu.make_async_copy(own(h), slot(net.z, net.x, h), local.at[h]) for h in range(2)
-        ]
-        for copy in copies:
-            copy.start()
-        drive(gather_stage(net, 0, own, slot, 4, net.z, net.x, net.on_z, net.on_x))
+        ones = [net.on_x(1), net.on_x(3), net.on_z(1), net.on_z(3)]
+        net.greet(ones + side.peers(net))
+        copies, stages = [], []
+
+        def stage(a):
+            half = ins[a].shape[0] // 2
+            slot = lambda o, i, h: outs[a].at[o, i, pl.ds(h * half, half)]
+            own = lambda h: ins[a].at[pl.ds(h * half, half)]
+            for h in range(2):
+                copy = pltpu.make_async_copy(
+                    own(h), slot(net.z, net.x, h), local.at[2 * a + h]
+                )
+                copy.start()
+                copies.append(copy)
+            base = gather_slots(4) * a
+            return gather_stage(net, base, own, slot, 4, net.z, net.x, net.on_z, net.on_x)
+
+        stages = [stage(a) for a in range(n)]
+        drive(*stages, *side.stages(net, gather_slots(4) * n, side_in, side_out, side_local))
         for copy in copies:
             copy.wait()
         net.finish()
@@ -370,23 +472,30 @@
     return call(
         kernel,
         collective_id,
-        like(shape, shard.dtype),
-        [ANY],
-        ANY,
-        [pltpu.SemaphoreType.DMA((2,)), *sems(gather_slots(4))],
-        (shard,),
+        [like((4, 4, *shard.shape), shard.dtype) for shard in shards] + side.outs,
+        [ANY] * (n + nt),
+        [ANY] * (n + nt),
+        [
+            pltpu.SemaphoreType.DMA((2 * n,)),
+            *side.local(),
+            *sems(gather_slots(4) * n + side.slots),
+        ],
+        (*shards, *side.arrays),
         name,
         cost,
     )
 
 
-def reduce_over(wide_parts, narrow_parts, dtypes, collective_id, name, cost):
+def reduce_over(wide_parts, narrow_parts, tasks, dtypes, collective_id, name, cost):
     parts = [*wide_parts, *narrow_parts]
-    n, split = len(parts), len(wide_parts)
+    n, split, nt = len(parts), len(wide_parts), len(tasks)
+    side = Side(tasks)
+    slots = split * reduce_slots(4) + (n - split) * reduce_slots(2)
 
     def kernel(*refs):
-        ins, outs = refs[:n], refs[n : 2 * n]
-        buffers, (send_sem, recv_sem) = refs[2 * n : -2], refs[-2:]
+        ins, side_in = refs[:n], refs[n : n + nt]
+        outs, side_out = refs[n + nt : 2 * n + nt], refs[2 * n + nt : 2 * (n + nt)]
+        buffers, (side_local, send_sem, recv_sem) = refs[2 * (n + nt) : -3], refs[-3:]
         net = Net(send_sem, recv_sem)
         sums = [Sum(ins[a], *buffers[6 * a : 6 * a + 6]) for a in range(n)]
         stages, ends, peers = [], [], []
@@ -403,8 +512,9 @@
             )
             stages.append(stage)
             ends += end
-        net.greet(peers)
-        drive(*stages)
+        net.greet(peers + side.peers(net))
+        extra = side.stages(net, slots, side_in, side_out, side_local)
+        drive(*stages, *extra)
         for a in range(n):
             for h in range(2):
                 outs[a][sums[a].h(h), :] = ends[a](h).astype(outs[a].dtype)
@@ -413,24 +523,26 @@
     scratch = []
     for p in parts:
         scratch += Sum.scratch(p.shape[0], p.shape[2], p.shape[3], p.dtype)
-    slots = split * reduce_slots(4) + (n - split) * reduce_slots(2)
     return call(
         kernel,
         collective_id,
-        [like(p.shape[2:], d) for p, d in zip(parts, dtypes)],
-        [VMEM] * n,
-        [VMEM] * n,
-        [*scratch, *sems(slots)],
-        tuple(parts),
+        [like(p.shape[2:], d) for p, d in zip(parts, dtypes)] + side.outs,
+        [VMEM] * n + [ANY] * nt,
+        [VMEM] * n + [ANY] * nt,
+        [*scratch, *side.local(), *sems(slots + side.slots)],
+        (*parts, *side.arrays),
         name,
         cost,
     )
 
 
-def softmax_narrow(logits, collective_id, name, cost):
+def softmax_narrow(logits, tasks, collective_id, name, cost):
     rows, columns = logits.shape
-
-    def kernel(l_ref, p_ref, mine, got, send_sem, recv_sem):
+    side, nt = Side(tasks), len(tasks)
+
+    def kernel(*refs):
+        l_ref, side_in, p_ref, side_out = refs[0], refs[1 : 1 + nt], refs[1 + nt], refs[2 + nt : -5]
+        mine, got, side_local, send_sem, recv_sem = refs[-5:]
         net = Net(send_sem, recv_sem)
         peers = [{"narrow": turn(net.narrow, k, 8)} for k in range(1, 8)]
         top = jnp.max(l_ref[...], axis=1, keepdims=True)
@@ -438,9 +550,13 @@
         mine[1] = jnp.broadcast_to(
             jnp.sum(jnp.exp(l_ref[...] - top), axis=1, keepdims=True), (rows, 128)
         )
-        net.greet(peers)
+        net.greet(peers + side.peers(net))
         for k in range(7):
             net.send(k, mine, got.at[k], peers[k])
+        extra = side.stages(net, 7, side_in, side_out, side_local)
+        for _ in range(2):
+            for stage in extra:
+                next(stage)
         for k in range(7):
             net.recv(k, got.at[k])
         largest = mine[0]
@@ -450,27 +566,36 @@
         for k in range(7):
             total += got[k, 1] * jnp.exp(got[k, 0] - largest)
         p_ref[...] = (jnp.exp(l_ref[...] - largest[:, :1]) / total[:, :1]).astype(BF16)
+        drive(*extra)
         net.finish()
 
     return call(
         kernel,
         collective_id,
-        like((rows, columns), BF16),
-        [VMEM],
-        VMEM,
-        [pltpu.VMEM((2, rows, 128), F32), pltpu.VMEM((7, 2, rows, 128), F32), *sems(7)],
-        (logits,),
+        [like((rows, columns), BF16)] + side.outs,
+        [VMEM] + [ANY] * nt,
+        [VMEM] + [ANY] * nt,
+        [
+            pltpu.VMEM((2, rows, 128), F32),
+            pltpu.VMEM((7, 2, rows, 128), F32),
+            *side.local(),
+            *sems(7 + side.slots),
+        ],
+        (logits, *side.arrays),
         name,
         cost,
     )
 
 
-def gather_back(shard, collective_id, name, cost):
+def gather_back(shard, tasks, collective_id, name, cost):
     _, rows, features = shard.shape
-
-    def kernel(x_ref, o_ref, mine, local, send_sem, recv_sem):
+    side, nt = Side(tasks), len(tasks)
+
+    def kernel(*refs):
+        x_ref, side_in, o_ref, side_out = refs[0], refs[1 : 1 + nt], refs[1 + nt], refs[2 + nt : -5]
+        mine, local, side_local, send_sem, recv_sem = refs[-5:]
         net = Net(send_sem, recv_sem)
-        net.greet([net.on_y(1), net.on_y(3), net.on_zl(1), net.on_core()])
+        net.greet([net.on_y(1), net.on_y(3), net.on_zl(1), net.on_core()] + side.peers(net))
         net.send(0, x_ref.at[1 - net.core], mine, net.on_core())
         slot = lambda o, i, h: o_ref.at[o, i, lax.rem(net.core + h, 2)]
         own = lambda h: mine if h else x_ref.at[net.core]
@@ -480,7 +605,10 @@
         ]
         for copy in copies:
             copy.start()
-        drive(gather_stage(net, 1, own, slot, 2, net.zl, net.y, net.on_zl, net.on_y))
+        drive(
+            gather_stage(net, 1, own, slot, 2, net.zl, net.y, net.on_zl, net.on_y),
+            *side.stages(net, 1 + gather_slots(2), side_in, side_out, side_local),
+        )
         for copy in copies:
             copy.wait()
         net.finish()
@@ -488,50 +616,83 @@
     return call(
         kernel,
         collective_id,
-        like((2, 4, 2, rows, features), shard.dtype),
-        [ANY],
-        ANY,
+        [like((2, 4, 2, rows, features), shard.dtype)] + side.outs,
+        [ANY] * (1 + nt),
+        [ANY] * (1 + nt),
         [
             pltpu.VMEM((rows, features), shard.dtype),
             pltpu.SemaphoreType.DMA((2,)),
-            *sems(1 + gather_slots(2)),
+            *side.local(),
+            *sems(1 + gather_slots(2) + side.slots),
         ],
-        (shard,),
+        (shard, *side.arrays),
         name,
         cost,
     )
 
 
-def rotate_all(hidden, gate, bases, inputs, collective_id, name, cost):
+def rotate_all(back, gate, downs, basis, thirds, inputs, collective_id, name, cost):
     tokens, depth = gate.shape
-    columns = bases[0].shape[0]
+    columns = basis.shape[1]
     rows = 2 * tokens
+    features = back.shape[2]
+    cuts = (pl.ds(0, 896), pl.ds(896, depth - 896))
 
     def kernel(*refs):
-        h_ref, g_ref = refs[:2]
-        b_refs, i_ref, o_ref, j_ref = refs[2:6], refs[6], refs[7], refs[8]
-        half_in, gated, other, every, part, fwd, mid, got, mine = refs[9:18]
-        local, send_sem, recv_sem = refs[18:]
+        back_ref, g_ref, d_refs, basis_ref = refs[0], refs[1], refs[2:6], refs[6]
+        t_refs, i_ref, o_ref, j_ref = refs[7:10], refs[10], refs[11], refs[12]
+        down, bases, h_ref = refs[13:16]
+        half_in, gated, other, every, part, fwd, mid, got, mine = refs[16:25]
+        local, send_sem, recv_sem = refs[25:]
         net = Net(send_sem, recv_sem)
+        c, z, x, zl, y = net.core, net.z, net.x, net.zl, net.y
+        base_z, base_r, base_n = 8, 40, 64
+        loads = [
+            pltpu.make_async_copy(d_refs[k], down.at[k], local.at[10 + k]) for k in range(4)
+        ]
+        loads += [
+            pltpu.make_async_copy(basis_ref.at[c], bases.at[0], local.at[14]),
+            pltpu.make_async_copy(basis_ref.at[1 - c], bases.at[1], local.at[15]),
+        ]
+        third = columns // 3
+        for j in range(3):
+            for m in range(2):
+                loads.append(
+                    pltpu.make_async_copy(
+                        t_refs[j].at[m],
+                        bases.at[2 + m, pl.ds(j * third, third)],
+                        local.at[16 + 2 * j + m],
+                    )
+                )
+        for load in loads:
+            load.start()
         ones = [net.on_x(1), net.on_x(3), net.on_z(1), net.on_z(3)]
         net.greet(ones + [net.on_y(1), net.on_y(3), net.on_zl(1), net.on_core()])
-        c, z, x, zl, y = net.core, net.z, net.x, net.zl, net.y
-        base_z, base_r, base_n = 8, 40, 64
-
-        net.send(0, h_ref.at[1 - c], half_in, net.on_core())
+        for load in loads[:4]:
+            load.wait()
+        quarter = features // 4
+        left = back_ref[...].reshape(2 * 4 * tokens, features)
+        for j, cut in enumerate(cuts):
+            total = None
+            for k in range(4):
+                right = down[k, :, :, cut].reshape(quarter, cut.size)
+                term = jnp.dot(
+                    left[:, k * quarter : (k + 1) * quarter], right, preferred_element_type=F32
+                )
+                total = term if total is None else total + term
+            h_ref[:, :, cut] = total.reshape(2, 4 * tokens, cut.size)
+            net.send((0, 7)[j], h_ref.at[1 - c, :, cut], half_in.at[:, cut], net.on_core())
         net.send(1, i_ref, j_ref, net.on_core())
-        net.recv(0, half_in)
-
-        def gate_rows(s):
-            cut = pl.ds(pl.multiple_of(s * tokens, tokens), tokens)
-            value = (h_ref[c, cut] + half_in[cut]) * g_ref[...].astype(F32)
-            gated[s] = value.astype(BF16)
-
-        for s in range(2):
-            gate_rows(2 * (1 - zl) + s)
-        net.send(2, gated.at[pl.ds(2 * (1 - zl), 2)], other, net.on_zl(1))
-        for s in range(2):
-            gate_rows(2 * zl + s)
+
+        def gate_rows(s, cut):
+            some = pl.ds(pl.multiple_of(s * tokens, tokens), tokens)
+            value = (h_ref[c, some, cut] + half_in[some, cut]) * g_ref[:, cut].astype(F32)
+            gated[s, :, cut] = value.astype(BF16)
+
+        for j, cut in enumerate(cuts):
+            net.recv((0, 7)[j], half_in.at[:, cut])
+            for s in range(2):
+                gate_rows(2 * zl + s, cut)
 
         own = lambda h: other if h else gated.at[pl.ds(2 * zl, 2)]
         slot = lambda o, i, h: every.at[o, h, i]
@@ -567,7 +728,7 @@
                 block = None
                 for h in range(2):
                     left = every[o, h].reshape(4 * rows, depth)
-                    term = contract_last(left, b_refs[2 * h + m][...])
+                    term = contract_last(left, bases[2 * h + m])
                     block = term if block is None else block + term
                 part[row, :, m] = block.reshape(4, rows, columns)
 
@@ -615,6 +776,10 @@
         net.send(base_z, own(0), slot(z, x, 0), net.on_z(1))
         net.send(base_z + 3, own(0), slot(z, x, 0), net.on_z(3))
         along(0, 0)
+        for cut in cuts:
+            for s in range(2):
+                gate_rows(2 * (1 - zl) + s, cut)
+        net.send(2, gated.at[pl.ds(2 * (1 - zl), 2)], other, net.on_zl(1))
         net.recv(2, other)
         net.send(base_z + 2, own(1), slot(z, x, 1), net.on_z(3))
         net.send(base_z + 1, own(1), slot(z, x, 1), net.on_z(1))
@@ -631,55 +796,53 @@
         for h in range(2):
             along(1, h)
         rest(0)
-        for copy in copies:
+        for copy in copies + loads[4:]:
             copy.wait()
         multiply(0)
         reduce_start(0)
+        forward(1)
         net.recv(base_z + 3, slot(zp, x, 0))
         for h in range(2):
             along(2, h)
-        forward(1)
         reduce_middle(0)
         rest(1)
+        reduce_end(0)
         multiply(1)
         reduce_start(1)
+        spread_0 = spread(0)
+        next(spread_0)
+        forward(2)
         net.recv(base_z + 4, slot(z2, x, 0))
         net.recv(base_z + 5, slot(z2, x, 1))
         for h in range(2):
             along(3, h)
-        forward(2)
-        reduce_end(0)
         reduce_middle(1)
-        spread_0 = spread(0)
         next(spread_0)
         rest(2)
+        reduce_end(1)
         multiply(2)
         reduce_start(2)
-        forward(3)
-        next(spread_0)
-        reduce_end(1)
-        reduce_middle(2)
         spread_1 = spread(1)
         next(spread_1)
         next(spread_0)
+        forward(3)
+        reduce_middle(2)
+        next(spread_1)
         rest(3)
         multiply(3)
         reduce_start(3)
-        next(spread_1)
         reduce_end(2)
-        reduce_middle(3)
         spread_2 = spread(2)
         next(spread_2)
         next(spread_1)
+        reduce_middle(3)
+        next(spread_2)
         reduce_end(3)
         spread_3 = spread(3)
         next(spread_3)
-        drive(spread_0)
-        for stage in (spread_2, spread_3, spread_2, spread_3):
-            next(stage)
-        drive(spread_1)
-        drive(spread_2)
-        drive(spread_3)
+        next(spread_2)
+        next(spread_3)
+        drive(spread_0, spread_1, spread_2, spread_3)
         for copy in last:
             copy.wait()
         net.recv(1, j_ref)
@@ -689,9 +852,12 @@
         kernel,
         collective_id,
         [like((4, 2, 2, 2, 4, tokens, columns), BF16), like(inputs.shape, BF16)],
-        [VMEM] * 6 + [ANY],
+        [VMEM] * 2 + [ANY] * 9,
         [ANY, ANY],
         [
+            pltpu.VMEM((4, 4, features // 16, depth), BF16),
+            pltpu.VMEM((4, columns, depth), BF16),
+            pltpu.VMEM((2, 4 * tokens, depth), F32),
             pltpu.VMEM((4 * tokens, depth), F32),
             pltpu.VMEM((4, tokens, depth), BF16),
             pltpu.VMEM((2, tokens, depth), BF16),
@@ -701,35 +867,37 @@
             pltpu.VMEM((4, 2, rows, columns), F32),
             pltpu.VMEM((4, 2, 2, rows, columns), F32),
             pltpu.VMEM((4, 3, 2, tokens, columns), BF16),
-            pltpu.SemaphoreType.DMA((10,)),
+            pltpu.SemaphoreType.DMA((22,)),
             *sems(64 + 4 * gather_slots(2)),
         ],
-        (hidden, gate, *bases, inputs),
+        (back, gate, *downs, basis, *thirds, inputs),
         name,
         cost,
     )
 
 
 def squares(rotated, own_inputs, other_inputs):
-    rows, width = rotated.shape[3], own_inputs.shape[2]
-    depth = own_inputs.shape[1]
-
-    def kernel(r_ref, a_ref, b_ref, o_ref, both):
+    rows, width = rotated.shape[3], own_inputs.shape[1]
+    depth = own_inputs.shape[2]
+
+    def kernel(r_ref, a_ref, b_ref, o_ref, both, total):
         example, sample = pl.program_id(0), pl.program_id(1)
 
         @pl.when((example == 0) & (sample == 0))
         def _():
-            o_ref[...] = jnp.zeros_like(o_ref)
+            total[...] = jnp.zeros_like(total)
 
         @pl.when(sample == 0)
         def _():
-            both[:depth] = a_ref[0]
-            both[depth:] = b_ref[0]
-
-        block = lax.dot_general(
-            r_ref[0, 0], both[...], (((0,), (0,)), ((), ())), preferred_element_type=F32
-        )
-        o_ref[...] += block * block * (1.0 / 16.0)
+            both[:, :depth] = a_ref[0]
+            both[:, depth:] = b_ref[0]
+
+        block = jnp.dot(both[...], r_ref[0, 0], preferred_element_type=F32)
+        total[...] += block * block * (1.0 / 16.0)
+
+        @pl.when((example == 3) & (sample == 3))
+        def _():
+            o_ref[...] = total[...].T
 
     return pl.pallas_call(
         kernel,
@@ -737,11 +905,11 @@
         out_shape=like((rows, width), F32),
         in_specs=[
             pl.BlockSpec((1, 1, 2 * depth, rows), lambda e, s: (e, s, 0, 0)),
-            pl.BlockSpec((1, depth, width), lambda e, s: (e, 0, 0)),
-            pl.BlockSpec((1, depth, width), lambda e, s: (e, 0, 0)),
+            pl.BlockSpec((1, width, depth), lambda e, s: (e, 0, 0)),
+            pl.BlockSpec((1, width, depth), lambda e, s: (e, 0, 0)),
         ],
         out_specs=pl.BlockSpec((rows, width), lambda e, s: (0, 0)),
-        scratch_shapes=[pltpu.VMEM((2 * depth, width), BF16)],
+        scratch_shapes=[pltpu.VMEM((width, 2 * depth), BF16), pltpu.VMEM((width, rows), F32)],
         name="squares",
     )(rotated, own_inputs, other_inputs)
 
@@ -772,8 +940,14 @@
     def blocks(rows):
         return rows.reshape(tokens, 16, pair).transpose(1, 0, 2)
 
-    normed_cols, inputs_cols, unembed_rows, basis_in_rows = exchange(
-        [blocks(normed), blocks(layer_in)], [unembed.T, basis_in], 0, "exchange", 20
+    down, basis = down_weight.T, basis_out.T
+    normed_cols, inputs_cols, unembed_rows, basis_in_rows, basis_both, down_0 = exchange(
+        [blocks(normed), blocks(layer_in)],
+        [unembed.T, basis_in, basis],
+        [("x", down, 0)],
+        0,
+        "exchange",
+        30,
     )
     unembed_rows = unembed_rows.reshape(pair, vocab)
     basis_in_rows = basis_in_rows.reshape(pair, width_in)
@@ -789,43 +963,31 @@
     shifted = mine.transpose(1, 0, 2, 3).reshape(core_tokens * samples) - narrow * vocab
     chosen = (shifted[:, None] == lax.broadcasted_iota(jnp.int32, (1, vocab), 1)).astype(BF16)
     picked = contract_last(chosen, unembed_rows).astype(BF16)
-    logits, inputs_rot, picked = reduce_over(
+    logits, inputs_rot, picked, down_z = reduce_over(
         [logits_part.reshape(4, 4, tokens, vocab), inputs_part.reshape(4, 4, tokens, width_in)],
         [picked.reshape(2, 4, 16 * few * samples, pair)],
+        [("z", down, 0)],
         [F32, BF16, BF16],
         1,
         "reduce_logits",
-        45,
-    )
-
-    down_cols, basis_rows, logits = lax.optimization_barrier(
-        (down_weight.T, basis_out.T, logits)
-    )
-    wide_count = lax.axis_size("wide")
-    same_core = [list(range(c, wide_count, 2)) for c in range(2)]
-    down_rows = lax.all_gather(
-        down_cols, "wide", axis=0, tiled=True, axis_index_groups=same_core
-    )
-    to_core = [(w, w + 1 - 2 * (w % 2)) for w in range(wide_count)]
-    to_zl = [(n, (n + 4) % 8) for n in range(8)]
-    basis_zl = lax.ppermute(basis_rows, "narrow", to_zl)
-    bases = [
-        basis_rows,
-        lax.ppermute(basis_rows, "wide", to_core),
-        basis_zl,
-        lax.ppermute(basis_zl, "wide", to_core),
-    ]
-
-    probs = softmax_narrow(logits, 2, "softmax", 6)
-    both = jnp.concatenate([probs, inputs_rot], axis=1)
-    both = gather_wide(both.reshape(2, tokens // 2, vocab + width_in), 3, "gather_probs", 24)
-    both = both.reshape(core_tokens, vocab + width_in)
-    inputs_all = both[:, vocab:].reshape(4, 4 * tokens, width_in)
-    common = contract_last(both[:, :vocab], unembed_rows)
+        60,
+    )
+    probs, down_1 = softmax_narrow(logits, [("x", down_z, 1)], 2, "softmax", 20)
+    probs_all, inputs_all, third_0, third_1 = gather_wide(
+        [probs.reshape(2, tokens // 2, vocab), inputs_rot.reshape(2, tokens // 2, width_in)],
+        [("basis", basis, 0), ("basis", basis, 1)],
+        3,
+        "gather_probs",
+        30,
+    )
+    inputs_all = inputs_all.reshape(4, 4 * tokens, width_in).transpose(0, 2, 1)
+    common = contract_last(probs_all.reshape(core_tokens, vocab), unembed_rows)
     common = common.reshape(16, 8, few, pair).transpose(1, 0, 2, 3).reshape(2, 4, 16 * few, pair)
-    (common,) = reduce_over([], [common], [F32], 4, "reduce_common", 10)
+    common, down_2, third_2 = reduce_over(
+        [], [common], [("x", down_z, 2), ("basis", basis, 2)], [F32], 4, "reduce_common", 20
+    )
     grads = common.reshape(16, few, 1, pair) - picked.astype(F32).reshape(16, few, samples, pair)
-    (grads,) = exchange([grads.reshape(16, few * samples, pair)], [], 5, "exchange_grads", 12)
+    (grads,) = exchange([grads.reshape(16, few * samples, pair)], [], [], 5, "exchange_grads", 12)
     grads = grads.transpose(1, 0, 2).reshape(few, samples, width)
     resid_few = lax.dynamic_slice_in_dim(resid_float, narrow * few, few, 0)
     inverse_few = lax.dynamic_slice_in_dim(inverse, narrow * few, few, 0)
@@ -834,20 +996,24 @@
         inverse_few[:, None, None] * final_gain * grads
         - resid_few[:, None, :] * (inverse_few**3)[:, None, None] * inner[:, :, None] / width
     )
-    back = back.astype(BF16).reshape(few * samples, 16, 2, part).transpose(2, 0, 1, 3)
-    back = gather_back(back.reshape(2, few * samples, width // 2), 6, "gather_back", 16)
+    back = back.astype(BF16).reshape(few * samples, 4, 4, 2, part).transpose(3, 0, 1, 2, 4)
+    back = lax.dynamic_slice_in_dim(
+        jnp.concatenate([back, back], axis=2), lax.div(wide, 8), 4, axis=2
+    )
+    back, down_3 = gather_back(
+        back.reshape(2, few * samples, width // 2), [("x", down_z, 3)], 6, "gather_back", 20
+    )
     back = back.reshape(8, 2, few, samples, width // 2).transpose(1, 3, 0, 2, 4)
-    hidden_part = jnp.dot(
-        back.reshape(2 * tokens * samples, width // 2), down_rows, preferred_element_type=F32
-    )
     rotated, inputs_other = rotate_all(
-        hidden_part.reshape(2, samples * tokens, hidden),
+        back.reshape(2, samples * tokens, width // 2),
         gate_value,
-        bases,
+        [down_0, down_1, down_2, down_3],
+        basis_both,
+        [third_0, third_1, third_2],
         inputs_all,
         7,
         "rotate_all",
-        90,
+        110,
     )
     return squares(
         rotated.reshape(4, samples, 8 * tokens, columns), inputs_all, inputs_other

time: 508 us -> 505 us (level)
  Pallas kernels: 421 us -> 462 us
  starting transfers between devices: 25.8 us -> 0 us
  between operations: 13.8 us -> 0.36 us
  matrix products: 20.9 us -> 11.7 us
    pallas_call x8, Pallas kernels: 408 us -> 449 us  [call(): pl.pallas_call(kernel, out_shape=outs, in_specs=in_specs, out_specs=out_s...]
    ppermute x3 -> x0, starting transfers between devices: 25.8 us -> none  [the longest x1 23.6 us: per_device(): lax.ppermute(basis_zl, 'wide', to_core)]
    dot_general x1 -> x0, matrix products: 7.41 us -> none  [per_device(): jnp.dot(back.reshape(2 * tokens * samples, width // 2), down_rows, prefer...]
  transfers between devices with their start and end apart: 4 -> 0, of which waited for: 0 -> 0; matrix products, arithmetic and copies ran while one was open for 6% -> 0% of each run, Pallas kernels for 32% -> 0%
where the time goes in v3:
time: 505 us; the launch traced here: 504 us
  Pallas kernels  462 us (91%)
  local copies, waits for them, and re-layouts  24.2 us (5%)
  matrix products  11.7 us (2%)
  other arithmetic  5.92 us (1%)
    pallas_call x8, Pallas kernels, call(): pl.pallas_call(kernel, out_shape=outs, in_specs=in_specs, out_specs=out_s...  449 us
    pallas_call x1, Pallas kernels, squares(): pl.pallas_call(kernel, grid=(4, 4), out_shape=like((rows, width), F32), i...  13.1 us

profile of v3, /device:TPU:1, one launch (start us, length us, event | category | flops | bytes accessed | tf_op | source)
XLA Modules:
  0.0 504.4 jit_solution(15999244763917169701)
XLA Ops:
  0.0 1.2 multiply_reduce_fusion
  1.2 0.1 multiply_multiply_fusion
  1.3 1.4 mul.119
  2.7 1.1 multiply_convert_fusion
  3.8 0.3 reshape.130
  4.2 0.3 reshape.131
  4.5 1.1 copy_bitcast_fusion.2
  5.6 0.5 reshape.134
  6.2 0.9 copy.18
  7.1 0.3 sub.40
  7.4 0.1 broadcast_multiply_fusion
  7.5 0.1 mul.117
  7.6 1.6 mul.118
  9.1 0.1 mul.122
  9.2 1.0 mul.123
  10.1 0.1 mul.107
  10.2 1.6 mul.108
  11.8 104.1 %exchange.1 = (bf16[16,32,320]{2,1,0:T(8,128)(2,1)}, bf16[16,32,320]{2,1,0:T(8,128)(2,1)}, bf16[2,160,2048]{2,1,0:T(8,128)(2,1)}, bf16[2,160,640]{2,1,0:T(8,128)...) custom-call(bf16[16,32,320]{2,1,0:T(8,128)(2,1)} %get-tuple-element.57.refs_0_, ...), custom_call_target="tpu_custom_call" | custom-call | flops 30000001024 | tf_op jit(solution)/shard_map/exchange/pallas_call | solution.py:357
  115.9 2.8 fusion.9.refs_1_
  118.7 3.8 fusion.2
  122.5 1.6 copy.19
  124.0 3.2 fusion.8.refs_0_
  127.3 76.6 %reduce_logits.1 = (f32[32,2048]{1,0:T(8,128)}, bf16[32,640]{1,0:T(8,128)(2,1)}, bf16[256,320]{1,0:T(8,128)(2,1)}, bf16[4,160,1728]{2,1,0:T(8,128)(2,1)}) custom-call(f32[4,4,32,2048]{3,2,1,0:T(8,128)} %fusion.8.refs_0_, f32[4,4,32,640]{3,2,1,0:T(8,128)} %fusion.9.refs_1_, bf16[2,4,256,320]{3,2,1,0:T(8,128)(2,1)} %bitcast.66, bf16[160,1728]{1,0:T(8,128)(2,1)} %bitcast.81), custom_call_target="tpu_custom_call" | custom-call | flops 60000002048 | tf_op jit(solution)/shard_map/reduce_logits/pallas_call | solution.py:357
  203.9 25.1 %softmax.1 = (bf16[32,2048]{1,0:T(8,128)(2,1)}, bf16[4,160,1728]{2,1,0:T(8,128)(2,1)}) custom-call(f32[32,2048]{1,0:T(8,128)} %get-tuple-element.32.refs_0_, bf16[4,160,1728]{2,1,0:T(8,128)(2,1)} %get-tuple-element.33.refs_1_), custom_call_target="tpu_custom_call" | custom-call | flops 20000000000 | tf_op jit(solution)/shard_map/softmax/pallas_call | solution.py:357
  229.0 49.0 %gather_probs.1 = (bf16[4,4,2,16,2048]{4,3,2,1,0:T(8,128)(2,1)}, bf16[4,4,2,16,640]{4,3,2,1,0:T(8,128)(2,1)}, bf16[2,144,1728]{2,1,0:T(8,128)(2,1)}, bf16[2,144,1728]{2,1,0:T(8,128)(2,1)}) custom-call(bf16[2,16,2048]{2,1,0:T(8,128)(2,1)} %bitcast.82, bf16[2,16,640]{2,1,0:T(8,128)(2,1)} %bitcast.83, bf16[432,1728]{1,0:T(8,128)(2,1)} %bitcast.76, ...), custom_call_target="tpu_custom_call" | custom-call | flops 30000001024 | tf_op jit(solution)/shard_map/gather_probs/pallas_call | solution.py:357
  278.1 2.9 dot_general.23
  281.0 1.9 fusion.10
  283.0 0.2 reshape.151
  283.2 1.0 copy.31.refs_0_
  284.2 1.1 copy.26
  285.3 25.6 %reduce_common.1 = (f32[64,320]{1,0:T(8,128)}, bf16[4,160,1728]{2,1,0:T(8,128)(2,1)}, bf16[2,144,1728]{2,1,0:T(8,128)(2,1)}) custom-call(f32[2,4,64,320]{3,2,1,0:T(8,128)} %copy.31.refs_0_, bf16[4,160,1728]{2,1,0:T(8,128)(2,1)} %get-tuple-element.33.refs_1_, bf16[432,1728]{1,0:T(8,128)(2,1)} %bitcast.78), custom_call_target="tpu_custom_call" | custom-call | flops 20000000000 | tf_op jit(solution)/shard_map/reduce_common/pallas_call | solution.py:357
  311.0 1.0 sub.41
  311.9 0.1 sub.42
  312.0 0.1 sub.43
  312.2 0.8 convert_subtract_fusion.refs_0_
  312.9 13.1 %exchange_grads.1 = f32[16,16,320]{2,1,0:T(8,128)} custom-call(f32[16,16,320]{2,1,0:T(8,128)} %convert_subtract_fusion.refs_0_), custom_call_target="tpu_custom_call" | custom-call | flops 12000000000 | tf_op jit(solution)/shard_map/exchange_grads/pallas_call | solution.py:357
  326.0 1.3 fusion.5
  327.4 1.4 reshape.141
  328.8 0.5 fusion.7
  329.4 0.7 fusion.6
  330.1 0.1 copy.24
  330.2 1.0 reshape.142.refs_0_
  331.2 28.4 %gather_back.1 = (bf16[2,4,2,16,2560]{4,3,2,1,0:T(8,128)(2,1)}, bf16[4,160,1728]{2,1,0:T(8,128)(2,1)}) custom-call(bf16[2,16,2560]{2,1,0:T(8,128)(2,1)} %reshape.142.refs_0_, bf16[4,160,1728]{2,1,0:T(8,128)(2,1)} %get-tuple-element.33.refs_1_), custom_call_target="tpu_custom_call" | custom-call | flops 20000000000 | tf_op jit(solution)/shard_map/gather_back/pallas_call | solution.py:357
  359.6 2.6 reshape.143
  362.2 0.5 copy.46
  362.7 1.3 reshape.144.refs_0_
  364.0 127.3 %rotate_all.1 = (bf16[4,2,2,2,4,32,432]{6,5,4,3,2,1,0:T(8,128)(2,1)}, bf16[4,640,128]{2,1,0:T(8,128)(2,1)}) custom-call(bf16[2,128,2560]{2,1,0:T(8,128)(2,1)} %reshape.144.refs_0_, bf16[32,1728]{1,0:T(8,128)(2,1)} %refs_1_.1, bf16[4,160,1728]{2,1,0:T(8,128)(2,1)} %get-tuple-element.40.refs_2_, bf16[4,160,1728]{2,1,0:T(8,128)(2,1)} %get-tuple-element.41.refs_3_, ...), custom_call_target="tpu_custom_call" | custom-call | flops 109999996928 | tf_op jit(solution)/shard_map/rotate_all/pallas_call | solution.py:357
  491.3 13.1 %squares.1 = f32[432,640]{1,0:T(8,128)} custom-call(bf16[4,4,256,432]{3,2,1,0:T(8,128)(2,1)} %bitcast.61, bf16[4,640,128]{2,1,0:T(8,128)(2,1)} %bitcast.64, bf16[4,640,128]{2,1,0:T(8,128)(2,1)} %get-tuple-element.50.b_ref), custom_call_target="tpu_custom_call" | custom-call | tf_op jit(solution)/shard_map/squares/pallas_call | solution.py:902
  (28 shorter events, 0.2 us)
Async XLA Ops:
  0.0 4.2 copy-start.7
  3.8 1.8 copy-start.11
  4.5 2.8 copy-start
  5.6 1.8 copy-start.9
  115.9 2.8 copy-start.4
  122.5 1.6 copy-start.6
  282.9 1.3 copy-start.5
  311.0 1.2 copy-start.8
  312.9 13.1 %copy-start.3 = (f32[16,16,320]{2,1,0:T(8,128)S(1)}, f32[16,16,320]{2,1,0:T(8,128)}, u32[]{:S(2)}) copy-start(f32[16,16,320]{2,1,0:T(8,128)} %mul.123) | copy-start | bytes 983044
  312.9 13.1 %copy-start.10 = (f32[16,320]{1,0:T(8,128)S(1)}, f32[16,320]{1,0:T(8,128)}, u32[]{:S(2)}) copy-start(f32[16,320]{1,0:T(8,128)} %mul.119) | copy-start | bytes 61444
  326.0 2.8 copy-start.1
  326.0 2.8 copy-start.2

commit v4 on v3

--- a/solution.py
+++ b/solution.py
@@ -176,7 +176,7 @@
     return 6 * outer_size + 6
 
 
-def reduce_stage(net, base, sums, outer_size, me_o, me_i, on_o, on_i):
+def reduce_stage(net, base, sums, outer_size, me_o, me_i, on_o, on_i, prepare=None):
     ip, im, i2 = (turn(me_i, s, 4) for s in (1, 3, 2))
     offsets = (2, 1, 3, 0) if outer_size == 4 else (1, 0)
     rows = [turn(me_o, off, outer_size) for off in offsets]
@@ -233,19 +233,26 @@
                 s.tot[2, s.h(1)] += s.zfwd[1]
                 net.send(z + 5, s.tot.at[2, s.h(1)], s.zgot.at[1, s.h(1)], on_o(3))
 
+    def ready(k):
+        if prepare is not None:
+            prepare(rows[k])
+
     def steps():
+        ready(0)
         start_far(0)
+        start_near(0)
+        ready(1)
         start_far(1)
-        start_near(0)
         yield
         for k in range(outer_size):
-            if k + 2 < outer_size:
-                start_far(k + 2)
+            middle(k)
             if k + 1 < outer_size:
                 start_near(k + 1)
-            middle(k)
             if k >= 1:
                 total(k - 1)
+            if k + 2 < outer_size:
+                ready(k + 2)
+                start_far(k + 2)
             yield
         total(outer_size - 1)
 
@@ -301,8 +308,9 @@
         for kind, array, _ in tasks:
             rows, depth = array.shape[-2:]
             shape = (2, rows // 3, depth) if kind == "basis" else (4, rows, depth)
+            shape = (4, 4, *array.shape) if kind == "all" else shape
             self.outs.append(like(shape, array.dtype))
-        self.slots = 6 * len(tasks)
+        self.slots = 30 * len(tasks)
 
     def local(self):
         return [pltpu.SemaphoreType.DMA((max(len(self.tasks), 1),))]
@@ -314,13 +322,15 @@
                 found += [net.on_x(1), net.on_x(3)]
             elif kind == "z":
                 found += [net.on_z(1), net.on_z(3)]
+            elif kind == "all":
+                found += [net.on_x(1), net.on_x(3), net.on_z(1), net.on_z(3)]
             else:
                 found += [net.on_zl(1), net.on_core()]
         return found
 
     def stages(self, net, base, ins, outs, local):
         return [
-            self.stage(net, base + 6 * t, kind, ins[t], outs[t], step, local.at[t])
+            self.stage(net, base + 30 * t, kind, ins[t], outs[t], step, local.at[t])
             for t, (kind, _, step) in enumerate(self.tasks)
         ]
 
@@ -335,6 +345,14 @@
             yield
             net.recv(base + 1, out.at[1])
             return
+        if kind == "all":
+            copy = pltpu.make_async_copy(src, out.at[net.z, net.x], local)
+            copy.start()
+            slot = lambda o, i, h: out.at[o, i, h]
+            own = lambda h: src.at[h]
+            yield from gather_stage(net, base, own, slot, 4, net.z, net.x, net.on_z, net.on_x)
+            copy.wait()
+            return
         half = out.shape[1] // 2
         cut = lambda h: pl.ds(h * half, half)
         row = src if len(src.shape) == 2 else src.at[turn(net.z, step, 4)]
@@ -343,10 +361,7 @@
         if kind == "z":
             yield from ring(net, base, own, slot, net.z, net.on_z)
         else:
-            copy = pltpu.make_async_copy(row, out.at[net.x], local)
-            copy.start()
             yield from ring(net, base, own, slot, net.x, net.on_x)
-            copy.wait()
 
 
 def sems(slots):
@@ -398,10 +413,7 @@
         for a in range(na):
             copies.append(pltpu.make_async_copy(ins[a].at[me], outs[a].at[me], local.at[a]))
         for b in range(np_):
-            net.send(15 * na + b, shared[b], both[b].at[net.core], net.on_core())
-            copies.append(
-                pltpu.make_async_copy(shared[b], both[b].at[net.core], local.at[na + b])
-            )
+            net.send(15 * na + b, shared[b], both[b], net.on_core())
         for copy in copies:
             copy.start()
         extra = side.stages(net, 15 * na + max(np_, 1), side_in, side_out, side_local)
@@ -413,13 +425,13 @@
             for a in range(na):
                 net.recv(j * na + a, outs[a].at[source])
         for b in range(np_):
-            net.recv(15 * na + b, both[b].at[1 - net.core])
+            net.recv(15 * na + b, both[b])
         drive(*extra)
         for copy in copies:
             copy.wait()
         net.finish()
 
-    outs = [like(a.shape, a.dtype) for a in arrays] + [like((2, *p.shape), p.dtype) for p in pairs]
+    outs = [like(a.shape, a.dtype) for a in (*arrays, *pairs)]
     return call(
         kernel,
         collective_id,
@@ -427,60 +439,11 @@
         [ANY] * (na + np_ + nt),
         [ANY] * (na + np_ + nt),
         [
-            pltpu.SemaphoreType.DMA((na + np_,)),
+            pltpu.SemaphoreType.DMA((na,)),
             *side.local(),
             *sems(15 * na + max(np_, 1) + side.slots),
         ],
         (*arrays, *pairs, *side.arrays),
-        name,
-        cost,
-    )
-
-
-def gather_wide(shards, tasks, collective_id, name, cost):
-    n, nt = len(shards), len(tasks)
-    side = Side(tasks)
-
-    def kernel(*refs):
-        ins, side_in = refs[:n], refs[n : n + nt]
-        outs, side_out = refs[n + nt : 2 * n + nt], refs[2 * n + nt : 2 * (n + nt)]
-        local, side_local, send_sem, recv_sem = refs[2 * (n + nt) :]
-        net = Net(send_sem, recv_sem)
-        ones = [net.on_x(1), net.on_x(3), net.on_z(1), net.on_z(3)]
-        net.greet(ones + side.peers(net))
-        copies, stages = [], []
-
-        def stage(a):
-            half = ins[a].shape[0] // 2
-            slot = lambda o, i, h: outs[a].at[o, i, pl.ds(h * half, half)]
-            own = lambda h: ins[a].at[pl.ds(h * half, half)]
-            for h in range(2):
-                copy = pltpu.make_async_copy(
-                    own(h), slot(net.z, net.x, h), local.at[2 * a + h]
-                )
-                copy.start()
-                copies.append(copy)
-            base = gather_slots(4) * a
-            return gather_stage(net, base, own, slot, 4, net.z, net.x, net.on_z, net.on_x)
-
-        stages = [stage(a) for a in range(n)]
-        drive(*stages, *side.stages(net, gather_slots(4) * n, side_in, side_out, side_local))
-        for copy in copies:
-            copy.wait()
-        net.finish()
-
-    return call(
-        kernel,
-        collective_id,
-        [like((4, 4, *shard.shape), shard.dtype) for shard in shards] + side.outs,
-        [ANY] * (n + nt),
-        [ANY] * (n + nt),
-        [
-            pltpu.SemaphoreType.DMA((2 * n,)),
-            *side.local(),
-            *sems(gather_slots(4) * n + side.slots),
-        ],
-        (*shards, *side.arrays),
         name,
         cost,
     )
@@ -536,52 +499,175 @@
     )
 
 
-def softmax_narrow(logits, tasks, collective_id, name, cost):
-    rows, columns = logits.shape
-    side, nt = Side(tasks), len(tasks)
+def front(normed, inputs, unembeds, bases_in, ids, down, basis, collective_id, name, cost):
+    tokens, features = normed.shape[2:]
+    half = features // 2
+    vocab, width = unembeds[0].shape[1], bases_in[0].shape[1]
+    count = ids.shape[0] // 8
+    tasks = [("z", down, 0), ("x", down, 1)] + [("basis", basis, j) for j in range(3)]
+    side = Side(tasks)
+    base_i = reduce_slots(4)
+    base_p = base_i + reduce_slots(4)
+    base_s = base_p + reduce_slots(2)
+    base_g = base_s + 7
+    base_t = base_g + gather_slots(4)
 
     def kernel(*refs):
-        l_ref, side_in, p_ref, side_out = refs[0], refs[1 : 1 + nt], refs[1 + nt], refs[2 + nt : -5]
-        mine, got, side_local, send_sem, recv_sem = refs[-5:]
+        n_ref, i_ref, id_ref, u0, u1, b0, b1, d_ref, basis_ref = refs[:9]
+        common_ref, rot_ref, picked_ref, dz_ref, dx_ref, t0, t1, t2 = refs[9:17]
+        unembed, basis_in, logit_part, input_part, pick_part = refs[17:22]
+        sum_l, sum_i, sum_p = (refs[22 + 6 * j : 28 + 6 * j] for j in range(3))
+        logits, mine, got, probs, every, local, send_sem, recv_sem = refs[40:]
         net = Net(send_sem, recv_sem)
-        peers = [{"narrow": turn(net.narrow, k, 8)} for k in range(1, 8)]
-        top = jnp.max(l_ref[...], axis=1, keepdims=True)
-        mine[0] = jnp.broadcast_to(top, (rows, 128))
+        c = net.core
+        loads = [
+            pltpu.make_async_copy(u0, unembed.at[pl.ds(c * half, half)], local.at[0]),
+            pltpu.make_async_copy(u1, unembed.at[pl.ds((1 - c) * half, half)], local.at[1]),
+            pltpu.make_async_copy(b0, basis_in.at[pl.ds(c * half, half)], local.at[2]),
+            pltpu.make_async_copy(b1, basis_in.at[pl.ds((1 - c) * half, half)], local.at[3]),
+        ]
+        for load in loads:
+            load.start()
+        ring_peers = [net.on_x(1), net.on_x(3), net.on_z(1), net.on_z(3), net.on_core()]
+        narrow_peers = [{"narrow": turn(net.narrow, k, 8)} for k in range(1, 8)]
+        net.greet(ring_peers + narrow_peers)
+        for load in loads:
+            load.wait()
+
+        def dot_row(left, right, part):
+            def run(row):
+                rows = left[row].reshape(4 * tokens, features)
+                value = jnp.dot(rows, right[...], preferred_element_type=F32)
+                part[row] = value.reshape(4, tokens, part.shape[3])
+
+            return run
+
+        main, (end,) = reduce_stage(
+            net, 0, [Sum(logit_part, *sum_l)], 4, net.z, net.x, net.on_z, net.on_x,
+            dot_row(n_ref, unembed, logit_part),
+        )
+        late, (end_i,) = reduce_stage(
+            net, base_i, [Sum(input_part, *sum_i)], 4, net.z, net.x, net.on_z, net.on_x,
+            dot_row(i_ref, basis_in, input_part),
+        )
+        picks, (end_p,) = reduce_stage(
+            net, base_p, [Sum(pick_part, *sum_p)], 2, net.zl, net.y, net.on_zl, net.on_y
+        )
+
+        def extra(t, out, kind, src, step):
+            return side.stage(net, base_t + 30 * t, kind, src, out, step, None)
+
+        ring_z = extra(0, dz_ref, "z", d_ref, 0)
+        ring_x = extra(1, dx_ref, "x", dz_ref, 1)
+        thirds = [extra(2 + j, out, "basis", basis_ref, j) for j, out in enumerate((t0, t1, t2))]
+
+        next(main)
+        next(ring_z)
+        next(main)
+
+        def pick(j, carry):
+            some = id_ref[pl.ds(pl.multiple_of(j * count, count), count)]
+            one = some == lax.broadcasted_iota(jnp.int32, (count, vocab), 1)
+            value = contract_last(jnp.where(one, 1.0, 0.0).astype(BF16), unembed[...])
+            pick_part[lax.div(j, 4), lax.rem(j, 4)] = value.astype(BF16)
+            return carry
+
+        lax.fori_loop(0, 4, pick, 0)
+        next(ring_z)
+        next(main)
+        lax.fori_loop(4, 8, pick, 0)
+        next(picks)
+        next(main)
+        next(ring_z)
+        next(picks)
+        next(main)
+        next(late)
+        drive(ring_z)
+        next(ring_x)
+        next(ring_x)
+        drive(main)
+        for h in range(2):
+            logits[pl.ds(h * (tokens // 2), tokens // 2), :] = end(h)
+        top = jnp.max(logits[...], axis=1, keepdims=True)
+        mine[0] = jnp.broadcast_to(top, (tokens, 128))
         mine[1] = jnp.broadcast_to(
-            jnp.sum(jnp.exp(l_ref[...] - top), axis=1, keepdims=True), (rows, 128)
+            jnp.sum(jnp.exp(logits[...] - top), axis=1, keepdims=True), (tokens, 128)
         )
-        net.greet(peers + side.peers(net))
         for k in range(7):
-            net.send(k, mine, got.at[k], peers[k])
-        extra = side.stages(net, 7, side_in, side_out, side_local)
-        for _ in range(2):
-            for stage in extra:
-                next(stage)
+            net.send(base_s + k, mine, got.at[k], narrow_peers[k])
+        next(late)
+        next(thirds[0])
         for k in range(7):
-            net.recv(k, got.at[k])
+            net.recv(base_s + k, got.at[k])
         largest = mine[0]
         for k in range(7):
             largest = jnp.maximum(largest, got[k, 0])
         total = mine[1] * jnp.exp(mine[0] - largest)
         for k in range(7):
             total += got[k, 1] * jnp.exp(got[k, 0] - largest)
-        p_ref[...] = (jnp.exp(l_ref[...] - largest[:, :1]) / total[:, :1]).astype(BF16)
-        drive(*extra)
+        value = (jnp.exp(logits[...] - largest[:, :1]) / total[:, :1]).astype(BF16)
+        probs[...] = value.reshape(2, tokens // 2, vocab)
+        every[net.z, net.x] = value.reshape(2, tokens // 2, vocab)
+        slot = lambda o, i, h: every.at[o, i, h]
+        own = lambda h: probs.at[h]
+        spread = gather_stage(
+            net, base_g, own, slot, 4, net.z, net.x, net.on_z, net.on_x
+        )
+        next(spread)
+        next(late)
+        next(ring_x)
+        next(spread)
+        next(thirds[1])
+        next(late)
+        next(thirds[0])
+        next(spread)
+        next(thirds[2])
+        next(picks)
+        next(spread)
+        next(late)
+        drive(late)
+        drive(spread)
+        for h in range(2):
+            rot_ref[h] = end_i(h).astype(BF16)
+        drive(picks)
+        for h in range(2):
+            picked_ref[pl.ds(h * (count // 2), count // 2), :] = end_p(h).astype(BF16)
+        for row in range(4):
+            common_ref[row] = contract_last(
+                every[row].reshape(4 * tokens, vocab), unembed[...]
+            )
+        drive(ring_x, *thirds)
         net.finish()
 
     return call(
         kernel,
         collective_id,
-        [like((rows, columns), BF16)] + side.outs,
-        [VMEM] + [ANY] * nt,
-        [VMEM] + [ANY] * nt,
         [
-            pltpu.VMEM((2, rows, 128), F32),
-            pltpu.VMEM((7, 2, rows, 128), F32),
-            *side.local(),
-            *sems(7 + side.slots),
+            like((4, 4 * tokens, features), F32),
+            like((2, tokens // 2, width), BF16),
+            like((count, features), BF16),
+            *side.outs,
         ],
-        (logits, *side.arrays),
+        [VMEM] * 3 + [ANY] * 6,
+        [VMEM] * 3 + [ANY] * 5,
+        [
+            pltpu.VMEM((features, vocab), BF16),
+            pltpu.VMEM((features, width), BF16),
+            pltpu.VMEM((4, 4, tokens, vocab), F32),
+            pltpu.VMEM((4, 4, tokens, width), F32),
+            pltpu.VMEM((2, 4, count, features), BF16),
+            *Sum.scratch(4, tokens, vocab, F32),
+            *Sum.scratch(4, tokens, width, F32),
+            *Sum.scratch(2, count, features, BF16),
+            pltpu.VMEM((tokens, vocab), F32),
+            pltpu.VMEM((2, tokens, 128), F32),
+            pltpu.VMEM((7, 2, tokens, 128), F32),
+            pltpu.VMEM((2, tokens // 2, vocab), BF16),
+            pltpu.VMEM((4, 4, 2, tokens // 2, vocab), BF16),
+            pltpu.SemaphoreType.DMA((4,)),
+            *sems(base_t + side.slots),
+        ],
+        (normed, inputs, ids, *unembeds, *bases_in, down, basis),
         name,
         cost,
     )
@@ -631,28 +717,36 @@
     )
 
 
-def rotate_all(back, gate, downs, basis, thirds, inputs, collective_id, name, cost):
+def rotate_all(back, gate, down, down_z, downs, bases, thirds, inputs, collective_id, name, cost):
     tokens, depth = gate.shape
-    columns = basis.shape[1]
+    columns = bases[0].shape[0]
+    width = inputs.shape[1]
     rows = 2 * tokens
     features = back.shape[2]
     cuts = (pl.ds(0, 896), pl.ds(896, depth - 896))
 
     def kernel(*refs):
-        back_ref, g_ref, d_refs, basis_ref = refs[0], refs[1], refs[2:6], refs[6]
-        t_refs, i_ref, o_ref, j_ref = refs[7:10], refs[10], refs[11], refs[12]
-        down, bases, h_ref = refs[13:16]
-        half_in, gated, other, every, part, fwd, mid, got, mine = refs[16:25]
-        local, send_sem, recv_sem = refs[25:]
+        back_ref, g_ref, i_ref, own_ref, z_ref, d_refs = *refs[:5], refs[5:9]
+        b_refs, t_refs, o_ref = refs[9:11], refs[11:14], refs[14]
+        down, bases, h_ref, j_ref, spun, pairs, corrected = refs[15:22]
+        half_in, gated, other, every, part, fwd, mid, got, mine = refs[22:31]
+        local, send_sem, recv_sem = refs[31:]
         net = Net(send_sem, recv_sem)
         c, z, x, zl, y = net.core, net.z, net.x, net.zl, net.y
         base_z, base_r, base_n = 8, 40, 64
-        loads = [
-            pltpu.make_async_copy(d_refs[k], down.at[k], local.at[10 + k]) for k in range(4)
-        ]
+        loads = []
+        for k in range(4):
+            block = z_ref.at[turn(z, k, 4)] if k else own_ref
+            loads.append(pltpu.make_async_copy(block, down.at[k, x], local.at[16 + 4 * k]))
+            for step in range(1, 4):
+                at = turn(x, step, 4)
+                loads.append(
+                    pltpu.make_async_copy(
+                        d_refs[k].at[at], down.at[k, at], local.at[16 + 4 * k + step]
+                    )
+                )
         loads += [
-            pltpu.make_async_copy(basis_ref.at[c], bases.at[0], local.at[14]),
-            pltpu.make_async_copy(basis_ref.at[1 - c], bases.at[1], local.at[15]),
+            pltpu.make_async_copy(b_refs[m], bases.at[m], local.at[8 + m]) for m in range(2)
         ]
         third = columns // 3
         for j in range(3):
@@ -661,14 +755,14 @@
                     pltpu.make_async_copy(
                         t_refs[j].at[m],
                         bases.at[2 + m, pl.ds(j * third, third)],
-                        local.at[16 + 2 * j + m],
+                        local.at[10 + 2 * j + m],
                     )
                 )
         for load in loads:
             load.start()
         ones = [net.on_x(1), net.on_x(3), net.on_z(1), net.on_z(3)]
         net.greet(ones + [net.on_y(1), net.on_y(3), net.on_zl(1), net.on_core()])
-        for load in loads[:4]:
+        for load in loads[:16]:
             load.wait()
         quarter = features // 4
         left = back_ref[...].reshape(2 * 4 * tokens, features)
@@ -760,16 +854,35 @@
             value = part[k, y, 0] + got[k, 0, 0] + got[k, 1, 0]
             mine[k, 0] = value.astype(BF16).reshape(2, tokens, columns)
 
-        last = []
+        def square(k, stage):
+            drive(stage)
+            if k == 0:
+                net.recv(1, j_ref)
+            e = order[k]
+            pairs[:, : 4 * tokens] = i_ref[e]
+            pairs[:, 4 * tokens :] = j_ref[e]
+
+            def tile(t, carry):
+                cut = pl.ds(pl.multiple_of(t * 128, 128), 128)
+                total = None
+                for o in range(2):
+                    for s in range(2):
+                        right = spun[k, o, s].reshape(8 * tokens, columns)
+                        block = jnp.dot(pairs[cut], right, preferred_element_type=F32)
+                        block = block * block
+                        total = block if total is None else total + block
+                total = total * (1.0 / 16.0)
+                corrected[cut] = total if k == 0 else corrected[cut] + total
+                return carry
+
+            lax.fori_loop(0, width // 128, tile, 0)
 
         def spread(k):
             mine_k = lambda h: mine.at[k, 2 * h]
-            place = lambda o, i, h: o_ref.at[order[k], o, :, h, i]
+            place = lambda o, i, h: spun.at[k, o, :, h, i]
             net.recv(3 + k, mine.at[k, 2])
             for h in range(2):
-                copy = pltpu.make_async_copy(mine_k(h), place(zl, y, h), local.at[2 + 2 * k + h])
-                copy.start()
-                last.append(copy)
+                spun[k, zl, :, h, y] = mine[k, 2 * h]
             base = base_n + gather_slots(2) * k
             return gather_stage(net, base, mine_k, place, 2, zl, y, net.on_zl, net.on_y)
 
@@ -796,7 +909,7 @@
         for h in range(2):
             along(1, h)
         rest(0)
-        for copy in copies + loads[4:]:
+        for copy in copies + loads[16:]:
             copy.wait()
         multiply(0)
         reduce_start(0)
@@ -836,28 +949,34 @@
         next(spread_2)
         next(spread_1)
         reduce_middle(3)
+        square(0, spread_0)
         next(spread_2)
         reduce_end(3)
         spread_3 = spread(3)
         next(spread_3)
         next(spread_2)
+        square(1, spread_1)
         next(spread_3)
-        drive(spread_0, spread_1, spread_2, spread_3)
-        for copy in last:
-            copy.wait()
-        net.recv(1, j_ref)
+        next(spread_3)
+        square(2, spread_2)
+        square(3, spread_3)
+        o_ref[...] = corrected[...].T
         net.finish()
 
     return call(
         kernel,
         collective_id,
-        [like((4, 2, 2, 2, 4, tokens, columns), BF16), like(inputs.shape, BF16)],
-        [VMEM] * 2 + [ANY] * 9,
-        [ANY, ANY],
+        like((columns, width), F32),
+        [VMEM] * 3 + [ANY] * 11,
+        VMEM,
         [
             pltpu.VMEM((4, 4, features // 16, depth), BF16),
             pltpu.VMEM((4, columns, depth), BF16),
             pltpu.VMEM((2, 4 * tokens, depth), F32),
+            pltpu.VMEM(inputs.shape, BF16),
+            pltpu.VMEM((4, 2, 2, 2, 4, tokens, columns), BF16),
+            pltpu.VMEM((width, 8 * tokens), BF16),
+            pltpu.VMEM((width, columns), F32),
             pltpu.VMEM((4 * tokens, depth), F32),
             pltpu.VMEM((4, tokens, depth), BF16),
             pltpu.VMEM((2, tokens, depth), BF16),
@@ -867,51 +986,13 @@
             pltpu.VMEM((4, 2, rows, columns), F32),
             pltpu.VMEM((4, 2, 2, rows, columns), F32),
             pltpu.VMEM((4, 3, 2, tokens, columns), BF16),
-            pltpu.SemaphoreType.DMA((22,)),
+            pltpu.SemaphoreType.DMA((32,)),
             *sems(64 + 4 * gather_slots(2)),
         ],
-        (back, gate, *downs, basis, *thirds, inputs),
+        (back, gate, inputs, down, down_z, *downs, *bases, *thirds),
         name,
         cost,
     )
-
-
-def squares(rotated, own_inputs, other_inputs):
-    rows, width = rotated.shape[3], own_inputs.shape[1]
-    depth = own_inputs.shape[2]
-
-    def kernel(r_ref, a_ref, b_ref, o_ref, both, total):
-        example, sample = pl.program_id(0), pl.program_id(1)
-
-        @pl.when((example == 0) & (sample == 0))
-        def _():
-            total[...] = jnp.zeros_like(total)
-
-        @pl.when(sample == 0)
-        def _():
-            both[:, :depth] = a_ref[0]
-            both[:, depth:] = b_ref[0]
-
-        block = jnp.dot(both[...], r_ref[0, 0], preferred_element_type=F32)
-        total[...] += block * block * (1.0 / 16.0)
-
-        @pl.when((example == 3) & (sample == 3))
-        def _():
-            o_ref[...] = total[...].T
-
-    return pl.pallas_call(
-        kernel,
-        grid=(4, 4),
-        out_shape=like((rows, width), F32),
-        in_specs=[
-            pl.BlockSpec((1, 1, 2 * depth, rows), lambda e, s: (e, s, 0, 0)),
-            pl.BlockSpec((1, width, depth), lambda e, s: (e, 0, 0)),
-            pl.BlockSpec((1, width, depth), lambda e, s: (e, 0, 0)),
-        ],
-        out_specs=pl.BlockSpec((rows, width), lambda e, s: (0, 0)),
-        scratch_shapes=[pltpu.VMEM((width, 2 * depth), BF16), pltpu.VMEM((width, rows), F32)],
-        name="squares",
-    )(rotated, own_inputs, other_inputs)
 
 
 def contract_last(left, right):
@@ -927,7 +1008,6 @@
     samples = labels.shape[1]
     vocab, part = unembed.shape
     hidden = down_weight.shape[0]
-    columns = basis_out.shape[1]
     width_in = basis_in.shape[1]
     pair = 2 * part
     core_tokens = 16 * tokens
@@ -941,7 +1021,7 @@
         return rows.reshape(tokens, 16, pair).transpose(1, 0, 2)
 
     down, basis = down_weight.T, basis_out.T
-    normed_cols, inputs_cols, unembed_rows, basis_in_rows, basis_both, down_0 = exchange(
+    normed_cols, inputs_cols, unembed_other, basis_in_other, basis_other, down_0 = exchange(
         [blocks(normed), blocks(layer_in)],
         [unembed.T, basis_in, basis],
         [("x", down, 0)],
@@ -949,43 +1029,27 @@
         "exchange",
         30,
     )
-    unembed_rows = unembed_rows.reshape(pair, vocab)
-    basis_in_rows = basis_in_rows.reshape(pair, width_in)
-    logits_part = jnp.dot(
-        normed_cols.reshape(core_tokens, pair), unembed_rows, preferred_element_type=F32
-    )
-    inputs_part = jnp.dot(
-        inputs_cols.reshape(core_tokens, pair), basis_in_rows, preferred_element_type=F32
-    )
     mine = lax.dynamic_index_in_dim(
         labels.reshape(16, 2, 8, few, samples), core, 1, keepdims=False
     )
-    shifted = mine.transpose(1, 0, 2, 3).reshape(core_tokens * samples) - narrow * vocab
-    chosen = (shifted[:, None] == lax.broadcasted_iota(jnp.int32, (1, vocab), 1)).astype(BF16)
-    picked = contract_last(chosen, unembed_rows).astype(BF16)
-    logits, inputs_rot, picked, down_z = reduce_over(
-        [logits_part.reshape(4, 4, tokens, vocab), inputs_part.reshape(4, 4, tokens, width_in)],
-        [picked.reshape(2, 4, 16 * few * samples, pair)],
-        [("z", down, 0)],
-        [F32, BF16, BF16],
+    shifted = mine.transpose(1, 0, 2, 3).reshape(core_tokens * samples, 1) - narrow * vocab
+    common, inputs_rot, picked, down_z, down_1, third_0, third_1, third_2 = front(
+        normed_cols.reshape(4, 4, tokens, pair),
+        inputs_cols.reshape(4, 4, tokens, pair),
+        [unembed.T, unembed_other],
+        [basis_in, basis_in_other],
+        shifted,
+        down,
+        basis,
         1,
-        "reduce_logits",
-        60,
-    )
-    probs, down_1 = softmax_narrow(logits, [("x", down_z, 1)], 2, "softmax", 20)
-    probs_all, inputs_all, third_0, third_1 = gather_wide(
-        [probs.reshape(2, tokens // 2, vocab), inputs_rot.reshape(2, tokens // 2, width_in)],
-        [("basis", basis, 0), ("basis", basis, 1)],
-        3,
-        "gather_probs",
-        30,
+        "front",
+        100,
+    )
+    common = common.reshape(16, 8, few, pair).transpose(1, 0, 2, 3).reshape(2, 4, 16 * few, pair)
+    common, down_2, inputs_all = reduce_over(
+        [], [common], [("x", down_z, 2), ("all", inputs_rot, 0)], [F32], 4, "reduce_common", 20
     )
     inputs_all = inputs_all.reshape(4, 4 * tokens, width_in).transpose(0, 2, 1)
-    common = contract_last(probs_all.reshape(core_tokens, vocab), unembed_rows)
-    common = common.reshape(16, 8, few, pair).transpose(1, 0, 2, 3).reshape(2, 4, 16 * few, pair)
-    common, down_2, third_2 = reduce_over(
-        [], [common], [("x", down_z, 2), ("basis", basis, 2)], [F32], 4, "reduce_common", 20
-    )
     grads = common.reshape(16, few, 1, pair) - picked.astype(F32).reshape(16, few, samples, pair)
     (grads,) = exchange([grads.reshape(16, few * samples, pair)], [], [], 5, "exchange_grads", 12)
     grads = grads.transpose(1, 0, 2).reshape(few, samples, width)
@@ -1004,19 +1068,18 @@
         back.reshape(2, few * samples, width // 2), [("x", down_z, 3)], 6, "gather_back", 20
     )
     back = back.reshape(8, 2, few, samples, width // 2).transpose(1, 3, 0, 2, 4)
-    rotated, inputs_other = rotate_all(
+    return rotate_all(
         back.reshape(2, samples * tokens, width // 2),
         gate_value,
+        down,
+        down_z,
         [down_0, down_1, down_2, down_3],
-        basis_both,
+        [basis, basis_other],
         [third_0, third_1, third_2],
         inputs_all,
         7,
         "rotate_all",
         110,
-    )
-    return squares(
-        rotated.reshape(4, samples, 8 * tokens, columns), inputs_all, inputs_other
     )
 
 

time: 505 us -> 411 us (0.81)
  Pallas kernels: 462 us -> 378 us
  matrix products: 11.7 us -> 0 us
    pallas_call x8 -> x6, Pallas kernels: 449 us -> 378 us  [call(): pl.pallas_call(kernel, out_shape=outs, in_specs=in_specs, out_specs=out_s...]
    pallas_call x1 -> x0, Pallas kernels: 13.1 us -> none  [squares(): pl.pallas_call(kernel, grid=(4, 4), out_shape=like((rows, width), F32), i...]
    dot_general x4 -> x0, matrix products: 11.7 us -> none  [the longest x2 5.66 us: contract_last(): lax.dot_general(left, right, (((1,), (1,)), ((), ())), preferred_element_...]
where the time goes in v4:
time: 411 us; the launch traced here: 410 us
  Pallas kernels  378 us (92%)
  local copies, waits for them, and re-layouts  25.5 us (6%)
  other arithmetic  5.96 us (1%)
    pallas_call x6, Pallas kernels, call(): pl.pallas_call(kernel, out_shape=outs, in_specs=in_specs, out_specs=out_s...  378 us

profile of v4, /device:TPU:1, one launch (start us, length us, event | category | flops | bytes accessed | tf_op | source)
XLA Modules:
  0.0 410.1 jit_solution(3465691219098852331)
XLA Ops:
  0.0 1.2 multiply_reduce_fusion
  1.2 0.1 multiply_multiply_fusion
  1.3 1.4 mul.119
  2.7 1.1 multiply_convert_fusion
  3.8 0.0 copy-start.8
  3.8 0.3 reshape.116
  4.2 0.0 copy-done.4
  4.2 0.3 reshape.117
  4.5 0.0 copy-start
  4.5 1.1 copy_bitcast_fusion.1
  5.6 0.0 copy-done.8
  5.6 0.5 reshape.120
  6.2 0.9 copy.17
  7.1 0.0 copy-done
  7.1 0.0 copy-done.6
  7.1 0.1 broadcast_multiply_fusion
  7.2 0.1 mul.117
  7.3 1.6 mul.118
  8.9 0.1 mul.122
  9.0 1.0 mul.123
  9.9 0.1 mul.107
  10.0 1.6 mul.108
  11.6 1.3 sub.39.refs_2_
  12.9 40.3 %exchange.1 = (bf16[16,32,320]{2,1,0:T(8,128)(2,1)}, bf16[16,32,320]{2,1,0:T(8,128)(2,1)}, bf16[160,2048]{1,0:T(8,128)(2,1)}, bf16[160,640]{1,0:T(8,128)(2,1)}, ...) custom-call(bf16[16,32,320]{2,1,0:T(8,128)(2,1)} %get-tuple-element.49.refs_0_, ...), custom_call_target="tpu_custom_call" | custom-call | flops 30000001024 | tf_op jit(solution)/shard_map/exchange/pallas_call | solution.py:372
  53.2 128.9 %front.1 = (f32[4,128,320]{2,1,0:T(8,128)}, bf16[2,16,640]{2,1,0:T(8,128)(2,1)}, bf16[256,320]{1,0:T(8,128)(2,1)}, bf16[4,160,1728]{2,1,0:T(8,128)(2,1)}, bf16[4...) custom-call(bf16[4,4,32,320]{3,2,1,0:T(8,128)(2,1)} %bitcast.45, ...), custom_call_target="tpu_custom_call" | custom-call | flops 99999997952 | tf_op jit(solution)/shard_map/front/pallas_call | solution.py:372
  182.1 1.4 reshape.121
  183.4 0.1 copy.19
  183.5 1.2 reshape.122.refs_0_
  184.7 35.0 %reduce_common.1 = (f32[64,320]{1,0:T(8,128)}, bf16[4,160,1728]{2,1,0:T(8,128)(2,1)}, bf16[4,4,2,16,640]{4,3,2,1,0:T(8,128)(2,1)}) custom-call(f32[2,4,64,320]{3,2,1,0:T(8,128)} %reshape.122.refs_0_, bf16[4,160,1728]{2,1,0:T(8,128)(2,1)} %get-tuple-element.29.refs_1_.refs_4_, bf16[2,16,640]{2,1,0:T(8,128)(2,1)} %get-tuple-element.30.refs_2_), custom_call_target="tpu_custom_call" | custom-call | flops 20000000000 | tf_op jit(solution)/shard_map/reduce_common/pallas_call | solution.py:372
  219.7 1.0 sub.34
  220.7 2.2 copy.24
  222.9 0.1 sub.35
  222.9 0.1 sub.36
  223.1 0.0 copy-done.5
  223.1 0.8 convert_subtract_fusion.refs_0_
  223.9 12.8 %exchange_grads.1 = f32[16,16,320]{2,1,0:T(8,128)} custom-call(f32[16,16,320]{2,1,0:T(8,128)} %convert_subtract_fusion.refs_0_), custom_call_target="tpu_custom_call" | custom-call | flops 12000000000 | tf_op jit(solution)/shard_map/exchange_grads/pallas_call | solution.py:372
  236.7 1.3 fusion.2
  238.1 1.4 reshape.125
  239.5 0.5 fusion.4
  240.0 0.7 fusion.3
  240.8 0.1 copy.22
  240.9 1.0 reshape.126.refs_0_
  241.9 30.1 %gather_back.1 = (bf16[2,4,2,16,2560]{4,3,2,1,0:T(8,128)(2,1)}, bf16[4,160,1728]{2,1,0:T(8,128)(2,1)}) custom-call(bf16[2,16,2560]{2,1,0:T(8,128)(2,1)} %reshape.126.refs_0_, bf16[4,160,1728]{2,1,0:T(8,128)(2,1)} %get-tuple-element.29.refs_1_.refs_4_), custom_call_target="tpu_custom_call" | custom-call | flops 20000000000 | tf_op jit(solution)/shard_map/gather_back/pallas_call | solution.py:372
  272.0 2.8 reshape.127
  274.9 0.5 copy.38
  275.4 1.2 reshape.128.refs_0_
  276.6 131.2 %rotate_all.1 = f32[432,640]{1,0:T(8,128)} custom-call(bf16[2,128,2560]{2,1,0:T(8,128)(2,1)} %reshape.128.refs_0_, bf16[32,1728]{1,0:T(8,128)(2,1)} %refs_1_.1, bf16[4,640,128]{2,1,0:T(8,128)(2,1)} %bitcast.34, bf16[160,1728]{1,0:T(8,128)(2,1)} %bitcast.44, bf16[4,160,1728]{2,1,0:T(8,128)(2,1)} %get-tuple-element.29.refs_1_.refs_4_, ...), custom_call_target="tpu_custom_call" | custom-call | flops 109999996928 | tf_op jit(solution)/shard_map/rotate_all/pallas_call | solution.py:372
  407.8 2.3 copy.40
  (14 shorter events, 0.1 us)
Async XLA Ops:
  0.0 4.2 %copy-start.4 = (bf16[32,5120]{1,0:T(8,128)(2,1)S(1)}, bf16[32,5120]{1,0:T(8,128)(2,1)}, u32[]{:S(2)}) copy-start(bf16[32,5120]{1,0:T(8,128)(2,1)} %param.13) | copy-start | bytes 983044
  3.8 1.8 copy-start.8
  4.5 2.6 copy-start
  5.6 1.5 copy-start.6
  219.7 3.4 copy-start.5
  223.9 12.8 %copy-start.3 = (f32[16,16,320]{2,1,0:T(8,128)S(1)}, f32[16,16,320]{2,1,0:T(8,128)}, u32[]{:S(2)}) copy-start(f32[16,16,320]{2,1,0:T(8,128)} %mul.123) | copy-start | bytes 983044
  223.9 12.8 %copy-start.7 = (f32[16,320]{1,0:T(8,128)S(1)}, f32[16,320]{1,0:T(8,128)}, u32[]{:S(2)}) copy-start(f32[16,320]{1,0:T(8,128)} %mul.119) | copy-start | bytes 61444
  236.7 2.8 copy-start.1
  236.7 2.8 copy-start.2

commit v5 on v4

--- a/solution.py
+++ b/solution.py
@@ -42,11 +42,14 @@
     def on_core(self):
         return {"wide": self.wide + 1 - 2 * self.core}
 
-    def greet(self, devices):
+    def call_out(self, devices):
         barrier = pltpu.get_barrier_semaphore()
         for device in devices:
             pl.semaphore_signal(barrier, inc=1, device_id=device, device_id_type=MESH)
-        pl.semaphore_wait(barrier, len(devices))
+        return lambda: pl.semaphore_wait(barrier, len(devices))
+
+    def greet(self, devices):
+        self.call_out(devices)()
 
     def copy(self, slot, src, dst, device):
         return pltpu.make_async_remote_copy(
@@ -79,20 +82,20 @@
     ip, im, i2 = (turn(me_i, s, 4) for s in (1, 3, 2))
     inner = lambda row: base + 6 + 6 * row
 
-    def along(row, o, first):
+    def along(row, o, h, first=False):
         b = inner(row)
-        src = own if first else (lambda h: slot(o, me_i, h))
-        net.send(b, src(0), slot(o, me_i, 0), on_i(1))
-        net.send(b + 2, src(1), slot(o, me_i, 1), on_i(3))
-        net.send(b + 1, src(1), slot(o, me_i, 1), on_i(1))
-        net.send(b + 3, src(0), slot(o, me_i, 0), on_i(3))
-
-    def forward(row, o):
+        src = own(h) if first else slot(o, me_i, h)
+        net.send(b + h, src, slot(o, me_i, h), on_i(1))
+        net.send(b + 3 - h, src, slot(o, me_i, h), on_i(3))
+
+    def forward(row, o, ways=(0, 1)):
         b = inner(row)
-        net.recv(b, slot(o, im, 0))
-        net.send(b + 4, slot(o, im, 0), slot(o, im, 0), on_i(1))
-        net.recv(b + 2, slot(o, ip, 1))
-        net.send(b + 5, slot(o, ip, 1), slot(o, ip, 1), on_i(3))
+        if 0 in ways:
+            net.recv(b, slot(o, im, 0))
+            net.send(b + 4, slot(o, im, 0), slot(o, im, 0), on_i(1))
+        if 1 in ways:
+            net.recv(b + 2, slot(o, ip, 1))
+            net.send(b + 5, slot(o, ip, 1), slot(o, ip, 1), on_i(3))
 
     def rest(row, o):
         b = inner(row)
@@ -107,24 +110,30 @@
         net.send(base + 2, own(1), slot(me_o, me_i, 1), on_o(3))
         net.send(base + 1, own(1), slot(me_o, me_i, 1), on_o(1))
         net.send(base + 3, own(0), slot(me_o, me_i, 0), on_o(3))
-        along(0, me_o, True)
+        for h in range(2):
+            along(0, me_o, h, True)
         yield
         net.recv(base, slot(om, me_i, 0))
         net.send(base + 4, slot(om, me_i, 0), slot(om, me_i, 0), on_o(1))
         net.recv(base + 2, slot(op, me_i, 1))
         net.send(base + 5, slot(op, me_i, 1), slot(op, me_i, 1), on_o(3))
         forward(0, me_o)
+        along(1, om, 0)
+        along(2, op, 1)
+        yield
         net.recv(base + 1, slot(om, me_i, 1))
-        along(1, om, False)
-        yield
+        along(1, om, 1)
         net.recv(base + 3, slot(op, me_i, 0))
-        along(2, op, False)
-        forward(1, om)
+        along(2, op, 0)
+        forward(1, om, (0,))
+        forward(2, op, (1,))
         yield
         net.recv(base + 4, slot(o2, me_i, 0))
+        along(3, o2, 0)
         net.recv(base + 5, slot(o2, me_i, 1))
-        along(3, o2, False)
-        forward(2, op)
+        along(3, o2, 1)
+        forward(1, om, (1,))
+        forward(2, op, (0,))
         yield
         forward(3, o2)
         for row, o in enumerate((me_o, om, op, o2)):
@@ -133,12 +142,13 @@
         oq = 1 - me_o
         for h in range(2):
             net.send(base + h, own(h), slot(me_o, me_i, h), on_o(1))
-        along(0, me_o, True)
+        for h in range(2):
+            along(0, me_o, h, True)
         yield
         forward(0, me_o)
         for h in range(2):
             net.recv(base + h, slot(oq, me_i, h))
-        along(1, oq, False)
+            along(1, oq, h)
         yield
         forward(1, oq)
         yield
@@ -337,6 +347,8 @@
     def stage(self, net, base, kind, src, out, step, local):
         if kind == "basis":
             rows = out.shape[1]
+            for _ in range((0, 2, 1)[step]):
+                yield
             net.send(base, src.at[pl.ds(rows * step, rows)], out.at[0], net.on_zl(1))
             yield
             yield
@@ -499,13 +511,12 @@
     )
 
 
-def front(normed, inputs, unembeds, bases_in, ids, down, basis, collective_id, name, cost):
+def front(normed, inputs, unembeds, bases_in, ids, down, collective_id, name, cost):
     tokens, features = normed.shape[2:]
     half = features // 2
     vocab, width = unembeds[0].shape[1], bases_in[0].shape[1]
     count = ids.shape[0] // 8
-    tasks = [("z", down, 0), ("x", down, 1)] + [("basis", basis, j) for j in range(3)]
-    side = Side(tasks)
+    side = Side([("z", down, 0), ("x", down, 0)])
     base_i = reduce_slots(4)
     base_p = base_i + reduce_slots(4)
     base_s = base_p + reduce_slots(2)
@@ -513,11 +524,11 @@
     base_t = base_g + gather_slots(4)
 
     def kernel(*refs):
-        n_ref, i_ref, id_ref, u0, u1, b0, b1, d_ref, basis_ref = refs[:9]
-        common_ref, rot_ref, picked_ref, dz_ref, dx_ref, t0, t1, t2 = refs[9:17]
-        unembed, basis_in, logit_part, input_part, pick_part = refs[17:22]
-        sum_l, sum_i, sum_p = (refs[22 + 6 * j : 28 + 6 * j] for j in range(3))
-        logits, mine, got, probs, every, local, send_sem, recv_sem = refs[40:]
+        n_ref, i_ref, id_ref, u0, u1, b0, b1, d_ref = refs[:8]
+        common_ref, rot_ref, picked_ref, dz_ref, dx_ref = refs[8:13]
+        unembed, basis_in, logit_part, input_part, pick_part = refs[13:18]
+        sum_l, sum_i, sum_p = (refs[18 + 6 * j : 24 + 6 * j] for j in range(3))
+        logits, mine, got, probs, every, local, send_sem, recv_sem = refs[36:]
         net = Net(send_sem, recv_sem)
         c = net.core
         loads = [
@@ -558,12 +569,7 @@
             return side.stage(net, base_t + 30 * t, kind, src, out, step, None)
 
         ring_z = extra(0, dz_ref, "z", d_ref, 0)
-        ring_x = extra(1, dx_ref, "x", dz_ref, 1)
-        thirds = [extra(2 + j, out, "basis", basis_ref, j) for j, out in enumerate((t0, t1, t2))]
-
-        next(main)
-        next(ring_z)
-        next(main)
+        ring_x = extra(1, dx_ref, "x", d_ref, 0)
 
         def pick(j, carry):
             some = id_ref[pl.ds(pl.multiple_of(j * count, count), count)]
@@ -572,20 +578,19 @@
             pick_part[lax.div(j, 4), lax.rem(j, 4)] = value.astype(BF16)
             return carry
 
-        lax.fori_loop(0, 4, pick, 0)
-        next(ring_z)
-        next(main)
-        lax.fori_loop(4, 8, pick, 0)
-        next(picks)
         next(main)
         next(ring_z)
-        next(picks)
-        next(main)
+        for j in range(4):
+            lax.fori_loop(2 * j, 2 * j + 2, pick, 0)
+            if j == 3:
+                next(picks)
+            next(main)
         next(late)
-        drive(ring_z)
         next(ring_x)
         next(ring_x)
+        next(picks)
         drive(main)
+        next(ring_z)
         for h in range(2):
             logits[pl.ds(h * (tokens // 2), tokens // 2), :] = end(h)
         top = jnp.max(logits[...], axis=1, keepdims=True)
@@ -596,7 +601,6 @@
         for k in range(7):
             net.send(base_s + k, mine, got.at[k], narrow_peers[k])
         next(late)
-        next(thirds[0])
         for k in range(7):
             net.recv(base_s + k, got.at[k])
         largest = mine[0]
@@ -614,17 +618,15 @@
             net, base_g, own, slot, 4, net.z, net.x, net.on_z, net.on_x
         )
         next(spread)
+        next(ring_x)
         next(late)
-        next(ring_x)
+        next(ring_z)
         next(spread)
-        next(thirds[1])
         next(late)
-        next(thirds[0])
-        next(spread)
-        next(thirds[2])
         next(picks)
         next(spread)
         next(late)
+        next(spread)
         drive(late)
         drive(spread)
         for h in range(2):
@@ -636,7 +638,7 @@
             common_ref[row] = contract_last(
                 every[row].reshape(4 * tokens, vocab), unembed[...]
             )
-        drive(ring_x, *thirds)
+        drive(ring_x, ring_z)
         net.finish()
 
     return call(
@@ -648,8 +650,8 @@
             like((count, features), BF16),
             *side.outs,
         ],
-        [VMEM] * 3 + [ANY] * 6,
         [VMEM] * 3 + [ANY] * 5,
+        [VMEM] * 3 + [ANY] * 2,
         [
             pltpu.VMEM((features, vocab), BF16),
             pltpu.VMEM((features, width), BF16),
@@ -667,7 +669,7 @@
             pltpu.SemaphoreType.DMA((4,)),
             *sems(base_t + side.slots),
         ],
-        (normed, inputs, ids, *unembeds, *bases_in, down, basis),
+        (normed, inputs, ids, *unembeds, *bases_in, down),
         name,
         cost,
     )
@@ -720,7 +722,7 @@
 def rotate_all(back, gate, down, down_z, downs, bases, thirds, inputs, collective_id, name, cost):
     tokens, depth = gate.shape
     columns = bases[0].shape[0]
-    width = inputs.shape[1]
+    width = inputs.shape[2]
     rows = 2 * tokens
     features = back.shape[2]
     cuts = (pl.ds(0, 896), pl.ds(896, depth - 896))
@@ -728,12 +730,12 @@
     def kernel(*refs):
         back_ref, g_ref, i_ref, own_ref, z_ref, d_refs = *refs[:5], refs[5:9]
         b_refs, t_refs, o_ref = refs[9:11], refs[11:14], refs[14]
-        down, bases, h_ref, j_ref, spun, pairs, corrected = refs[15:22]
-        half_in, gated, other, every, part, fwd, mid, got, mine = refs[22:31]
-        local, send_sem, recv_sem = refs[31:]
+        down, bases, h_ref, ours_in, j_ref, spun, pairs, corrected = refs[15:23]
+        half_in, gated, other, every, part, fwd, mid, got, mine = refs[23:32]
+        local, send_sem, recv_sem = refs[32:]
         net = Net(send_sem, recv_sem)
         c, z, x, zl, y = net.core, net.z, net.x, net.zl, net.y
-        base_z, base_r, base_n = 8, 40, 64
+        base_z, base_r, base_n, base_i = 8, 40, 64, 136
         loads = []
         for k in range(4):
             block = z_ref.at[turn(z, k, 4)] if k else own_ref
@@ -758,35 +760,52 @@
                         local.at[10 + 2 * j + m],
                     )
                 )
-        for load in loads:
+        ones = [net.on_x(1), net.on_x(3), net.on_z(1), net.on_z(3)]
+        all_here = net.call_out(ones + [net.on_y(1), net.on_y(3), net.on_zl(1), net.on_core()])
+        for load in loads[:16]:
             load.start()
-        ones = [net.on_x(1), net.on_x(3), net.on_z(1), net.on_z(3)]
-        net.greet(ones + [net.on_y(1), net.on_y(3), net.on_zl(1), net.on_core()])
-        for load in loads[:16]:
-            load.wait()
         quarter = features // 4
         left = back_ref[...].reshape(2 * 4 * tokens, features)
         for j, cut in enumerate(cuts):
             total = None
             for k in range(4):
+                if j == 0:
+                    for load in loads[4 * k : 4 * k + 4]:
+                        load.wait()
                 right = down[k, :, :, cut].reshape(quarter, cut.size)
                 term = jnp.dot(
                     left[:, k * quarter : (k + 1) * quarter], right, preferred_element_type=F32
                 )
                 total = term if total is None else total + term
             h_ref[:, :, cut] = total.reshape(2, 4 * tokens, cut.size)
-            net.send((0, 7)[j], h_ref.at[1 - c, :, cut], half_in.at[:, cut], net.on_core())
-        net.send(1, i_ref, j_ref, net.on_core())
-
-        def gate_rows(s, cut):
+        for load in loads[16:]:
+            load.start()
+        all_here()
+        theirs, ours = (
+            pl.ds(pl.multiple_of(2 * tokens * o, 2 * tokens), 2 * tokens) for o in (1 - zl, zl)
+        )
+        net.send(0, h_ref.at[1 - c, theirs], half_in.at[theirs], net.on_core())
+        net.send(7, h_ref.at[1 - c, ours], half_in.at[ours], net.on_core())
+        ours_in[z, x] = i_ref[...]
+        inputs_stage = gather_stage(
+            net, base_i, lambda h: i_ref.at[h], lambda o, i, h: ours_in.at[o, i, h],
+            4, z, x, net.on_z, net.on_x,
+        )
+        next(inputs_stage)
+
+        def gate_rows(s):
             some = pl.ds(pl.multiple_of(s * tokens, tokens), tokens)
-            value = (h_ref[c, some, cut] + half_in[some, cut]) * g_ref[:, cut].astype(F32)
-            gated[s, :, cut] = value.astype(BF16)
-
-        for j, cut in enumerate(cuts):
-            net.recv((0, 7)[j], half_in.at[:, cut])
-            for s in range(2):
-                gate_rows(2 * zl + s, cut)
+            value = (h_ref[c, some] + half_in[some]) * g_ref[...].astype(F32)
+            gated[s] = value.astype(BF16)
+
+        net.recv(0, half_in.at[theirs])
+        for s in range(2):
+            gate_rows(2 * (1 - zl) + s)
+        net.send(2, gated.at[pl.ds(2 * (1 - zl), 2)], other, net.on_zl(1))
+        next(inputs_stage)
+        net.recv(7, half_in.at[ours])
+        for s in range(2):
+            gate_rows(2 * zl + s)
 
         own = lambda h: other if h else gated.at[pl.ds(2 * zl, 2)]
         slot = lambda o, i, h: every.at[o, h, i]
@@ -799,15 +818,17 @@
         def along(row, h):
             o, b = order[row], inner(row)
             src = own(h) if row == 0 else slot(o, x, h)
-            net.send(b + (0, 1)[h], src, slot(o, x, h), net.on_x(1))
-            net.send(b + (3, 2)[h], src, slot(o, x, h), net.on_x(3))
-
-        def forward(row):
+            net.send(b + h, src, slot(o, x, h), net.on_x(1))
+            net.send(b + 3 - h, src, slot(o, x, h), net.on_x(3))
+
+        def forward(row, ways=(0, 1)):
             o, b = order[row], inner(row)
-            net.recv(b, slot(o, xm, 0))
-            net.send(b + 4, slot(o, xm, 0), slot(o, xm, 0), net.on_x(1))
-            net.recv(b + 2, slot(o, xp, 1))
-            net.send(b + 5, slot(o, xp, 1), slot(o, xp, 1), net.on_x(3))
+            if 0 in ways:
+                net.recv(b, slot(o, xm, 0))
+                net.send(b + 4, slot(o, xm, 0), slot(o, xm, 0), net.on_x(1))
+            if 1 in ways:
+                net.recv(b + 2, slot(o, xp, 1))
+                net.send(b + 5, slot(o, xp, 1), slot(o, xp, 1), net.on_x(3))
 
         def rest(row):
             o, b = order[row], inner(row)
@@ -859,8 +880,8 @@
             if k == 0:
                 net.recv(1, j_ref)
             e = order[k]
-            pairs[:, : 4 * tokens] = i_ref[e]
-            pairs[:, 4 * tokens :] = j_ref[e]
+            pairs[:, : 4 * tokens] = ours_in[e].reshape(4 * tokens, width).T
+            pairs[:, 4 * tokens :] = j_ref[e].reshape(4 * tokens, width).T
 
             def tile(t, carry):
                 cut = pl.ds(pl.multiple_of(t * 128, 128), 128)
@@ -889,10 +910,7 @@
         net.send(base_z, own(0), slot(z, x, 0), net.on_z(1))
         net.send(base_z + 3, own(0), slot(z, x, 0), net.on_z(3))
         along(0, 0)
-        for cut in cuts:
-            for s in range(2):
-                gate_rows(2 * (1 - zl) + s, cut)
-        net.send(2, gated.at[pl.ds(2 * (1 - zl), 2)], other, net.on_zl(1))
+        next(inputs_stage)
         net.recv(2, other)
         net.send(base_z + 2, own(1), slot(z, x, 1), net.on_z(3))
         net.send(base_z + 1, own(1), slot(z, x, 1), net.on_z(1))
@@ -900,25 +918,30 @@
         copies = [pltpu.make_async_copy(own(h), slot(z, x, h), local.at[h]) for h in range(2)]
         for copy in copies:
             copy.start()
+        drive(inputs_stage)
+        net.send(1, ours_in, j_ref, net.on_core())
         net.recv(base_z, slot(zm, x, 0))
         net.send(base_z + 4, slot(zm, x, 0), slot(zm, x, 0), net.on_z(1))
         net.recv(base_z + 2, slot(zp, x, 1))
         net.send(base_z + 5, slot(zp, x, 1), slot(zp, x, 1), net.on_z(3))
         forward(0)
+        along(1, 0)
         net.recv(base_z + 1, slot(zm, x, 1))
-        for h in range(2):
-            along(1, h)
+        along(1, 1)
         rest(0)
         for copy in copies + loads[16:]:
             copy.wait()
         multiply(0)
         reduce_start(0)
         forward(1)
+        along(2, 1)
         net.recv(base_z + 3, slot(zp, x, 0))
-        for h in range(2):
-            along(2, h)
+        along(2, 0)
         reduce_middle(0)
         rest(1)
+        last = inner(3)
+        net.send(last + 1, slot(zm, xp, 1), slot(zm, xp, 1), net.on_z(1))
+        net.send(last + 2, slot(zm, xm, 1), slot(zm, xm, 1), net.on_z(1))
         reduce_end(0)
         multiply(1)
         reduce_start(1)
@@ -926,22 +949,26 @@
         next(spread_0)
         forward(2)
         net.recv(base_z + 4, slot(z2, x, 0))
-        net.recv(base_z + 5, slot(z2, x, 1))
-        for h in range(2):
-            along(3, h)
+        along(3, 0)
         reduce_middle(1)
         next(spread_0)
         rest(2)
+        net.send(last + 5, slot(zp, x2, 1), slot(zp, x2, 1), net.on_z(3))
         reduce_end(1)
         multiply(2)
         reduce_start(2)
         spread_1 = spread(1)
         next(spread_1)
         next(spread_0)
-        forward(3)
+        forward(3, (0,))
         reduce_middle(2)
         next(spread_1)
-        rest(3)
+        net.recv(base_z + 5, slot(z2, x, 1))
+        net.recv(last + 3, slot(z2, xp, 0))
+        net.recv(last + 4, slot(z2, x2, 0))
+        net.recv(last + 1, slot(z2, xp, 1))
+        net.recv(last + 2, slot(z2, xm, 1))
+        net.recv(last + 5, slot(z2, x2, 1))
         multiply(3)
         reduce_start(3)
         reduce_end(2)
@@ -973,7 +1000,8 @@
             pltpu.VMEM((4, 4, features // 16, depth), BF16),
             pltpu.VMEM((4, columns, depth), BF16),
             pltpu.VMEM((2, 4 * tokens, depth), F32),
-            pltpu.VMEM(inputs.shape, BF16),
+            pltpu.VMEM((4, 4, *inputs.shape), BF16),
+            pltpu.VMEM((4, 4, *inputs.shape), BF16),
             pltpu.VMEM((4, 2, 2, 2, 4, tokens, columns), BF16),
             pltpu.VMEM((width, 8 * tokens), BF16),
             pltpu.VMEM((width, columns), F32),
@@ -987,7 +1015,7 @@
             pltpu.VMEM((4, 2, 2, rows, columns), F32),
             pltpu.VMEM((4, 3, 2, tokens, columns), BF16),
             pltpu.SemaphoreType.DMA((32,)),
-            *sems(64 + 4 * gather_slots(2)),
+            *sems(64 + 4 * gather_slots(2) + gather_slots(4)),
         ],
         (back, gate, inputs, down, down_z, *downs, *bases, *thirds),
         name,
@@ -1021,10 +1049,10 @@
         return rows.reshape(tokens, 16, pair).transpose(1, 0, 2)
 
     down, basis = down_weight.T, basis_out.T
-    normed_cols, inputs_cols, unembed_other, basis_in_other, basis_other, down_0 = exchange(
+    normed_cols, inputs_cols, unembed_other, basis_in_other, basis_other = exchange(
         [blocks(normed), blocks(layer_in)],
         [unembed.T, basis_in, basis],
-        [("x", down, 0)],
+        [],
         0,
         "exchange",
         30,
@@ -1033,25 +1061,36 @@
         labels.reshape(16, 2, 8, few, samples), core, 1, keepdims=False
     )
     shifted = mine.transpose(1, 0, 2, 3).reshape(core_tokens * samples, 1) - narrow * vocab
-    common, inputs_rot, picked, down_z, down_1, third_0, third_1, third_2 = front(
+    common, inputs_rot, picked, down_z, down_0 = front(
         normed_cols.reshape(4, 4, tokens, pair),
         inputs_cols.reshape(4, 4, tokens, pair),
         [unembed.T, unembed_other],
         [basis_in, basis_in_other],
         shifted,
         down,
-        basis,
         1,
         "front",
         100,
     )
     common = common.reshape(16, 8, few, pair).transpose(1, 0, 2, 3).reshape(2, 4, 16 * few, pair)
-    common, down_2, inputs_all = reduce_over(
-        [], [common], [("x", down_z, 2), ("all", inputs_rot, 0)], [F32], 4, "reduce_common", 20
-    )
-    inputs_all = inputs_all.reshape(4, 4 * tokens, width_in).transpose(0, 2, 1)
+    common, down_1, third_0, third_1 = reduce_over(
+        [],
+        [common],
+        [("x", down_z, 1), ("basis", basis, 0), ("basis", basis, 1)],
+        [F32],
+        4,
+        "reduce_common",
+        30,
+    )
     grads = common.reshape(16, few, 1, pair) - picked.astype(F32).reshape(16, few, samples, pair)
-    (grads,) = exchange([grads.reshape(16, few * samples, pair)], [], [], 5, "exchange_grads", 12)
+    grads, down_2 = exchange(
+        [grads.reshape(16, few * samples, pair)],
+        [],
+        [("x", down_z, 2)],
+        5,
+        "exchange_grads",
+        20,
+    )
     grads = grads.transpose(1, 0, 2).reshape(few, samples, width)
     resid_few = lax.dynamic_slice_in_dim(resid_float, narrow * few, few, 0)
     inverse_few = lax.dynamic_slice_in_dim(inverse, narrow * few, few, 0)
@@ -1064,8 +1103,12 @@
     back = lax.dynamic_slice_in_dim(
         jnp.concatenate([back, back], axis=2), lax.div(wide, 8), 4, axis=2
     )
-    back, down_3 = gather_back(
-        back.reshape(2, few * samples, width // 2), [("x", down_z, 3)], 6, "gather_back", 20
+    back, down_3, third_2 = gather_back(
+        back.reshape(2, few * samples, width // 2),
+        [("x", down_z, 3), ("basis", basis, 2)],
+        6,
+        "gather_back",
+        20,
     )
     back = back.reshape(8, 2, few, samples, width // 2).transpose(1, 3, 0, 2, 4)
     return rotate_all(
@@ -1076,7 +1119,7 @@
         [down_0, down_1, down_2, down_3],
         [basis, basis_other],
         [third_0, third_1, third_2],
-        inputs_all,
+        inputs_rot,
         7,
         "rotate_all",
         110,

time: 411 us -> 392 us (0.954)
  Pallas kernels: 378 us -> 360 us
    pallas_call x6, Pallas kernels: 378 us -> 360 us  [call(): pl.pallas_call(kernel, out_shape=outs, in_specs=in_specs, out_specs=out_s...]
where the time goes in v5:
time: 392 us; the launch traced here: 390 us
  Pallas kernels  360 us (92%)
  local copies, waits for them, and re-layouts  23.1 us (6%)
  other arithmetic  5.92 us (2%)
    pallas_call x6, Pallas kernels, call(): pl.pallas_call(kernel, out_shape=outs, in_specs=in_specs, out_specs=out_s...  360 us

profile of v5, /device:TPU:1, one launch (start us, length us, event | category | flops | bytes accessed | tf_op | source)
XLA Modules:
  0.0 389.6 jit_solution(2895781513548615716)
XLA Ops:
  0.0 1.2 multiply_reduce_fusion
  1.2 0.1 multiply_multiply_fusion
  1.3 1.4 mul.119
  2.7 1.1 multiply_convert_fusion
  3.8 0.0 copy-start.8
  3.8 0.3 reshape.113
  4.2 0.3 reshape.114
  4.5 0.0 copy-start
  4.5 1.1 copy_bitcast_fusion.1
  5.6 0.5 reshape.117
  6.2 0.9 copy.16
  7.1 0.0 copy-done
  7.1 0.0 copy-done.6
  7.1 0.1 broadcast_multiply_fusion
  7.2 0.1 mul.117
  7.3 1.6 mul.118
  8.9 0.1 mul.122
  8.9 1.0 mul.123
  9.9 0.1 mul.107
  10.0 1.6 mul.108
  11.5 1.3 sub.39.refs_2_
  12.8 29.0 %exchange.1 = (bf16[16,32,320]{2,1,0:T(8,128)(2,1)}, bf16[16,32,320]{2,1,0:T(8,128)(2,1)}, bf16[160,2048]{1,0:T(8,128)(2,1)}, bf16[160,640]{1,0:T(8,128)(2,1)}, bf16[432,1728]{1,0:T(8,128)(2,1)}) custom-call(bf16[16,32,320]{2,1,0:T(8,128)(2,1)} %get-tuple-element.49.refs_0_, bf16[16,32,320]{2,1,0:T(8,128)(2,1)} %get-tuple-element.48.refs_1_, ...), custom_call_target="tpu_custom_call" | custom-call | flops 30000001024 | tf_op jit(solution)/shard_map/exchange/pallas_call | solution.py:384
  41.8 97.0 %front.1 = (f32[4,128,320]{2,1,0:T(8,128)}, bf16[2,16,640]{2,1,0:T(8,128)(2,1)}, bf16[256,320]{1,0:T(8,128)(2,1)}, bf16[4,160,1728]{2,1,0:T(8,128)(2,1)}, bf16[4,160,1728]{2,1,0:T(8,128)(2,1)}) custom-call(bf16[4,4,32,320]{3,2,1,0:T(8,128)(2,1)} %bitcast.42, bf16[4,4,32,320]{3,2,1,0:T(8,128)(2,1)} %bitcast.43, s32[2048,1]{1,0:T(8,128)} %sub.39.refs_2_, ...), custom_call_target="tpu_custom_call" | custom-call | flops 99999997952 | tf_op jit(solution)/shard_map/front/pallas_call | solution.py:384
  138.9 1.4 reshape.118
  140.3 0.1 copy.18
  140.3 1.2 reshape.119.refs_0_
  141.5 37.3 %reduce_common.1 = (f32[64,320]{1,0:T(8,128)}, bf16[4,160,1728]{2,1,0:T(8,128)(2,1)}, bf16[2,144,1728]{2,1,0:T(8,128)(2,1)}, bf16[2,144,1728]{2,1,0:T(8,128)(2,1)}) custom-call(f32[2,4,64,320]{3,2,1,0:T(8,128)} %reshape.119.refs_0_, bf16[4,160,1728]{2,1,0:T(8,128)(2,1)} %get-tuple-element.29.refs_1_.refs_4_, bf16[432,1728]{1,0:T(8,128)(2,1)} %bitcast.34, ...), custom_call_target="tpu_custom_call" | custom-call | flops 30000001024 | tf_op jit(solution)/shard_map/reduce_common/pallas_call | solution.py:384
  178.8 1.0 sub.34
  179.8 0.1 sub.35
  179.8 0.1 sub.36
  180.0 0.8 convert_subtract_fusion.refs_0_
  180.8 32.7 %exchange_grads.1 = (f32[16,16,320]{2,1,0:T(8,128)}, bf16[4,160,1728]{2,1,0:T(8,128)(2,1)}) custom-call(f32[16,16,320]{2,1,0:T(8,128)} %convert_subtract_fusion.refs_0_, bf16[4,160,1728]{2,1,0:T(8,128)(2,1)} %get-tuple-element.29.refs_1_.refs_4_), custom_call_target="tpu_custom_call" | custom-call | flops 20000000000 | tf_op jit(solution)/shard_map/exchange_grads/pallas_call | solution.py:384
  213.5 0.0 copy-start.1
  213.5 0.0 copy-start.2
  213.5 0.0 copy-done.3
  213.5 0.0 copy-done.7
  213.5 1.3 fusion.2
  214.9 1.4 reshape.122
  216.3 0.5 fusion.4
  216.8 0.7 fusion.3
  217.6 0.1 copy.21
  217.7 1.0 reshape.123.refs_0_
  218.7 30.5 %gather_back.1 = (bf16[2,4,2,16,2560]{4,3,2,1,0:T(8,128)(2,1)}, bf16[4,160,1728]{2,1,0:T(8,128)(2,1)}, bf16[2,144,1728]{2,1,0:T(8,128)(2,1)}) custom-call(bf16[2,16,2560]{2,1,0:T(8,128)(2,1)} %reshape.123.refs_0_, bf16[4,160,1728]{2,1,0:T(8,128)(2,1)} %get-tuple-element.29.refs_1_.refs_4_, bf16[432,1728]{1,0:T(8,128)(2,1)} %bitcast.36), custom_call_target="tpu_custom_call" | custom-call | flops 20000000000 | tf_op jit(solution)/shard_map/gather_back/pallas_call | solution.py:384
  249.2 2.6 reshape.124
  251.8 0.5 copy.36
  252.3 1.2 reshape.125.refs_0_
  253.6 133.8 %rotate_all.1 = f32[432,640]{1,0:T(8,128)} custom-call(bf16[2,128,2560]{2,1,0:T(8,128)(2,1)} %reshape.125.refs_0_, bf16[32,1728]{1,0:T(8,128)(2,1)} %refs_1_.1, bf16[2,16,640]{2,1,0:T(8,128)(2,1)} %get-tuple-element.34.refs_2_, bf16[160,1728]{1,0:T(8,128)(2,1)} %bitcast.41, bf16[4,160,1728]{2,1,0:T(8,128)(2,1)} %get-tuple-element.29.refs_1_.refs_4_, ...), custom_call_target="tpu_custom_call" | custom-call | flops 109999996928 | tf_op jit(solution)/shard_map/rotate_all/pallas_call | solution.py:384
  387.3 2.3 copy.38
  (13 shorter events, 0.1 us)
Async XLA Ops:
  0.0 4.2 %copy-start.4 = (bf16[32,5120]{1,0:T(8,128)(2,1)S(1)}, bf16[32,5120]{1,0:T(8,128)(2,1)}, u32[]{:S(2)}) copy-start(bf16[32,5120]{1,0:T(8,128)(2,1)} %param.13) | copy-start | bytes 983044
  3.8 1.8 copy-start.8
  4.5 2.5 copy-start
  5.6 1.5 copy-start.6
  178.8 1.2 copy-start.5
  180.8 32.7 %copy-start.3 = (f32[16,16,320]{2,1,0:T(8,128)S(1)}, f32[16,16,320]{2,1,0:T(8,128)}, u32[]{:S(2)}) copy-start(f32[16,16,320]{2,1,0:T(8,128)} %mul.123) | copy-start | bytes 983044
  180.8 32.8 %copy-start.7 = (f32[16,320]{1,0:T(8,128)S(1)}, f32[16,320]{1,0:T(8,128)}, u32[]{:S(2)}) copy-start(f32[16,320]{1,0:T(8,128)} %mul.119) | copy-start | bytes 61444
  213.5 2.8 copy-start.1
  213.5 2.8 copy-start.2

commit v6 on v5

--- a/solution.py
+++ b/solution.py
@@ -138,6 +138,7 @@
         forward(3, o2)
         for row, o in enumerate((me_o, om, op, o2)):
             rest(row, o)
+            yield
     else:
         oq = 1 - me_o
         for h in range(2):
@@ -511,10 +512,10 @@
     )
 
 
-def front(normed, inputs, unembeds, bases_in, ids, down, collective_id, name, cost):
-    tokens, features = normed.shape[2:]
+def front(normed, inputs, unembed_own, basis_in_own, basis_own, ids, down, collective_id, name, cost):
+    tokens, features = normed.shape[1:]
     half = features // 2
-    vocab, width = unembeds[0].shape[1], bases_in[0].shape[1]
+    vocab, width = unembed_own.shape[1], basis_in_own.shape[1]
     count = ids.shape[0] // 8
     side = Side([("z", down, 0), ("x", down, 0)])
     base_i = reduce_slots(4)
@@ -522,44 +523,72 @@
     base_s = base_p + reduce_slots(2)
     base_g = base_s + 7
     base_t = base_g + gather_slots(4)
+    base_x = base_t + side.slots
 
     def kernel(*refs):
-        n_ref, i_ref, id_ref, u0, u1, b0, b1, d_ref = refs[:8]
-        common_ref, rot_ref, picked_ref, dz_ref, dx_ref = refs[8:13]
-        unembed, basis_in, logit_part, input_part, pick_part = refs[13:18]
-        sum_l, sum_i, sum_p = (refs[18 + 6 * j : 24 + 6 * j] for j in range(3))
-        logits, mine, got, probs, every, local, send_sem, recv_sem = refs[36:]
+        id_ref, nb_ref, ib_ref, u_ref, b_ref, basis_ref, d_ref = refs[:7]
+        common_ref, rot_ref, picked_ref, other_ref, dz_ref, dx_ref = refs[7:13]
+        n_ref, i_ref, unembed, basis_in, logit_part, input_part, pick_part = refs[13:20]
+        sum_l, sum_i, sum_p = (refs[20 + 6 * j : 26 + 6 * j] for j in range(3))
+        logits, mine, got, probs, every, local, send_sem, recv_sem = refs[38:]
         net = Net(send_sem, recv_sem)
-        c = net.core
-        loads = [
-            pltpu.make_async_copy(u0, unembed.at[pl.ds(c * half, half)], local.at[0]),
-            pltpu.make_async_copy(u1, unembed.at[pl.ds((1 - c) * half, half)], local.at[1]),
-            pltpu.make_async_copy(b0, basis_in.at[pl.ds(c * half, half)], local.at[2]),
-            pltpu.make_async_copy(b1, basis_in.at[pl.ds((1 - c) * half, half)], local.at[3]),
+        c, z, x = net.core, net.z, net.x
+        my_rows, its_rows = (
+            pl.ds(pl.multiple_of(o * half, half), half) for o in (c, 1 - c)
+        )
+        steps = [(dz, dx) for dz in range(4) for dx in range(4) if (dz, dx) != (0, 0)]
+        steps.sort(key=lambda s: -(min(s[0], 4 - s[0]) * 2 + min(s[1], 4 - s[1])))
+        peers = [
+            {"wide": turn(z, dz, 4) * 8 + turn(x, dx, 4) * 2 + c} for dz, dx in steps
         ]
-        for load in loads:
-            load.start()
-        ring_peers = [net.on_x(1), net.on_x(3), net.on_z(1), net.on_z(3), net.on_core()]
         narrow_peers = [{"narrow": turn(net.narrow, k, 8)} for k in range(1, 8)]
-        net.greet(ring_peers + narrow_peers)
-        for load in loads:
-            load.wait()
-
-        def dot_row(left, right, part):
+        all_here = net.call_out(peers + [net.on_core()] + narrow_peers)
+        keeps = [
+            pltpu.make_async_copy(nb_ref.at[z * 4 + x], n_ref.at[z, x], local.at[0]),
+            pltpu.make_async_copy(ib_ref.at[z * 4 + x], i_ref.at[z, x], local.at[1]),
+            pltpu.make_async_copy(u_ref, unembed.at[my_rows], local.at[2]),
+            pltpu.make_async_copy(b_ref, basis_in.at[my_rows], local.at[3]),
+        ]
+        for keep in keeps:
+            keep.start()
+        all_here()
+
+        def scatter(base, src, dst):
+            for j, (dz, dx) in enumerate(steps):
+                target = turn(z, dz, 4) * 4 + turn(x, dx, 4)
+                net.send(base + j, src.at[target], dst.at[z, x], peers[j])
+
+        scatter(base_x, nb_ref, n_ref)
+        net.send(base_x + 30, u_ref, unembed.at[my_rows], net.on_core())
+        scatter(base_x + 15, ib_ref, i_ref)
+        net.send(base_x + 31, b_ref, basis_in.at[my_rows], net.on_core())
+        net.send(base_x + 32, basis_ref, other_ref, net.on_core())
+
+        def dot_row(base, left, keep, right, part):
+            offsets = iter((2, 1, 3, 0))
+
             def run(row):
+                offset = next(offsets)
+                for j, (dz, dx) in enumerate(steps):
+                    if (4 - dz) % 4 == offset:
+                        net.recv(base + j, left.at[row, turn(x, (4 - dx) % 4, 4)])
+                if offset == 0:
+                    keep.wait()
                 rows = left[row].reshape(4 * tokens, features)
                 value = jnp.dot(rows, right[...], preferred_element_type=F32)
                 part[row] = value.reshape(4, tokens, part.shape[3])
 
             return run
 
+        keeps[2].wait()
+        net.recv(base_x + 30, unembed.at[its_rows])
         main, (end,) = reduce_stage(
             net, 0, [Sum(logit_part, *sum_l)], 4, net.z, net.x, net.on_z, net.on_x,
-            dot_row(n_ref, unembed, logit_part),
+            dot_row(base_x, n_ref, keeps[0], unembed, logit_part),
         )
         late, (end_i,) = reduce_stage(
             net, base_i, [Sum(input_part, *sum_i)], 4, net.z, net.x, net.on_z, net.on_x,
-            dot_row(i_ref, basis_in, input_part),
+            dot_row(base_x + 15, i_ref, keeps[1], basis_in, input_part),
         )
         picks, (end_p,) = reduce_stage(
             net, base_p, [Sum(pick_part, *sum_p)], 2, net.zl, net.y, net.on_zl, net.on_y
@@ -585,6 +614,8 @@
             if j == 3:
                 next(picks)
             next(main)
+        keeps[3].wait()
+        net.recv(base_x + 31, basis_in.at[its_rows])
         next(late)
         next(ring_x)
         next(ring_x)
@@ -627,6 +658,10 @@
         next(spread)
         next(late)
         next(spread)
+        for step in (0, 3, 1, 2):
+            next(spread)
+            row = turn(net.z, step, 4)
+            common_ref[row] = contract_last(every[row].reshape(4 * tokens, vocab), unembed[...])
         drive(late)
         drive(spread)
         for h in range(2):
@@ -634,11 +669,8 @@
         drive(picks)
         for h in range(2):
             picked_ref[pl.ds(h * (count // 2), count // 2), :] = end_p(h).astype(BF16)
-        for row in range(4):
-            common_ref[row] = contract_last(
-                every[row].reshape(4 * tokens, vocab), unembed[...]
-            )
         drive(ring_x, ring_z)
+        net.recv(base_x + 32, other_ref)
         net.finish()
 
     return call(
@@ -648,11 +680,14 @@
             like((4, 4 * tokens, features), F32),
             like((2, tokens // 2, width), BF16),
             like((count, features), BF16),
+            like(basis_own.shape, BF16),
             *side.outs,
         ],
-        [VMEM] * 3 + [ANY] * 5,
-        [VMEM] * 3 + [ANY] * 2,
+        [VMEM] + [ANY] * 6,
+        [VMEM] * 3 + [ANY] * 3,
         [
+            pltpu.VMEM((4, 4, tokens, features), BF16),
+            pltpu.VMEM((4, 4, tokens, features), BF16),
             pltpu.VMEM((features, vocab), BF16),
             pltpu.VMEM((features, width), BF16),
             pltpu.VMEM((4, 4, tokens, vocab), F32),
@@ -667,9 +702,9 @@
             pltpu.VMEM((2, tokens // 2, vocab), BF16),
             pltpu.VMEM((4, 4, 2, tokens // 2, vocab), BF16),
             pltpu.SemaphoreType.DMA((4,)),
-            *sems(base_t + side.slots),
+            *sems(base_x + 33),
         ],
-        (normed, inputs, ids, *unembeds, *bases_in, down),
+        (ids, normed, inputs, unembed_own, basis_in_own, basis_own, down),
         name,
         cost,
     )
@@ -1049,28 +1084,21 @@
         return rows.reshape(tokens, 16, pair).transpose(1, 0, 2)
 
     down, basis = down_weight.T, basis_out.T
-    normed_cols, inputs_cols, unembed_other, basis_in_other, basis_other = exchange(
-        [blocks(normed), blocks(layer_in)],
-        [unembed.T, basis_in, basis],
-        [],
-        0,
-        "exchange",
-        30,
-    )
     mine = lax.dynamic_index_in_dim(
         labels.reshape(16, 2, 8, few, samples), core, 1, keepdims=False
     )
     shifted = mine.transpose(1, 0, 2, 3).reshape(core_tokens * samples, 1) - narrow * vocab
-    common, inputs_rot, picked, down_z, down_0 = front(
-        normed_cols.reshape(4, 4, tokens, pair),
-        inputs_cols.reshape(4, 4, tokens, pair),
-        [unembed.T, unembed_other],
-        [basis_in, basis_in_other],
+    common, inputs_rot, picked, basis_other, down_z, down_0 = front(
+        blocks(normed),
+        blocks(layer_in),
+        unembed.T,
+        basis_in,
+        basis,
         shifted,
         down,
         1,
         "front",
-        100,
+        120,
     )
     common = common.reshape(16, 8, few, pair).transpose(1, 0, 2, 3).reshape(2, 4, 16 * few, pair)
     common, down_1, third_0, third_1 = reduce_over(

time: 392 us -> 381 us (0.972)
  Pallas kernels: 360 us -> 349 us
    pallas_call x6 -> x5, Pallas kernels: 360 us -> 349 us  [call(): pl.pallas_call(kernel, out_shape=outs, in_specs=in_specs, out_specs=out_s...]
where the time goes in v6:
time: 381 us; the launch traced here: 378 us
  Pallas kernels  349 us (92%)
  local copies, waits for them, and re-layouts  23.2 us (6%)
  other arithmetic  5.92 us (2%)
    pallas_call x5, Pallas kernels, call(): pl.pallas_call(kernel, out_shape=outs, in_specs=in_specs, out_specs=out_s...  349 us

profile of v6, /device:TPU:1, one launch (start us, length us, event | category | flops | bytes accessed | tf_op | source)
XLA Modules:
  0.0 378.0 jit_solution(14341569752892507141)
XLA Ops:
  0.0 1.2 multiply_reduce_fusion
  1.2 0.1 multiply_multiply_fusion
  1.3 1.4 mul.119
  2.7 1.1 multiply_convert_fusion
  3.8 0.0 copy-start.8
  3.8 0.3 reshape.108
  4.2 0.3 reshape.109
  4.5 0.0 copy-start
  4.5 1.1 copy_bitcast_fusion.1
  5.6 0.5 reshape.107
  6.2 0.9 copy.14
  7.1 0.0 copy-done.6
  7.1 0.1 broadcast_multiply_fusion
  7.2 0.1 mul.117
  7.3 1.6 mul.118
  8.9 0.1 mul.122
  8.9 1.0 mul.123
  9.9 0.1 mul.107
  10.0 1.6 mul.108
  11.6 1.3 sub.39.refs_0_
  12.9 115.8 %front.1 = (f32[4,128,320]{2,1,0:T(8,128)}, bf16[2,16,640]{2,1,0:T(8,128)(2,1)}, bf16[256,320]{1,0:T(8,128)(2,1)}, bf16[432,1728]{1,0:T(8,128)(2,1)}, bf16[4,160...) custom-call(s32[2048,1]{1,0:T(8,128)} %sub.39.refs_0_, bf16[16,32,320]{2,1,0:T(8,128)(2,1)} %get-tuple-element.41.refs_1_, ...), custom_call_target="tpu_custom_call" | custom-call | flops 120000004096 | tf_op jit(solution)/shard_map/front/pallas_call | solution.py:385
  128.7 1.4 reshape.110
  130.1 0.1 copy.18
  130.2 1.2 reshape.111.refs_0_
  131.3 37.2 %reduce_common.1 = (f32[64,320]{1,0:T(8,128)}, bf16[4,160,1728]{2,1,0:T(8,128)(2,1)}, bf16[2,144,1728]{2,1,0:T(8,128)(2,1)}, bf16[2,144,1728]{2,1,0:T(8,128)(2,1)}) custom-call(f32[2,4,64,320]{3,2,1,0:T(8,128)} %reshape.111.refs_0_, bf16[4,160,1728]{2,1,0:T(8,128)(2,1)} %get-tuple-element.21.refs_1_.refs_4_, bf16[432,1728]{1,0:T(8,128)(2,1)} %bitcast.32, ...), custom_call_target="tpu_custom_call" | custom-call | flops 30000001024 | tf_op jit(solution)/shard_map/reduce_common/pallas_call | solution.py:385
  168.5 0.0 copy-start.5
  168.5 1.0 sub.34
  169.5 0.1 sub.35
  169.5 0.1 sub.36
  169.7 0.0 copy-done.5
  169.7 0.8 convert_subtract_fusion.refs_0_
  170.5 32.2 %exchange_grads.1 = (f32[16,16,320]{2,1,0:T(8,128)}, bf16[4,160,1728]{2,1,0:T(8,128)(2,1)}) custom-call(f32[16,16,320]{2,1,0:T(8,128)} %convert_subtract_fusion.refs_0_, bf16[4,160,1728]{2,1,0:T(8,128)(2,1)} %get-tuple-element.21.refs_1_.refs_4_), custom_call_target="tpu_custom_call" | custom-call | flops 20000000000 | tf_op jit(solution)/shard_map/exchange_grads/pallas_call | solution.py:385
  202.7 0.0 copy-start.1
  202.7 0.0 copy-start.2
  202.8 0.0 copy-done.3
  202.8 0.0 copy-done.7
  202.8 1.3 fusion.2
  204.1 1.4 reshape.114
  205.6 0.5 fusion.4
  206.1 0.7 fusion.3
  206.8 0.1 copy.21
  206.9 1.0 reshape.115.refs_0_
  207.9 31.2 %gather_back.1 = (bf16[2,4,2,16,2560]{4,3,2,1,0:T(8,128)(2,1)}, bf16[4,160,1728]{2,1,0:T(8,128)(2,1)}, bf16[2,144,1728]{2,1,0:T(8,128)(2,1)}) custom-call(bf16[2,16,2560]{2,1,0:T(8,128)(2,1)} %reshape.115.refs_0_, bf16[4,160,1728]{2,1,0:T(8,128)(2,1)} %get-tuple-element.21.refs_1_.refs_4_, bf16[432,1728]{1,0:T(8,128)(2,1)} %bitcast.34), custom_call_target="tpu_custom_call" | custom-call | flops 20000000000 | tf_op jit(solution)/shard_map/gather_back/pallas_call | solution.py:385
  239.2 2.6 reshape.116
  241.8 0.5 copy.36
  242.3 1.2 reshape.117.refs_0_
  243.5 132.2 %rotate_all.1 = f32[432,640]{1,0:T(8,128)} custom-call(bf16[2,128,2560]{2,1,0:T(8,128)(2,1)} %reshape.117.refs_0_, bf16[32,1728]{1,0:T(8,128)(2,1)} %refs_1_.1, bf16[2,16,640]{2,1,0:T(8,128)(2,1)} %get-tuple-element.26.refs_2_, bf16[160,1728]{1,0:T(8,128)(2,1)} %bitcast.38, bf16[4,160,1728]{2,1,0:T(8,128)(2,1)} %get-tuple-element.21.refs_1_.refs_4_, ...), custom_call_target="tpu_custom_call" | custom-call | flops 109999996928 | tf_op jit(solution)/shard_map/rotate_all/pallas_call | solution.py:385
  375.7 2.3 copy.38
  (12 shorter events, 0.1 us)
Async XLA Ops:
  0.0 4.2 %copy-start.4 = (bf16[32,5120]{1,0:T(8,128)(2,1)S(1)}, bf16[32,5120]{1,0:T(8,128)(2,1)}, u32[]{:S(2)}) copy-start(bf16[32,5120]{1,0:T(8,128)(2,1)} %param.13) | copy-start | bytes 983044
  3.8 1.8 copy-start.8
  4.5 2.6 copy-start
  5.6 1.5 copy-start.6
  168.5 1.2 copy-start.5
  170.5 32.3 %copy-start.3 = (f32[16,16,320]{2,1,0:T(8,128)S(1)}, f32[16,16,320]{2,1,0:T(8,128)}, u32[]{:S(2)}) copy-start(f32[16,16,320]{2,1,0:T(8,128)} %mul.123) | copy-start | bytes 983044
  170.5 32.3 %copy-start.7 = (f32[16,320]{1,0:T(8,128)S(1)}, f32[16,320]{1,0:T(8,128)}, u32[]{:S(2)}) copy-start(f32[16,320]{1,0:T(8,128)} %mul.119) | copy-start | bytes 61444
  202.7 2.8 copy-start.1
  202.7 2.8 copy-start.2
